TPU v7x, 32 devices: a whole 2x2x4 slice. The times are simulated.
32 devices in a mesh: gz: 8 (over z, y), gx: 4 (over x, core).
Axes of the slice: x: 2, y: 2, z: 4, core: 2. Of those that a mesh axis runs over, the one named last changes fastest.
Arguments:
- density: float32 [16, 256, 256], P('gz', 'gx'), may hold values from -6 to 6
- green: float32 [2, 32, 512, 512], P(None, None, 'gz', 'gx'), may hold values from -12 to 12
- image_green: float32 [2, 32, 512, 512], P(None, None, 'gz', 'gx'), may hold values from -12 to 12
Outputs:
- grad_x: float32 [16, 256, 256], P('gz', 'gx')
- grad_y: float32 [16, 256, 256], P('gz', 'gx')
- grad_z: float32 [16, 256, 256], P('gz', 'gx')
All inputs are finite; a program needn't handle non-finite values.
Results may differ from a plain program's by a relative error of at most 0.00007.
Values sent between devices are 32-bit elements; how exact they have to be, the bound alone decides.
No kernel may reach another device: no remote copies, remote signals or barrier semaphores. Data moves between devices by JAX's collectives and lax.ppermute only.
A program may use at most 64 MiB of HBM per device.

v0:
```python
import functools
import math

import jax
import jax.numpy as jnp
import numpy as np
from jax import lax
from jax.experimental import pallas as pl
from jax.experimental.pallas import tpu as pltpu
from jax.sharding import PartitionSpec as P

VMEM = pltpu.VMEM
SMEM = pltpu.SMEM


def halves(table):
    high = table.astype(jnp.bfloat16)
    low = (table - high.astype(np.float64)).astype(jnp.bfloat16)
    return high, low


def split(value):
    high = value.astype(jnp.bfloat16)
    return high, (value - high.astype(jnp.float32)).astype(jnp.bfloat16)


def product3(left, right, dims):
    one = functools.partial(
        lax.dot_general, dimension_numbers=(dims, ((), ())), preferred_element_type=jnp.float32
    )
    return one(left[0], right[0]) + (one(left[1], right[0]) + one(left[0], right[1]))


def turned(value):
    wide = value.shape[1] // 2
    swapped = jnp.concatenate([-value[:, wide:], value[:, :wide]], axis=1)
    return jnp.concatenate([value, swapped], axis=0)


def angles(space, freq):
    turns = np.outer(np.arange(freq), np.arange(space)) % freq
    return turns * (2.0 * math.pi / freq)


def column_table(space, blocks):
    angle = angles(space, 2 * space).reshape(blocks, -1, space)
    return halves(np.concatenate([np.cos(angle), -np.sin(angle)], axis=1))


def forward_table(space):
    angle = angles(space, 2 * space)
    return halves(np.concatenate([np.cos(angle), -np.sin(angle)], axis=1))


def inverse_table(space):
    angle = angles(space, 2 * space).T
    return halves(np.concatenate([np.cos(angle), np.sin(angle)], axis=1))


def times(value, turns, length):
    turns %= length
    re, im = value
    if turns == 0:
        return value
    if 4 * turns == length:
        return -im, re
    if 2 * turns == length:
        return -re, -im
    if 4 * turns == 3 * length:
        return im, -re
    c = math.cos(2.0 * math.pi * turns / length)
    s = math.sin(2.0 * math.pi * turns / length)
    if 8 * turns % length == 0:
        r = math.sqrt(0.5)
        if c * s > 0:
            return math.copysign(r, c) * (re - im), math.copysign(r, c) * (re + im)
        return math.copysign(r, c) * (re + im), math.copysign(r, c) * (im - re)
    return c * re - s * im, c * im + s * re


def add(a, b):
    return a[0] + b[0], a[1] + b[1]


def sub(a, b):
    return a[0] - b[0], a[1] - b[1]


def fft(values, sign):
    count = len(values)
    if count == 1:
        return values
    even, odd = fft(values[0::2], sign), fft(values[1::2], sign)
    odd = [times(v, sign * k, count) for k, v in enumerate(odd)]
    return [add(a, b) for a, b in zip(even, odd)] + [sub(a, b) for a, b in zip(even, odd)]


def forward_kernel(x_ref, yh_ref, yl_ref, th_ref, tl_ref, out_ref):
    table_y = (yh_ref[...], yl_ref[...])
    table_x = (th_ref[...], tl_ref[...])
    spec = product3(split(x_ref[0]), table_y, ((1,), (1,)))
    both = product3(table_x, split(turned(spec)), ((1,), (0,)))
    out_ref[:, 0] = both.reshape(out_ref.shape[0], *out_ref.shape[2:])


def forward(rows, table_y, table_x, blocks):
    slabs, width, height = rows.shape
    wide = table_y[0].shape[0]
    kx = 2 * width // blocks
    whole = lambda a: pl.BlockSpec(a.shape, lambda z: (0,) * a.ndim)
    return pl.pallas_call(
        forward_kernel,
        grid=(slabs,),
        in_specs=[pl.BlockSpec((1, width, height), lambda z: (z, 0, 0))]
        + [whole(a) for a in (*table_y, *table_x)],
        out_specs=pl.BlockSpec((blocks, 1, kx, wide), lambda z: (0, z, 0, 0)),
        out_shape=jax.ShapeDtypeStruct((blocks, slabs, kx, wide), jnp.float32),
        name="forward_xy",
    )(rows, *table_y, *table_x)


def middle_kernel(f_ref, g_ref, h_ref, out_ref):
    slabs = f_ref.shape[1]
    depth = f_ref.shape[0] * slabs
    length = 2 * depth
    half = f_ref.shape[3] // 2
    field = [
        (f_ref[z // slabs, z % slabs, :, :half], f_ref[z // slabs, z % slabs, :, half:])
        for z in range(depth)
    ]
    even = fft(field, -1)
    odd = fft([times(v, -z, length) for z, v in enumerate(field)], -1)
    spec = [v for pair in zip(even, odd) for v in pair]
    product = []
    for k in range(length):
        re, im = spec[k]
        mre, mim = times(spec[-k % length], -k * (depth - 1), length)
        gre, gim, hre, him = g_ref[0, k], g_ref[1, k], h_ref[0, k], h_ref[1, k]
        product.append(
            (
                gre * re - gim * im + hre * mre - him * mim,
                gre * im + gim * re + hre * mim + him * mre,
            )
        )
    even = fft(product[0::2], 1)
    odd = fft(product[1::2], 1)
    for z in range(depth):
        re, im = add(even[z], times(odd[z], z, length))
        out_ref[z // slabs, z % slabs, :, :half] = re
        out_ref[z // slabs, z % slabs, :, half:] = im


def middle(field, green, image_green):
    blocks, slabs, kx, wide = field.shape
    tile = 8
    spec = pl.BlockSpec((blocks, slabs, tile, wide), lambda i: (0, 0, i, 0))
    gspec = pl.BlockSpec((*green.shape[:2], tile, green.shape[3]), lambda i: (0, 0, i, 0))
    return pl.pallas_call(
        middle_kernel,
        grid=(kx // tile,),
        in_specs=[spec, gspec, gspec],
        out_specs=spec,
        out_shape=jax.ShapeDtypeStruct(field.shape, jnp.float32),
        name="middle_z",
    )(field, green, image_green)


def inverse_x_kernel(q_ref, th_ref, tl_ref, out_ref):
    field = q_ref[:, 0].reshape(-1, q_ref.shape[3])
    rows = product3((th_ref[...], tl_ref[...]), split(turned(field)), ((1,), (0,)))
    parts = out_ref.shape[0]
    count = rows.shape[0] // parts
    for part in range(parts):
        start = part * count
        before, after = max(start - 1, 0), min(start + count, rows.shape[0] - 1)
        out_ref[part, 0, :count] = rows[start : start + count]
        out_ref[part, 0, count : count + 8] = jnp.concatenate(
            [rows[before : before + 1], rows[after : after + 1], rows[:6]], axis=0
        )


def inverse_x(field, table, parts):
    blocks, slabs, kx, wide = field.shape
    width = blocks * kx // 2
    whole = lambda a: pl.BlockSpec(a.shape, lambda z: (0,) * a.ndim)
    shape = (parts, slabs, width // parts + 8, wide)
    return pl.pallas_call(
        inverse_x_kernel,
        grid=(slabs,),
        in_specs=[pl.BlockSpec((blocks, 1, kx, wide), lambda z: (0, z, 0, 0))]
        + [whole(a) for a in table],
        out_specs=pl.BlockSpec((parts, 1, *shape[2:]), lambda z: (0, z, 0, 0)),
        out_shape=jax.ShapeDtypeStruct(shape, jnp.float32),
        name="inverse_x",
    )(field, *table)


def inverse_y_kernel(scale, parts, me_ref, s_ref, th_ref, tl_ref, pot_ref, gx_ref, gy_ref):
    me = me_ref[0]
    count = s_ref.shape[2] - 8
    height = th_ref.shape[2]
    for z in range(s_ref.shape[1]):
        total = None
        for part in range(parts):
            term = product3(
                split(s_ref[part, z]), (th_ref[part], tl_ref[part]), ((1,), (0,))
            )
            total = term if total is None else total + term
        total = total * scale
        main = total[:count]
        row = lax.broadcasted_iota(jnp.int32, main.shape, 0)
        before = jnp.where(row == 0, total[count : count + 1], pltpu.roll(main, 1, 0))
        after = jnp.where(
            row == count - 1, total[count + 1 : count + 2], pltpu.roll(main, count - 1, 0)
        )
        edge = ((row == 0) & (me == 0)) | ((row == count - 1) & (me == parts - 1))
        gx_ref[z] = (after - before) * jnp.where(edge, 1.0, 0.5)
        col = lax.broadcasted_iota(jnp.int32, main.shape, 1)
        before = jnp.where(col == 0, main, pltpu.roll(main, 1, 1))
        after = jnp.where(col == height - 1, main, pltpu.roll(main, height - 1, 1))
        gy_ref[z] = (after - before) * jnp.where((col == 0) | (col == height - 1), 1.0, 0.5)
        pot_ref[z] = main


def inverse_y(rows, table, me, scale):
    parts, slabs, count, _ = rows.shape
    shape = jax.ShapeDtypeStruct((slabs, count - 8, table[0].shape[2]), jnp.float32)
    vmem = pl.BlockSpec(memory_space=VMEM)
    return pl.pallas_call(
        functools.partial(inverse_y_kernel, scale, parts),
        in_specs=[pl.BlockSpec(memory_space=SMEM), vmem, vmem, vmem],
        out_specs=(vmem, vmem, vmem),
        out_shape=(shape, shape, shape),
        name="inverse_y",
    )(me, rows, *table)


def slope_z(pot):
    slabs = pot.shape[0]
    size, me = lax.axis_size("gz"), lax.axis_index("gz")
    below = lax.ppermute(pot[-1], "gz", [(i, i + 1) for i in range(size - 1)])
    above = lax.ppermute(pot[0], "gz", [(i + 1, i) for i in range(size - 1)])
    below = jnp.where(me == 0, pot[0], below)
    above = jnp.where(me == size - 1, pot[-1], above)
    padded = jnp.concatenate([below[None], pot, above[None]])
    row = lax.broadcasted_iota(jnp.int32, (slabs, 1, 1), 0)
    edge = ((row == 0) & (me == 0)) | ((row == slabs - 1) & (me == size - 1))
    return (padded[2:] - padded[:-2]) * jnp.where(edge, 1.0, 0.5)


def per_device(density, green, image_green):
    slabs, _, height = density.shape
    gz, gx = lax.axis_size("gz"), lax.axis_size("gx")
    width = density.shape[1] * gx
    depth = slabs * gz
    column = column_table(height, gx)
    me = lax.axis_index("gx")
    own = tuple(lax.dynamic_index_in_dim(jnp.asarray(t), me, 0, keepdims=False) for t in column)
    rows = lax.all_gather(density, "gx", axis=1, tiled=True)
    field = forward(rows, own, forward_table(width), gz)
    field = lax.all_to_all(field, "gz", split_axis=0, concat_axis=0, tiled=True)
    field = middle(field, green, image_green)
    field = lax.all_to_all(field, "gz", split_axis=0, concat_axis=0, tiled=True)
    part = inverse_x(field, inverse_table(width), gx)
    part = lax.all_to_all(part, "gx", split_axis=0, concat_axis=0, tiled=True)
    scale = 1.0 / (8.0 * depth * width * height)
    pot, grad_x, grad_y = inverse_y(part, column, me.astype(jnp.int32).reshape(1), scale)
    return grad_x, grad_y, slope_z(pot)


def solution(mesh):
    return jax.shard_map(
        per_device,
        mesh=mesh,
        in_specs=(P("gz", "gx", None), P(None, None, "gz", "gx"), P(None, None, "gz", "gx")),
        out_specs=(P("gz", "gx", None), P("gz", "gx", None), P("gz", "gx", None)),
        check_vma=False,
    )
```

profile of v0, /device:TPU:8, one launch (start us, length us, event | category | flops | bytes accessed | tf_op | source)
XLA Modules:
  0.0 117.8 jit_solution(14282341256925318336)
XLA Ops:
  0.6 8.7 %all_gather.3.x_ref = f32[2,256,256]{2,1,0:T(8,128)} all-gather(f32[2,64,256]{2,1,0:T(8,128)} %param.9), channel_id=1, replica_groups=mesh['gz'=8,'gx'=4] {'gx'}, dimensions={1}, use_global_device_ids=true | all-gather | bytes 655360 | tf_op jit(solution)/shard_map/all_gather | solution.py:259
  9.4 1.7 %dynamic-slice_bitcast_fusion = (bf16[256,256]{1,0:T(8,128)(2,1)}, bf16[256,256]{1,0:T(8,128)(2,1)}) fusion(bf16[4,256,256]{2,1,0:T(8,128)(2,1)} %constant.40.clone.tl_ref, s32[]{:T(128)S(6)} %select_n.28, bf16[4,256,256]{2,1,0:T(8,128)(2,1)} %constant.39.clone.th_ref), kind=kLoop, calls=%fused_computation.4 | loop fusion | bytes 524292 | tf_op jit(solution)/shard_map/jit(dynamic_index_in_dim)/squeeze | solution.py:258
  11.1 4.4 %forward_xy.1 = f32[8,2,64,256]{3,2,1,0:T(8,128)} custom-call(f32[2,256,256]{2,1,0:T(8,128)} %all_gather.3.x_ref, bf16[256,256]{1,0:T(8,128)(2,1)} %get-tuple-element.14.yh_ref, bf16[256,256]{1,0:T(8,128)(2,1)} %get-tuple-element.13.yl_ref, bf16[512,512]{1,0:T(8,128)(2,1)} %constant.41.clone.th_ref, bf16[512,512]{1,0:T(8,128)(2,1)} %constant.42.clone.tl_ref), custom_call_target="tpu_custom_call" | custom-call | tf_op jit(solution)/shard_map/forward_xy/pallas_call | solution.py:111
  15.4 31.7 %all_to_all.15.f_ref = f32[8,2,64,256]{3,2,1,0:T(8,128)} all-to-all(f32[8,2,64,256]{3,2,1,0:T(8,128)} %forward_xy.1), channel_id=1, replica_groups=mesh['gz'=8,'gx'=4] {'gz'}, dimensions={0} | all-to-all | bytes 2097152 | tf_op jit(solution)/shard_map/all_to_all | solution.py:261
  47.1 6.9 %middle_z.1 = f32[8,2,64,256]{3,2,1,0:T(8,128)} custom-call(f32[8,2,64,256]{3,2,1,0:T(8,128)} %all_to_all.15.f_ref, f32[2,32,64,128]{3,2,1,0:T(8,128)} %g_ref.1, f32[2,32,64,128]{3,2,1,0:T(8,128)} %h_ref.1), custom_call_target="tpu_custom_call" | custom-call | tf_op jit(solution)/shard_map/middle_z/pallas_call | solution.py:158
  54.0 29.7 %all_to_all.16.q_ref = f32[8,2,64,256]{3,2,1,0:T(8,128)} all-to-all(f32[8,2,64,256]{3,2,1,0:T(8,128)} %middle_z.1), channel_id=1, replica_groups=mesh['gz'=8,'gx'=4] {'gz'}, dimensions={0} | all-to-all | bytes 2097152 | tf_op jit(solution)/shard_map/all_to_all | solution.py:263
  83.7 3.3 %inverse_x.1 = f32[4,2,72,256]{3,2,1,0:T(8,128)} custom-call(f32[8,2,64,256]{3,2,1,0:T(8,128)} %all_to_all.16.q_ref, bf16[256,1024]{1,0:T(8,128)(2,1)} %constant.43.clone.th_ref, bf16[256,1024]{1,0:T(8,128)(2,1)} %constant.44.clone.tl_ref), custom_call_target="tpu_custom_call" | custom-call | tf_op jit(solution)/shard_map/inverse_x/pallas_call | solution.py:187
  87.0 3.5 %all-to-all-start.2 = ((f32[4,2,72,256]{3,2,1,0:T(8,128)}), f32[4,2,72,256]{3,2,1,0:T(8,128)S(1)}, u32[]{:S(2)}, u32[]{:S(2)}) async-start(f32[4,2,72,256]{3,2,1,0:T(8,128)} %inverse_x.1), calls=%async_computation.2 | async-start | bytes 1179648 | tf_op jit(solution)/shard_map/all_to_all | solution.py:265
  90.5 9.5 %all-to-all-done.2.s_ref = f32[4,2,72,256]{3,2,1,0:T(8,128)S(1)} async-done(((f32[4,2,72,256]{3,2,1,0:T(8,128)}), f32[4,2,72,256]{3,2,1,0:T(8,128)S(1)}, u32[]{:S(2)}, u32[]{:S(2)}) %all-to-all-start.2) | async-done | bytes 589856 | tf_op jit(solution)/shard_map/all_to_all | solution.py:265
  100.0 0.0 copy-start
  100.0 0.8 copy-done
  100.8 2.8 %inverse_y.1 = (f32[2,64,256]{2,1,0:T(8,128)}, f32[2,64,256]{2,1,0:T(8,128)}, f32[2,64,256]{2,1,0:T(8,128)}) custom-call(s32[1]{0:T(128)} %bitcast.me_ref, f32[4,2,72,256]{3,2,1,0:T(8,128)} %copy-done, bf16[4,256,256]{2,1,0:T(8,128)(2,1)} %constant.39.clone.th_ref, bf16[4,256,256]{2,1,0:T(8,128)(2,1)} %constant.40.clone.tl_ref), custom_call_target="tpu_custom_call" | custom-call | tf_op jit(solution)/shard_map/inverse_y/pallas_call | solution.py:229
  103.6 0.9 slice_bitcast_fusion
  104.5 3.7 %collective-permute-start = (f32[64,256]{1,0:T(8,128)S(1)}, f32[64,256]{1,0:T(8,128)S(1)}, u32[]{:S(2)}, u32[]{:S(2)}) collective-permute-start(f32[64,256]{1,0:T(8,128)S(1)} %get-tuple-element.11), channel_id=1, source_target_pairs={{4,0},{8,4},{12,8},{16,12},{20,16},{24,20},{28,24},{5,1},{9,5},{13... | collective-permute-start | bytes 196616 | tf_op jit(solution)/shard_map/ppermute | solution.py:242
  108.3 2.1 %collective-permute-start.1 = (f32[64,256]{1,0:T(8,128)S(1)}, f32[64,256]{1,0:T(8,128)S(1)}, u32[]{:S(2)}, u32[]{:S(2)}) collective-permute-start(f32[64,256]{1,0:T(8,128)S(1)} %get-tuple-element.12), channel_id=1, source_target_pairs={{0,4},{4,8},{8,12},{12,16},{16,20},{20,24},{24,28},{1,5},{5,9},{9,... | collective-permute-start | bytes 196616 | tf_op jit(solution)/shard_map/ppermute | solution.py:241
  110.4 0.3 collective-permute-done
  110.7 4.6 %collective-permute-done.1 = f32[64,256]{1,0:T(8,128)S(1)} collective-permute-done((f32[64,256]{1,0:T(8,128)S(1)}, f32[64,256]{1,0:T(8,128)S(1)}, u32[]{:S(2)}, u32[]{:S(2)}) %collective-permute-start.1) | collective-permute-done | bytes 65568 | tf_op jit(solution)/shard_map/ppermute | solution.py:241
  115.3 0.9 select_bitcast_fusion.1
  116.2 1.6 %fusion.1 = f32[2,64,256]{2,1,0:T(8,128)} fusion(f32[2,64,256]{2,1,0:T(8,128)} %get-tuple-element.8, f32[1,64,256]{2,1,0:T(8,128)S(1)} %get-tuple-element.10, f32[1,64,256]{2,1,0:T(8,128)S(1)} %get-tuple-element.9, f32[2]{0:T(128)S(1)} %or_select_fusion), kind=kLoop, calls=%fused_computation.2 | loop fusion | flops 131072 | bytes 393224 | tf_op jit(solution)/shard_map/mul | solution.py:248
  (1 shorter events, 0.0 us)
Async XLA Ops:
  87.0 13.0 %all-to-all-start.2 = ((f32[4,2,72,256]{3,2,1,0:T(8,128)}), f32[4,2,72,256]{3,2,1,0:T(8,128)S(1)}, u32[]{:S(2)}, u32[]{:S(2)}) async-start(f32[4,2,72,256]{3,2,1,0:T(8,128)} %inverse_x.1), calls=%async_computation.2 | async-start | bytes 1179648 | tf_op jit(solution)/shard_map/all_to_all | solution.py:265
  100.0 0.8 copy-start
  104.5 6.2 %collective-permute-start = (f32[64,256]{1,0:T(8,128)S(1)}, f32[64,256]{1,0:T(8,128)S(1)}, u32[]{:S(2)}, u32[]{:S(2)}) collective-permute-start(f32[64,256]{1,0:T(8,128)S(1)} %get-tuple-element.11), channel_id=1, source_target_pairs={{4,0},{8,4},{12,8},{16,12},{20,16},{24,20},{28,24},{5,1},{9,5},{13... | collective-permute-start | bytes 196616 | tf_op jit(solution)/shard_map/ppermute | solution.py:242
  108.3 7.1 %collective-permute-start.1 = (f32[64,256]{1,0:T(8,128)S(1)}, f32[64,256]{1,0:T(8,128)S(1)}, u32[]{:S(2)}, u32[]{:S(2)}) collective-permute-start(f32[64,256]{1,0:T(8,128)S(1)} %get-tuple-element.12), channel_id=1, source_target_pairs={{0,4},{4,8},{8,12},{12,16},{16,20},{20,24},{24,28},{1,5},{5,9},{9,... | collective-permute-start | bytes 196616 | tf_op jit(solution)/shard_map/ppermute | solution.py:241
where the time goes:
time: 119 us; the launch traced here: 118 us
  blocking collectives  70.1 us (59%)
  Pallas kernels  17.4 us (15%)
  waiting for transfers between devices  14.4 us (12%)
  starting transfers between devices  9.32 us (8%)
  local copies, waits for them, and re-layouts  3.38 us (3%)
  other arithmetic  2.51 us (2%)
    all_to_all x2, blocking collectives, per_device(): field = lax.all_to_all(field, 'gz', split_axis=0, concat_axis=0, tiled=True)  61.4 us
    all_to_all x1, waiting for transfers between devices, per_device(): part = lax.all_to_all(part, 'gx', split_axis=0, concat_axis=0, tiled=True)  9.5 us
    all_gather x1, blocking collectives, per_device(): rows = lax.all_gather(density, 'gx', axis=1, tiled=True)  8.74 us
    pallas_call x1, Pallas kernels, middle(): pl.pallas_call(middle_kernel, grid=(kx // tile,), in_specs=[spec, gspec,...  6.9 us
    ppermute x1, waiting for transfers between devices, slope_z(): below = lax.ppermute(pot[-1], 'gz', [(i, i + 1) for i in range(size - 1)])  4.63 us
    pallas_call x1, Pallas kernels, forward(): pl.pallas_call(forward_kernel, grid=(slabs,), in_specs=[pl.BlockSpec((1,...  4.38 us
    ppermute x1, starting transfers between devices, slope_z(): above = lax.ppermute(pot[0], 'gz', [(i + 1, i) for i in range(size - 1)])  3.72 us
    all_to_all x1, starting transfers between devices, per_device(): part = lax.all_to_all(part, 'gx', split_axis=0, concat_axis=0, tiled=True)  3.48 us
  transfers between devices with their start and end apart: 3, of which 3 were waited for; matrix products, arithmetic and copies ran while one was open for 0% of the time, Pallas kernels for 0%

commit v1 on v0

--- a/solution.py
+++ b/solution.py
@@ -55,6 +55,17 @@
 def inverse_table(space):
     angle = angles(space, 2 * space).T
     return halves(np.concatenate([np.cos(angle), np.sin(angle)], axis=1))
+
+
+def half_inverse_table(space, parts):
+    angle = angles(space, 2 * space).T
+    count = space // parts
+    rows = []
+    for start in range(0, space, count):
+        rows += [*range(start, start + count), max(start - 1, 0), min(start + count, space - 1)]
+        rows += [start] * 6
+    angle = angle[np.array(rows)].reshape(len(rows), 2, space).transpose(1, 0, 2)
+    return halves(np.concatenate([np.cos(angle), np.sin(angle)], axis=2))
 
 
 def times(value, turns, length):
@@ -195,10 +206,23 @@
     )(field, *table)
 
 
+def differences(total, me, parts, gx_ref, gy_ref):
+    count, height = total.shape[0] - 8, total.shape[1]
+    main = total[:count]
+    row = lax.broadcasted_iota(jnp.int32, main.shape, 0)
+    before = jnp.where(row == 0, total[count : count + 1], pltpu.roll(main, 1, 0))
+    after = jnp.where(row == count - 1, total[count + 1 : count + 2], pltpu.roll(main, count - 1, 0))
+    edge = ((row == 0) & (me == 0)) | ((row == count - 1) & (me == parts - 1))
+    gx_ref[...] = (after - before) * jnp.where(edge, 1.0, 0.5)
+    col = lax.broadcasted_iota(jnp.int32, main.shape, 1)
+    before = jnp.where(col == 0, main, pltpu.roll(main, 1, 1))
+    after = jnp.where(col == height - 1, main, pltpu.roll(main, height - 1, 1))
+    gy_ref[...] = (after - before) * jnp.where((col == 0) | (col == height - 1), 1.0, 0.5)
+    return main
+
+
 def inverse_y_kernel(scale, parts, me_ref, s_ref, th_ref, tl_ref, pot_ref, gx_ref, gy_ref):
     me = me_ref[0]
-    count = s_ref.shape[2] - 8
-    height = th_ref.shape[2]
     for z in range(s_ref.shape[1]):
         total = None
         for part in range(parts):
@@ -207,18 +231,7 @@
             )
             total = term if total is None else total + term
         total = total * scale
-        main = total[:count]
-        row = lax.broadcasted_iota(jnp.int32, main.shape, 0)
-        before = jnp.where(row == 0, total[count : count + 1], pltpu.roll(main, 1, 0))
-        after = jnp.where(
-            row == count - 1, total[count + 1 : count + 2], pltpu.roll(main, count - 1, 0)
-        )
-        edge = ((row == 0) & (me == 0)) | ((row == count - 1) & (me == parts - 1))
-        gx_ref[z] = (after - before) * jnp.where(edge, 1.0, 0.5)
-        col = lax.broadcasted_iota(jnp.int32, main.shape, 1)
-        before = jnp.where(col == 0, main, pltpu.roll(main, 1, 1))
-        after = jnp.where(col == height - 1, main, pltpu.roll(main, height - 1, 1))
-        gy_ref[z] = (after - before) * jnp.where((col == 0) | (col == height - 1), 1.0, 0.5)
+        main = differences(total, me, parts, gx_ref.at[z], gy_ref.at[z])
         pot_ref[z] = main
 
 
@@ -235,21 +248,266 @@
     )(me, rows, *table)
 
 
-def slope_z(pot):
-    slabs = pot.shape[0]
+def slope_z(*pot):
+    slabs = len(pot)
     size, me = lax.axis_size("gz"), lax.axis_index("gz")
     below = lax.ppermute(pot[-1], "gz", [(i, i + 1) for i in range(size - 1)])
     above = lax.ppermute(pot[0], "gz", [(i + 1, i) for i in range(size - 1)])
     below = jnp.where(me == 0, pot[0], below)
     above = jnp.where(me == size - 1, pot[-1], above)
-    padded = jnp.concatenate([below[None], pot, above[None]])
+    padded = jnp.stack([below, *pot, above])
     row = lax.broadcasted_iota(jnp.int32, (slabs, 1, 1), 0)
     edge = ((row == 0) & (me == 0)) | ((row == slabs - 1) & (me == size - 1))
     return (padded[2:] - padded[:-2]) * jnp.where(edge, 1.0, 0.5)
 
 
+def pieces_spec(count):
+    return [pl.BlockSpec(memory_space=VMEM)] * count
+
+
+def place():
+    half = lax.axis_size("gz") // 2
+    mine = lax.axis_index("gz")
+    return jnp.stack([lax.axis_index("gx"), mine // half, mine % half]).astype(jnp.int32)
+
+
+def forward_half_kernel(at_ref, *refs):
+    parts = lax.axis_size("gx")
+    group = lax.axis_size("gz") // 2
+    me, side, member = at_ref[0], at_ref[1], at_ref[2]
+    rows, refs = refs[:parts], refs[parts:]
+    yh_ref, yl_ref, th_ref, tl_ref, *refs = refs
+    outs, (high_ref, low_ref, res_ref) = refs[:group], refs[group:]
+    table_y = (yh_ref[me], yl_ref[me])
+    table_x = (th_ref[side], tl_ref[side])
+    count = rows[0].shape[1]
+    width = count * parts
+    for z in range(rows[0].shape[0]):
+        both = jnp.concatenate([r[z] for r in rows], axis=0)
+        spec = product3(split(both), table_y, ((1,), (1,)))
+        wide = spec.shape[1] // 2
+        high, low = split(spec)
+        for k in range(parts):
+            start = pl.multiple_of((me ^ k) * count, count)
+            for ref, value in ((high_ref, high), (low_ref, low)):
+                value = value[k * count : (k + 1) * count]
+                ref[z, pl.ds(start, count), :] = value
+                ref[z, pl.ds(width + start, count), :wide] = -value[:, wide:]
+                ref[z, pl.ds(width + start, count), wide:] = value[:, :wide]
+        res = product3(table_x, (high_ref[z], low_ref[z]), ((1,), (0,)))
+        res_ref[z] = res.reshape(res_ref.shape[1:])
+        for k in range(group):
+            outs[k][z] = res_ref[z, member ^ k]
+
+
+def cost(flops, arrays):
+    size = sum(math.prod(a.shape) * a.dtype.itemsize for a in arrays)
+    return pl.CostEstimate(flops=flops, bytes_accessed=size, transcendentals=0)
+
+
+def forward_half(at, rows, table_y, table_x, group):
+    slabs, count, height = rows[0].shape
+    width = count * len(rows)
+    wide = table_y[0].shape[1]
+    kx = width // group
+    shape = jax.ShapeDtypeStruct((slabs, kx, wide), jnp.float32)
+    ins = (*rows, *table_y, *table_x)
+    return pl.pallas_call(
+        forward_half_kernel,
+        in_specs=[pl.BlockSpec(memory_space=SMEM)] + pieces_spec(len(ins)),
+        out_specs=pieces_spec(group),
+        out_shape=[shape] * group,
+        scratch_shapes=[
+            VMEM((slabs, 2 * width, wide), jnp.bfloat16),
+            VMEM((slabs, 2 * width, wide), jnp.bfloat16),
+            VMEM((slabs, group, kx, wide), jnp.float32),
+        ],
+        cost_estimate=cost(6 * slabs * width * wide * (height + 2 * width), (*ins, *[shape] * group)),
+        name="forward_half",
+    )(at, *ins)
+
+
+def middle_half_kernel(at_ref, *refs):
+    group = lax.axis_size("gz") // 2
+    side, member = at_ref[1], at_ref[2]
+    ins, (g_ref, h_ref), refs = refs[: 2 * group], refs[2 * group : 2 * group + 2], refs[2 * group + 2 :]
+    outs, (in_ref, out_ref) = refs[: 2 * group], refs[2 * group :]
+    for k in range(2 * group):
+        slab = (side ^ (k // group)) * group + (member ^ (k % group))
+        in_ref[slab] = ins[k][...]
+    middle_kernel(in_ref, g_ref, h_ref, out_ref)
+    for k in range(2 * group):
+        slab = (side ^ (k // group)) * group + (member ^ (k % group))
+        outs[k][...] = out_ref[slab]
+
+
+def middle_half(at, field, green, image_green):
+    slabs, kx, wide = field[0].shape
+    tile = 8
+    spec = pl.BlockSpec((slabs, tile, wide), lambda i: (0, i, 0))
+    gspec = pl.BlockSpec((*green.shape[:2], tile, green.shape[3]), lambda i: (0, 0, i, 0))
+    ins = (*field, green, image_green)
+    shape = jax.ShapeDtypeStruct(field[0].shape, jnp.float32)
+    return pl.pallas_call(
+        middle_half_kernel,
+        grid=(kx // tile,),
+        in_specs=[pl.BlockSpec(memory_space=SMEM)] + [spec] * len(field) + [gspec, gspec],
+        out_specs=[spec] * len(field),
+        out_shape=[shape] * len(field),
+        scratch_shapes=[VMEM((len(field), slabs, tile, wide), jnp.float32)] * 2,
+        cost_estimate=cost(30000 * kx * wide, (*ins, *[shape] * len(field))),
+        name="middle_half",
+    )(at, *ins)
+
+
+def inverse_x_half_kernel(at_ref, *refs):
+    parts = lax.axis_size("gx")
+    group = lax.axis_size("gz") // 2
+    me, side, member = at_ref[0], at_ref[1], at_ref[2]
+    ins, (th_ref, tl_ref), refs = refs[:group], refs[group : group + 2], refs[group + 2 :]
+    outs, (high_ref, low_ref, res_ref) = refs[:parts], refs[parts:]
+    table = (th_ref[side], tl_ref[side])
+    _, kx, wide = ins[0].shape
+    wide //= 2
+    for z in range(ins[0].shape[0]):
+        for k in range(group):
+            start = pl.multiple_of((member ^ k) * kx, kx)
+            for ref, value in zip((high_ref, low_ref), split(ins[k][z])):
+                ref[z, pl.ds(start, kx), :] = value
+                ref[z, pl.ds(group * kx + start, kx), :wide] = -value[:, wide:]
+                ref[z, pl.ds(group * kx + start, kx), wide:] = value[:, :wide]
+        res = product3(table, (high_ref[z], low_ref[z]), ((1,), (0,)))
+        res_ref[z] = res.reshape(res_ref.shape[1:])
+        for k in range(parts):
+            outs[k][z] = res_ref[z, me ^ k]
+
+
+def inverse_x_half(at, field, table, parts):
+    slabs, kx, wide = field[0].shape
+    width = len(field) * kx
+    count = width // parts + 8
+    shape = jax.ShapeDtypeStruct((slabs, count, wide), jnp.float32)
+    ins = (*field, *table)
+    return pl.pallas_call(
+        inverse_x_half_kernel,
+        in_specs=[pl.BlockSpec(memory_space=SMEM)] + pieces_spec(len(ins)),
+        out_specs=pieces_spec(parts),
+        out_shape=[shape] * parts,
+        scratch_shapes=[
+            VMEM((slabs, 2 * width, wide), jnp.bfloat16),
+            VMEM((slabs, 2 * width, wide), jnp.bfloat16),
+            VMEM((slabs, parts, count, wide), jnp.float32),
+        ],
+        cost_estimate=cost(12 * slabs * parts * count * width * wide, (*ins, *[shape] * parts)),
+        name="inverse_x_half",
+    )(at, *ins)
+
+
+def rows_of(ins, th_ref, tl_ref, me, z):
+    total = None
+    for k, ref in enumerate(ins):
+        term = product3(split(ref[z]), (th_ref[me ^ k], tl_ref[me ^ k]), ((1,), (0,)))
+        total = term if total is None else total + term
+    return total
+
+
+def inverse_y_partial_kernel(at_ref, *refs):
+    parts = lax.axis_size("gx")
+    ins, (th_ref, tl_ref, out_ref) = refs[:parts], refs[parts:]
+    me = at_ref[0]
+    for z in range(out_ref.shape[0]):
+        out_ref[z] = rows_of(ins, th_ref, tl_ref, me, z)
+
+
+def inverse_y_partial(at, rows, table):
+    slabs, count, wide = rows[0].shape
+    shape = jax.ShapeDtypeStruct((slabs, count, table[0].shape[2]), jnp.float32)
+    ins = (*rows, *table)
+    return pl.pallas_call(
+        inverse_y_partial_kernel,
+        in_specs=[pl.BlockSpec(memory_space=SMEM)] + pieces_spec(len(ins)),
+        out_specs=pl.BlockSpec(memory_space=VMEM),
+        out_shape=shape,
+        cost_estimate=cost(6 * slabs * count * wide * len(rows) * shape.shape[2], (*ins, shape)),
+        name="inverse_y_partial",
+    )(at, *ins)
+
+
+def inverse_y_half_kernel(scale, at_ref, *refs):
+    parts = lax.axis_size("gx")
+    ins, (other_ref, th_ref, tl_ref, low_ref, high_ref, gx_ref, gy_ref) = refs[:parts], refs[parts:]
+    me = at_ref[0]
+    slabs = gx_ref.shape[0]
+    for z in range(slabs):
+        total = (rows_of(ins, th_ref, tl_ref, me, z) + other_ref[z]) * scale
+        main = differences(total, me, parts, gx_ref.at[z], gy_ref.at[z])
+        if z == 0:
+            low_ref[...] = main
+        if z == slabs - 1:
+            high_ref[...] = main
+
+
+def inverse_y_half(at, rows, other, table, scale):
+    slabs, count, wide = rows[0].shape
+    height = table[0].shape[2]
+    full = jax.ShapeDtypeStruct((slabs, count - 8, height), jnp.float32)
+    one = jax.ShapeDtypeStruct((count - 8, height), jnp.float32)
+    ins = (*rows, other, *table)
+    shapes = [one, one, full, full]
+    return pl.pallas_call(
+        functools.partial(inverse_y_half_kernel, scale),
+        in_specs=[pl.BlockSpec(memory_space=SMEM)] + pieces_spec(len(ins)),
+        out_specs=pieces_spec(4),
+        out_shape=shapes,
+        cost_estimate=cost(6 * slabs * count * wide * len(rows) * height, (*ins, *shapes)),
+        name="inverse_y_half",
+    )(at, *ins)
+
+
+def swap(value, axis, mask):
+    return lax.ppermute(value, axis, [(s, s ^ mask) for s in range(lax.axis_size(axis))])
+
+
+def gather_rows(own):
+    pieces = [own]
+    for k in range(1, lax.axis_size("gx")):
+        low = k & -k
+        pieces.append(swap(pieces[k - low], "gx", low))
+    return pieces
+
+
+def exchange(pieces, axis):
+    return [pieces[0]] + [swap(p, axis, k) for k, p in enumerate(pieces) if k > 0]
+
+
+def halves_device(density, green, image_green):
+    slabs, _, height = density.shape
+    gz, gx = lax.axis_size("gz"), lax.axis_size("gx")
+    group = gz // 2
+    width = density.shape[1] * gx
+    column = column_table(height, gx)
+    ahead = [t.reshape(2, width, 2 * width) for t in forward_table(width)]
+    back = half_inverse_table(width, gx)
+    at = place()
+    other = swap(density, "gz", group)
+    field = []
+    for raw in (density, other):
+        pieces = forward_half(at, gather_rows(raw), column, ahead, group)
+        field += exchange(pieces, "gz")
+    field = middle_half(at, field, green, image_green)
+    part = inverse_x_half(at, exchange(field[group:], "gz"), back, gx)
+    part = inverse_y_partial(at, exchange(part, "gx"), column)
+    part = swap(part, "gz", group)
+    rows = inverse_x_half(at, exchange(field[:group], "gz"), back, gx)
+    scale = 1.0 / (8.0 * slabs * gz * width * height)
+    low, high, grad_x, grad_y = inverse_y_half(at, exchange(rows, "gx"), part, column, scale)
+    return grad_x, grad_y, slope_z(low, high)
+
+
 def per_device(density, green, image_green):
     slabs, _, height = density.shape
+    if lax.axis_size("gz") <= 8 and slabs == 2:
+        return halves_device(density, green, image_green)
     gz, gx = lax.axis_size("gz"), lax.axis_size("gx")
     width = density.shape[1] * gx
     depth = slabs * gz
@@ -265,7 +523,7 @@
     part = lax.all_to_all(part, "gx", split_axis=0, concat_axis=0, tiled=True)
     scale = 1.0 / (8.0 * depth * width * height)
     pot, grad_x, grad_y = inverse_y(part, column, me.astype(jnp.int32).reshape(1), scale)
-    return grad_x, grad_y, slope_z(pot)
+    return grad_x, grad_y, slope_z(*pot)
 
 
 def solution(mesh):

time: 119 us -> 102 us (0.86)
  the two profiles are of different devices: /device:TPU:8 before, /device:TPU:0 now
where the time goes in v1:
time: 102 us; the launch traced here: 101 us
  starting transfers between devices  34.5 us (34%)
  waiting for transfers between devices  29.4 us (29%)
  Pallas kernels  27.3 us (27%)
  local copies, waits for them, and re-layouts  5.9 us (6%)
  other arithmetic  3.13 us (3%)
    ppermute x26, starting transfers between devices, swap(): lax.ppermute(value, axis, [(s, s ^ mask) for s in range(lax.axis_size(axi...  29.8 us
    ppermute x26, waiting for transfers between devices, swap(): lax.ppermute(value, axis, [(s, s ^ mask) for s in range(lax.axis_size(axi...  25.1 us
    pallas_call x2, Pallas kernels, forward_half(): pl.pallas_call(forward_half_kernel, in_specs=[pl.BlockSpec(memory_space=S...  8 us
    pallas_call x1, Pallas kernels, middle_half(): pl.pallas_call(middle_half_kernel, grid=(kx // tile,), in_specs=[pl.Block...  7.24 us
    pallas_call x2, Pallas kernels, inverse_x_half(): pl.pallas_call(inverse_x_half_kernel, in_specs=[pl.BlockSpec(memory_space...  6.27 us
    unnamed x52, local copies, waits for them, and re-layouts  5.9 us
    ppermute x1, starting transfers between devices, slope_z(): below = lax.ppermute(pot[-1], 'gz', [(i, i + 1) for i in range(size - 1)])  3.38 us
    ppermute x1, waiting for transfers between devices, slope_z(): above = lax.ppermute(pot[0], 'gz', [(i + 1, i) for i in range(size - 1)])  3.33 us
  transfers between devices with their start and end apart: 28, of which 12 were waited for; matrix products, arithmetic and copies ran while one was open for 1% of the time, Pallas kernels for 17%

profile of v1, /device:TPU:0, one launch (start us, length us, event | category | flops | bytes accessed | tf_op | source)
XLA Modules:
  0.0 101.0 jit_solution(4747383771405297542)
XLA Ops:
  0.6 4.1 %collective-permute-start.6 = (f32[2,64,256]{2,1,0:T(8,128)}, f32[2,64,256]{2,1,0:T(8,128)S(1)}, u32[]{:S(2)}, u32[]{:S(2)}) collective-permute-start(f32[2,64,256]{2,1,0:T(8,128)} %refs_0_.1), channel_id=1, source_target_pairs={{0,16},{4,20},{8,24},{12,28},{16,0},{20,4},{24,8},{28,12},{1,17},{... | collective-permute-start | bytes 393224 | tf_op jit(solution)/shard_map/ppermute | solution.py:468
  6.2 5.0 %collective-permute-done.6.refs_0_ = f32[2,64,256]{2,1,0:T(8,128)S(1)} collective-permute-done((f32[2,64,256]{2,1,0:T(8,128)}, f32[2,64,256]{2,1,0:T(8,128)S(1)}, u32[]{:S(2)}, u32[]{:S(2)}) %collective-permute-start.6) | collective-permute-done | bytes 131104 | tf_op jit(solution)/shard_map/ppermute | solution.py:468
  11.3 1.5 %collective-permute-start.8 = (f32[2,64,256]{2,1,0:T(8,128)S(1)}, f32[2,64,256]{2,1,0:T(8,128)S(1)}, u32[]{:S(2)}, u32[]{:S(2)}) collective-permute-start(f32[2,64,256]{2,1,0:T(8,128)S(1)} %collective-permute-done.6.refs_0_), channel_id=1, source_target_pairs={{0,2},{1,3},{2,0},{3,1},{4,6},{5,7},{6,4},{7,5},{8,10},{9,11},{10,... | collective-permute-start | bytes 393224 | tf_op jit(solution)/shard_map/ppermute | solution.py:468
  14.0 2.2 %collective-permute-done.8.refs_2_ = f32[2,64,256]{2,1,0:T(8,128)S(1)} collective-permute-done((f32[2,64,256]{2,1,0:T(8,128)S(1)}, f32[2,64,256]{2,1,0:T(8,128)S(1)}, u32[]{:S(2)}, u32[]{:S(2)}) %collective-permute-start.8) | collective-permute-done | bytes 131104 | tf_op jit(solution)/shard_map/ppermute | solution.py:468
  17.6 4.0 %forward_half.2 = (f32[2,64,256]{2,1,0:T(8,128)}, f32[2,64,256]{2,1,0:T(8,128)}, f32[2,64,256]{2,1,0:T(8,128)}, f32[2,64,256]{2,1,0:T(8,128)}) custom-call(s32[3]{0:T(128)} %pad_add_fusion.at_ref, f32[2,64,256]{2,1,0:T(8,128)} %refs_0_.1, f32[2,64,256]{2,1,0:T(8,128)} %copy-done.10, f32[2,64,256]{2,1,0:T(8,128)} %copy-done.9, f32[2,64,256]{2,1,0:T(8,128)} %copy-done.11, ...), custom_call_target="tpu_custom_call" | custom-call | flops 603979776 | bytes 3145728 | tf_op jit(solution)/shard_map/forward_half/pallas_call | solution.py:315
  21.6 1.6 %collective-permute-start.3 = (f32[2,64,256]{2,1,0:T(8,128)}, f32[2,64,256]{2,1,0:T(8,128)S(1)}, u32[]{:S(2)}, u32[]{:S(2)}) collective-permute-start(f32[2,64,256]{2,1,0:T(8,128)} %get-tuple-element.32), channel_id=1, source_target_pairs={{0,4},{4,0},{8,12},{12,8},{16,20},{20,16},{24,28},{28,24},{1,5},{5... | collective-permute-start | bytes 393224 | tf_op jit(solution)/shard_map/ppermute | solution.py:468
  26.4 4.0 %forward_half.3 = (f32[2,64,256]{2,1,0:T(8,128)}, f32[2,64,256]{2,1,0:T(8,128)}, f32[2,64,256]{2,1,0:T(8,128)}, f32[2,64,256]{2,1,0:T(8,128)}) custom-call(s32[3]{0:T(128)} %pad_add_fusion.at_ref, f32[2,64,256]{2,1,0:T(8,128)} %copy-done.7, f32[2,64,256]{2,1,0:T(8,128)} %copy-done.18, f32[2,64,256]{2,1,0:T(8,128)} %copy-done.8, f32[2,64,256]{2,1,0:T(8,128)} %copy-done.21, ...), custom_call_target="tpu_custom_call" | custom-call | flops 603979776 | bytes 3145728 | tf_op jit(solution)/shard_map/forward_half/pallas_call | solution.py:315
  30.4 1.6 %collective-permute-start.10 = (f32[2,64,256]{2,1,0:T(8,128)}, f32[2,64,256]{2,1,0:T(8,128)S(1)}, u32[]{:S(2)}, u32[]{:S(2)}) collective-permute-start(f32[2,64,256]{2,1,0:T(8,128)} %get-tuple-element.36), channel_id=1, source_target_pairs={{0,4},{4,0},{8,12},{12,8},{16,20},{20,16},{24,28},{28,24},{1,5},{5... | collective-permute-start | bytes 393224 | tf_op jit(solution)/shard_map/ppermute | solution.py:468
  33.9 1.7 %collective-permute-done.10.refs_5_ = f32[2,64,256]{2,1,0:T(8,128)S(1)} collective-permute-done((f32[2,64,256]{2,1,0:T(8,128)}, f32[2,64,256]{2,1,0:T(8,128)S(1)}, u32[]{:S(2)}, u32[]{:S(2)}) %collective-permute-start.10) | collective-permute-done | bytes 131104 | tf_op jit(solution)/shard_map/ppermute | solution.py:468
  35.6 2.7 %collective-permute-done.11.refs_6_ = f32[2,64,256]{2,1,0:T(8,128)S(1)} collective-permute-done((f32[2,64,256]{2,1,0:T(8,128)}, f32[2,64,256]{2,1,0:T(8,128)S(1)}, u32[]{:S(2)}, u32[]{:S(2)}) %collective-permute-start.11) | collective-permute-done | bytes 131104 | tf_op jit(solution)/shard_map/ppermute | solution.py:468
  40.5 7.2 %middle_half.1 = (f32[2,64,256]{2,1,0:T(8,128)}, f32[2,64,256]{2,1,0:T(8,128)}, f32[2,64,256]{2,1,0:T(8,128)}, f32[2,64,256]{2,1,0:T(8,128)}, f32[2,64,256]{2,1,...) custom-call(s32[3]{0:T(128)} %pad_add_fusion.at_ref, ...), custom_call_target="tpu_custom_call" | custom-call | flops 491520000 | bytes 6291456 | tf_op jit(solution)/shard_map/middle_half/pallas_call | solution.py:351
  55.1 2.6 %collective-permute-start.15 = (f32[2,64,256]{2,1,0:T(8,128)}, f32[2,64,256]{2,1,0:T(8,128)S(1)}, u32[]{:S(2)}, u32[]{:S(2)}) collective-permute-start(f32[2,64,256]{2,1,0:T(8,128)} %get-tuple-element.42), channel_id=1, source_target_pairs={{0,12},{4,8},{8,4},{12,0},{16,28},{20,24},{24,20},{28,16},{1,13},{... | collective-permute-start | bytes 393224 | tf_op jit(solution)/shard_map/ppermute | solution.py:468
  59.5 3.1 %inverse_x_half.3 = (f32[2,72,256]{2,1,0:T(8,128)}, f32[2,72,256]{2,1,0:T(8,128)}, f32[2,72,256]{2,1,0:T(8,128)}, f32[2,72,256]{2,1,0:T(8,128)}) custom-call(s32[3]{0:T(128)} %pad_add_fusion.at_ref, f32[2,64,256]{2,1,0:T(8,128)} %get-tuple-element.47.refs_0_, f32[2,64,256]{2,1,0:T(8,128)} %copy-done.23, f32[2,64,256]{2,1,0:T(8,128)} %copy-done.24, ...), custom_call_target="tpu_custom_call" | custom-call | flops 452984832 | bytes 2293760 | tf_op jit(solution)/shard_map/inverse_x_half/pallas_call | solution.py:391
  62.6 1.6 %collective-permute-start.23 = (f32[2,72,256]{2,1,0:T(8,128)}, f32[2,72,256]{2,1,0:T(8,128)S(1)}, u32[]{:S(2)}, u32[]{:S(2)}) collective-permute-start(f32[2,72,256]{2,1,0:T(8,128)} %get-tuple-element.53), channel_id=1, source_target_pairs={{0,2},{1,3},{2,0},{3,1},{4,6},{5,7},{6,4},{7,5},{8,10},{9,11},{10,... | collective-permute-start | bytes 442376 | tf_op jit(solution)/shard_map/ppermute | solution.py:468
  65.2 3.1 %inverse_x_half.2 = (f32[2,72,256]{2,1,0:T(8,128)}, f32[2,72,256]{2,1,0:T(8,128)}, f32[2,72,256]{2,1,0:T(8,128)}, f32[2,72,256]{2,1,0:T(8,128)}) custom-call(s32[3]{0:T(128)} %pad_add_fusion.at_ref, f32[2,64,256]{2,1,0:T(8,128)} %get-tuple-element.39.refs_0_, f32[2,64,256]{2,1,0:T(8,128)} %copy-done.15, f32[2,64,256]{2,1,0:T(8,128)} %copy-done.16, ...), custom_call_target="tpu_custom_call" | custom-call | flops 452984832 | bytes 2293760 | tf_op jit(solution)/shard_map/inverse_x_half/pallas_call | solution.py:391
  68.6 1.5 %collective-permute-start.17 = (f32[2,72,256]{2,1,0:T(8,128)}, f32[2,72,256]{2,1,0:T(8,128)S(1)}, u32[]{:S(2)}, u32[]{:S(2)}) collective-permute-start(f32[2,72,256]{2,1,0:T(8,128)} %get-tuple-element.45), channel_id=1, source_target_pairs={{0,2},{1,3},{2,0},{3,1},{4,6},{5,7},{6,4},{7,5},{8,10},{9,11},{10,... | collective-permute-start | bytes 442376 | tf_op jit(solution)/shard_map/ppermute | solution.py:468
  70.2 1.6 %collective-permute-done.24.refs_3_ = f32[2,72,256]{2,1,0:T(8,128)S(1)} collective-permute-done((f32[2,72,256]{2,1,0:T(8,128)}, f32[2,72,256]{2,1,0:T(8,128)S(1)}, u32[]{:S(2)}, u32[]{:S(2)}) %collective-permute-start.24) | collective-permute-done | bytes 147488 | tf_op jit(solution)/shard_map/ppermute | solution.py:468
  72.5 2.8 %inverse_y_partial.1 = f32[2,72,256]{2,1,0:T(8,128)} custom-call(s32[3]{0:T(128)} %pad_add_fusion.at_ref, f32[2,72,256]{2,1,0:T(8,128)} %get-tuple-element.51.refs_0_, f32[2,72,256]{2,1,0:T(8,128)} %copy-done.1, f32[2,72,256]{2,1,0:T(8,128)} %copy-done.3, f32[2,72,256]{2,1,0:T(8,128)} %copy-done.5, bf16[4,256,256]{2,1,0:T(8,128)(2,1)} %constant.56.clone.refs_4_.refs_5_, ...), custom_call_target="tpu_custom_call" | custom-call | flops 226492416 | bytes 1785856 | tf_op jit(solution)/shard_map/inverse_y_partial/pallas_call | solution.py:426
  75.3 2.6 %collective-permute-start.25 = (f32[2,72,256]{2,1,0:T(8,128)}, f32[2,72,256]{2,1,0:T(8,128)S(1)}, u32[]{:S(2)}, u32[]{:S(2)}) collective-permute-start(f32[2,72,256]{2,1,0:T(8,128)} %inverse_y_partial.1), channel_id=1, source_target_pairs={{0,16},{4,20},{8,24},{12,28},{16,0},{20,4},{24,8},{28,12},{1,17},{... | collective-permute-start | bytes 442376 | tf_op jit(solution)/shard_map/ppermute | solution.py:468
  78.1 7.8 %collective-permute-done.25.refs_4_ = f32[2,72,256]{2,1,0:T(8,128)S(1)} collective-permute-done((f32[2,72,256]{2,1,0:T(8,128)}, f32[2,72,256]{2,1,0:T(8,128)S(1)}, u32[]{:S(2)}, u32[]{:S(2)}) %collective-permute-start.25) | collective-permute-done | bytes 147488 | tf_op jit(solution)/shard_map/ppermute | solution.py:468
  86.6 2.9 %inverse_y_half.1 = (f32[64,256]{1,0:T(8,128)}, f32[64,256]{1,0:T(8,128)}, f32[2,64,256]{2,1,0:T(8,128)}, f32[2,64,256]{2,1,0:T(8,128)}) custom-call(s32[3]{0:T(128)} %pad_add_fusion.at_ref, f32[2,72,256]{2,1,0:T(8,128)} %get-tuple-element.43.refs_0_, f32[2,72,256]{2,1,0:T(8,128)} %copy-done, f32[2,72,256]{2,1,0:T(8,128)} %copy-done.2, ...), custom_call_target="tpu_custom_call" | custom-call | flops 226492416 | bytes 2179072 | tf_op jit(solution)/shard_map/inverse_y_half/pallas_call | solution.py:457
  89.6 3.4 %collective-permute-start.27 = (f32[64,256]{1,0:T(8,128)}, f32[64,256]{1,0:T(8,128)S(1)}, u32[]{:S(2)}, u32[]{:S(2)}) collective-permute-start(f32[64,256]{1,0:T(8,128)} %get-tuple-element.57), channel_id=1, source_target_pairs={{0,4},{4,8},{8,12},{12,16},{16,20},{20,24},{24,28},{1,5},{5,9},{9,... | collective-permute-start | bytes 196616 | tf_op jit(solution)/shard_map/ppermute | solution.py:254
  96.0 3.3 %collective-permute-done.26 = f32[64,256]{1,0:T(8,128)S(1)} collective-permute-done((f32[64,256]{1,0:T(8,128)}, f32[64,256]{1,0:T(8,128)S(1)}, u32[]{:S(2)}, u32[]{:S(2)}) %collective-permute-start.26) | collective-permute-done | bytes 65568 | tf_op jit(solution)/shard_map/ppermute | solution.py:255
  99.3 1.6 %fusion = f32[2,64,256]{2,1,0:T(8,128)} fusion(f32[1,64,256]{2,1,0:T(8,128)S(1)} %select_bitcast_fusion.1, f32[1,64,256]{2,1,0:T(8,128)} %bitcast.10, f32[1,64,256]{2,1,0:T(8,128)} %bitcast.9, f32[1,64,256]{2,1,0:T(8,128)S(1)} %select_bitcast_fusion, f32[2]{0:T(128)S(1)} %or_select_fusion), kind=kLoop, calls=%fused_computation.1 | loop fusion | flops 131072 | bytes 393224 | tf_op jit(solution)/shard_map/mul | solution.py:261
  (96 shorter events, 26.3 us)
Async XLA Ops:
  0.6 10.6 %collective-permute-start.6 = (f32[2,64,256]{2,1,0:T(8,128)}, f32[2,64,256]{2,1,0:T(8,128)S(1)}, u32[]{:S(2)}, u32[]{:S(2)}) collective-permute-start(f32[2,64,256]{2,1,0:T(8,128)} %refs_0_.1), channel_id=1, source_target_pairs={{0,16},{4,20},{8,24},{12,28},{16,0},{20,4},{24,8},{28,12},{1,17},{... | collective-permute-start | bytes 393224 | tf_op jit(solution)/shard_map/ppermute | solution.py:468
  4.7 8.1 %collective-permute-start.1 = (f32[2,64,256]{2,1,0:T(8,128)}, f32[2,64,256]{2,1,0:T(8,128)S(1)}, u32[]{:S(2)}, u32[]{:S(2)}) collective-permute-start(f32[2,64,256]{2,1,0:T(8,128)} %refs_0_.1), channel_id=1, source_target_pairs={{0,2},{1,3},{2,0},{3,1},{4,6},{5,7},{6,4},{7,5},{8,10},{9,11},{10,... | collective-permute-start | bytes 393224 | tf_op jit(solution)/shard_map/ppermute | solution.py:468
  14.0 11.1 %collective-permute-start.7 = (f32[2,64,256]{2,1,0:T(8,128)S(1)}, f32[2,64,256]{2,1,0:T(8,128)S(1)}, u32[]{:S(2)}, u32[]{:S(2)}) collective-permute-start(f32[2,64,256]{2,1,0:T(8,128)S(1)} %collective-permute-done.6.refs_0_), channel_id=1, source_target_pairs={{0,1},{1,0},{2,3},{3,2},{4,5},{5,4},{6,7},{7,6},{8,9},{9,8},{10,11... | collective-permute-start | bytes 393224 | tf_op jit(solution)/shard_map/ppermute | solution.py:468
  16.2 8.8 %collective-permute-start.9 = (f32[2,64,256]{2,1,0:T(8,128)S(1)}, f32[2,64,256]{2,1,0:T(8,128)S(1)}, u32[]{:S(2)}, u32[]{:S(2)}) collective-permute-start(f32[2,64,256]{2,1,0:T(8,128)S(1)} %collective-permute-done.8.refs_2_), channel_id=1, source_target_pairs={{0,1},{1,0},{2,3},{3,2},{4,5},{5,4},{6,7},{7,6},{8,9},{9,8},{10,11... | collective-permute-start | bytes 393224 | tf_op jit(solution)/shard_map/ppermute | solution.py:468
  21.6 11.6 %collective-permute-start.3 = (f32[2,64,256]{2,1,0:T(8,128)}, f32[2,64,256]{2,1,0:T(8,128)S(1)}, u32[]{:S(2)}, u32[]{:S(2)}) collective-permute-start(f32[2,64,256]{2,1,0:T(8,128)} %get-tuple-element.32), channel_id=1, source_target_pairs={{0,4},{4,0},{8,12},{12,8},{16,20},{20,16},{24,28},{28,24},{1,5},{5... | collective-permute-start | bytes 393224 | tf_op jit(solution)/shard_map/ppermute | solution.py:468
  23.1 10.8 %collective-permute-start.4 = (f32[2,64,256]{2,1,0:T(8,128)}, f32[2,64,256]{2,1,0:T(8,128)S(1)}, u32[]{:S(2)}, u32[]{:S(2)}) collective-permute-start(f32[2,64,256]{2,1,0:T(8,128)} %get-tuple-element.33), channel_id=1, source_target_pairs={{0,8},{4,12},{8,0},{12,4},{16,24},{20,28},{24,16},{28,20},{1,9},{5... | collective-permute-start | bytes 393224 | tf_op jit(solution)/shard_map/ppermute | solution.py:468
  24.4 9.5 %collective-permute-start.5 = (f32[2,64,256]{2,1,0:T(8,128)}, f32[2,64,256]{2,1,0:T(8,128)S(1)}, u32[]{:S(2)}, u32[]{:S(2)}) collective-permute-start(f32[2,64,256]{2,1,0:T(8,128)} %get-tuple-element.34), channel_id=1, source_target_pairs={{0,12},{4,8},{8,4},{12,0},{16,28},{20,24},{24,20},{28,16},{1,13},{... | collective-permute-start | bytes 393224 | tf_op jit(solution)/shard_map/ppermute | solution.py:468
  31.9 6.4 %collective-permute-start.11 = (f32[2,64,256]{2,1,0:T(8,128)}, f32[2,64,256]{2,1,0:T(8,128)S(1)}, u32[]{:S(2)}, u32[]{:S(2)}) collective-permute-start(f32[2,64,256]{2,1,0:T(8,128)} %get-tuple-element.37), channel_id=1, source_target_pairs={{0,8},{4,12},{8,0},{12,4},{16,24},{20,28},{24,16},{28,20},{1,9},{5... | collective-permute-start | bytes 393224 | tf_op jit(solution)/shard_map/ppermute | solution.py:468
  33.2 6.6 %collective-permute-start.12 = (f32[2,64,256]{2,1,0:T(8,128)}, f32[2,64,256]{2,1,0:T(8,128)S(1)}, u32[]{:S(2)}, u32[]{:S(2)}) collective-permute-start(f32[2,64,256]{2,1,0:T(8,128)} %get-tuple-element.38), channel_id=1, source_target_pairs={{0,12},{4,8},{8,4},{12,0},{16,28},{20,24},{24,20},{28,16},{1,13},{... | collective-permute-start | bytes 393224 | tf_op jit(solution)/shard_map/ppermute | solution.py:468
  47.7 7.4 %collective-permute-start.19 = (f32[2,64,256]{2,1,0:T(8,128)}, f32[2,64,256]{2,1,0:T(8,128)S(1)}, u32[]{:S(2)}, u32[]{:S(2)}) collective-permute-start(f32[2,64,256]{2,1,0:T(8,128)} %get-tuple-element.48), channel_id=1, source_target_pairs={{0,4},{4,0},{8,12},{12,8},{16,20},{20,16},{24,28},{28,24},{1,5},{5... | collective-permute-start | bytes 393224 | tf_op jit(solution)/shard_map/ppermute | solution.py:468
  49.1 8.6 %collective-permute-start.20 = (f32[2,64,256]{2,1,0:T(8,128)}, f32[2,64,256]{2,1,0:T(8,128)S(1)}, u32[]{:S(2)}, u32[]{:S(2)}) collective-permute-start(f32[2,64,256]{2,1,0:T(8,128)} %get-tuple-element.49), channel_id=1, source_target_pairs={{0,8},{4,12},{8,0},{12,4},{16,24},{20,28},{24,16},{28,20},{1,9},{5... | collective-permute-start | bytes 393224 | tf_op jit(solution)/shard_map/ppermute | solution.py:468
  50.4 8.4 %collective-permute-start.21 = (f32[2,64,256]{2,1,0:T(8,128)}, f32[2,64,256]{2,1,0:T(8,128)S(1)}, u32[]{:S(2)}, u32[]{:S(2)}) collective-permute-start(f32[2,64,256]{2,1,0:T(8,128)} %get-tuple-element.50), channel_id=1, source_target_pairs={{0,12},{4,8},{8,4},{12,0},{16,28},{20,24},{24,20},{28,16},{1,13},{... | collective-permute-start | bytes 393224 | tf_op jit(solution)/shard_map/ppermute | solution.py:468
  51.3 12.9 %collective-permute-start.13 = (f32[2,64,256]{2,1,0:T(8,128)}, f32[2,64,256]{2,1,0:T(8,128)S(1)}, u32[]{:S(2)}, u32[]{:S(2)}) collective-permute-start(f32[2,64,256]{2,1,0:T(8,128)} %get-tuple-element.40), channel_id=1, source_target_pairs={{0,4},{4,0},{8,12},{12,8},{16,20},{20,16},{24,28},{28,24},{1,5},{5... | collective-permute-start | bytes 393224 | tf_op jit(solution)/shard_map/ppermute | solution.py:468
  52.6 11.8 %collective-permute-start.14 = (f32[2,64,256]{2,1,0:T(8,128)}, f32[2,64,256]{2,1,0:T(8,128)S(1)}, u32[]{:S(2)}, u32[]{:S(2)}) collective-permute-start(f32[2,64,256]{2,1,0:T(8,128)} %get-tuple-element.41), channel_id=1, source_target_pairs={{0,8},{4,12},{8,0},{12,4},{16,24},{20,28},{24,16},{28,20},{1,9},{5... | collective-permute-start | bytes 393224 | tf_op jit(solution)/shard_map/ppermute | solution.py:468
  55.1 9.4 %collective-permute-start.15 = (f32[2,64,256]{2,1,0:T(8,128)}, f32[2,64,256]{2,1,0:T(8,128)S(1)}, u32[]{:S(2)}, u32[]{:S(2)}) collective-permute-start(f32[2,64,256]{2,1,0:T(8,128)} %get-tuple-element.42), channel_id=1, source_target_pairs={{0,12},{4,8},{8,4},{12,0},{16,28},{20,24},{24,20},{28,16},{1,13},{... | collective-permute-start | bytes 393224 | tf_op jit(solution)/shard_map/ppermute | solution.py:468
  62.6 7.6 %collective-permute-start.22 = (f32[2,72,256]{2,1,0:T(8,128)}, f32[2,72,256]{2,1,0:T(8,128)S(1)}, u32[]{:S(2)}, u32[]{:S(2)}) collective-permute-start(f32[2,72,256]{2,1,0:T(8,128)} %get-tuple-element.52), channel_id=1, source_target_pairs={{0,1},{1,0},{2,3},{3,2},{4,5},{5,4},{6,7},{7,6},{8,9},{9,8},{10,11... | collective-permute-start | bytes 442376 | tf_op jit(solution)/shard_map/ppermute | solution.py:468
  62.6 7.6 %collective-permute-start.23 = (f32[2,72,256]{2,1,0:T(8,128)}, f32[2,72,256]{2,1,0:T(8,128)S(1)}, u32[]{:S(2)}, u32[]{:S(2)}) collective-permute-start(f32[2,72,256]{2,1,0:T(8,128)} %get-tuple-element.53), channel_id=1, source_target_pairs={{0,2},{1,3},{2,0},{3,1},{4,6},{5,7},{6,4},{7,5},{8,10},{9,11},{10,... | collective-permute-start | bytes 442376 | tf_op jit(solution)/shard_map/ppermute | solution.py:468
  64.2 7.6 %collective-permute-start.24 = (f32[2,72,256]{2,1,0:T(8,128)}, f32[2,72,256]{2,1,0:T(8,128)S(1)}, u32[]{:S(2)}, u32[]{:S(2)}) collective-permute-start(f32[2,72,256]{2,1,0:T(8,128)} %get-tuple-element.54), channel_id=1, source_target_pairs={{0,3},{1,2},{2,1},{3,0},{4,7},{5,6},{6,5},{7,4},{8,11},{9,10},{10,... | collective-permute-start | bytes 442376 | tf_op jit(solution)/shard_map/ppermute | solution.py:468
  68.3 9.6 %collective-permute-start.16 = (f32[2,72,256]{2,1,0:T(8,128)}, f32[2,72,256]{2,1,0:T(8,128)S(1)}, u32[]{:S(2)}, u32[]{:S(2)}) collective-permute-start(f32[2,72,256]{2,1,0:T(8,128)} %get-tuple-element.44), channel_id=1, source_target_pairs={{0,1},{1,0},{2,3},{3,2},{4,5},{5,4},{6,7},{7,6},{8,9},{9,8},{10,11... | collective-permute-start | bytes 442376 | tf_op jit(solution)/shard_map/ppermute | solution.py:468
  68.6 9.3 %collective-permute-start.17 = (f32[2,72,256]{2,1,0:T(8,128)}, f32[2,72,256]{2,1,0:T(8,128)S(1)}, u32[]{:S(2)}, u32[]{:S(2)}) collective-permute-start(f32[2,72,256]{2,1,0:T(8,128)} %get-tuple-element.45), channel_id=1, source_target_pairs={{0,2},{1,3},{2,0},{3,1},{4,6},{5,7},{6,4},{7,5},{8,10},{9,11},{10,... | collective-permute-start | bytes 442376 | tf_op jit(solution)/shard_map/ppermute | solution.py:468
  70.2 8.0 %collective-permute-start.18 = (f32[2,72,256]{2,1,0:T(8,128)}, f32[2,72,256]{2,1,0:T(8,128)S(1)}, u32[]{:S(2)}, u32[]{:S(2)}) collective-permute-start(f32[2,72,256]{2,1,0:T(8,128)} %get-tuple-element.46), channel_id=1, source_target_pairs={{0,3},{1,2},{2,1},{3,0},{4,7},{5,6},{6,5},{7,4},{8,11},{9,10},{10,... | collective-permute-start | bytes 442376 | tf_op jit(solution)/shard_map/ppermute | solution.py:468
  75.3 10.7 %collective-permute-start.25 = (f32[2,72,256]{2,1,0:T(8,128)}, f32[2,72,256]{2,1,0:T(8,128)S(1)}, u32[]{:S(2)}, u32[]{:S(2)}) collective-permute-start(f32[2,72,256]{2,1,0:T(8,128)} %inverse_y_partial.1), channel_id=1, source_target_pairs={{0,16},{4,20},{8,24},{12,28},{16,0},{20,4},{24,8},{28,12},{1,17},{... | collective-permute-start | bytes 442376 | tf_op jit(solution)/shard_map/ppermute | solution.py:468
  89.6 5.6 %collective-permute-start.27 = (f32[64,256]{1,0:T(8,128)}, f32[64,256]{1,0:T(8,128)S(1)}, u32[]{:S(2)}, u32[]{:S(2)}) collective-permute-start(f32[64,256]{1,0:T(8,128)} %get-tuple-element.57), channel_id=1, source_target_pairs={{0,4},{4,8},{8,12},{12,16},{16,20},{20,24},{24,28},{1,5},{5,9},{9,... | collective-permute-start | bytes 196616 | tf_op jit(solution)/shard_map/ppermute | solution.py:254
  93.0 6.4 %collective-permute-start.26 = (f32[64,256]{1,0:T(8,128)}, f32[64,256]{1,0:T(8,128)S(1)}, u32[]{:S(2)}, u32[]{:S(2)}) collective-permute-start(f32[64,256]{1,0:T(8,128)} %get-tuple-element.58), channel_id=1, source_target_pairs={{4,0},{8,4},{12,8},{16,12},{20,16},{24,20},{28,24},{5,1},{9,5},{13... | collective-permute-start | bytes 196616 | tf_op jit(solution)/shard_map/ppermute | solution.py:255
  (30 other events, 106.8 us)

commit v2 on v1

--- a/solution.py
+++ b/solution.py
@@ -11,6 +11,7 @@
 
 VMEM = pltpu.VMEM
 SMEM = pltpu.SMEM
+LIMIT = 16 * 2**20
 
 
 def halves(table):
@@ -323,6 +324,7 @@
             VMEM((slabs, group, kx, wide), jnp.float32),
         ],
         cost_estimate=cost(6 * slabs * width * wide * (height + 2 * width), (*ins, *[shape] * group)),
+        compiler_params=pltpu.CompilerParams(vmem_limit_bytes=LIMIT),
         name="forward_half",
     )(at, *ins)
 
@@ -356,6 +358,7 @@
         out_shape=[shape] * len(field),
         scratch_shapes=[VMEM((len(field), slabs, tile, wide), jnp.float32)] * 2,
         cost_estimate=cost(30000 * kx * wide, (*ins, *[shape] * len(field))),
+        compiler_params=pltpu.CompilerParams(vmem_limit_bytes=LIMIT),
         name="middle_half",
     )(at, *ins)
 
@@ -399,6 +402,7 @@
             VMEM((slabs, parts, count, wide), jnp.float32),
         ],
         cost_estimate=cost(12 * slabs * parts * count * width * wide, (*ins, *[shape] * parts)),
+        compiler_params=pltpu.CompilerParams(vmem_limit_bytes=LIMIT),
         name="inverse_x_half",
     )(at, *ins)
 
@@ -429,6 +433,7 @@
         out_specs=pl.BlockSpec(memory_space=VMEM),
         out_shape=shape,
         cost_estimate=cost(6 * slabs * count * wide * len(rows) * shape.shape[2], (*ins, shape)),
+        compiler_params=pltpu.CompilerParams(vmem_limit_bytes=LIMIT),
         name="inverse_y_partial",
     )(at, *ins)
 
@@ -460,6 +465,7 @@
         out_specs=pieces_spec(4),
         out_shape=shapes,
         cost_estimate=cost(6 * slabs * count * wide * len(rows) * height, (*ins, *shapes)),
+        compiler_params=pltpu.CompilerParams(vmem_limit_bytes=LIMIT),
         name="inverse_y_half",
     )(at, *ins)
 

time: 102 us -> 89.9 us (0.88)
  Pallas kernels: 27.3 us -> 13.6 us
  waiting for transfers between devices: 29.4 us -> 32.1 us
  other arithmetic: 3.13 us -> 0.83 us
  local copies, waits for them, and re-layouts: 5.9 us -> 7.16 us
    pallas_call x2, Pallas kernels: 8 us -> 3.99 us  [forward_half(): pl.pallas_call(forward_half_kernel, in_specs=[pl.BlockSpec(memory_space=S...]
    pallas_call x2, Pallas kernels: 6.27 us -> 2.66 us  [inverse_x_half(): pl.pallas_call(inverse_x_half_kernel, in_specs=[pl.BlockSpec(memory_space...]
    pallas_call x1, Pallas kernels: 7.24 us -> 3.78 us  [middle_half(): pl.pallas_call(middle_half_kernel, grid=(kx // tile,), in_specs=[pl.Block...]
    ppermute x26, waiting for transfers between devices: 25.1 us -> 27.2 us  [swap(): lax.ppermute(value, axis, [(s, s ^ mask) for s in range(lax.axis_size(axi...]
    pallas_call x1, Pallas kernels: 2.83 us -> 1.19 us  [inverse_y_partial(): pl.pallas_call(inverse_y_partial_kernel, in_specs=[pl.BlockSpec(memory_sp...]
    unnamed x52 -> x26, local copies, waits for them, and re-layouts: 5.9 us -> 7.16 us
  transfers between devices with their start and end apart: 28 -> 28, of which waited for: 12 -> 14; matrix products, arithmetic and copies ran while one was open for 1% -> 0% of each run, Pallas kernels for 17% -> 9%
where the time goes in v2:
time: 89.9 us; the launch traced here: 89.4 us
  starting transfers between devices  34.9 us (39%)
  waiting for transfers between devices  32.1 us (36%)
  Pallas kernels  13.6 us (15%)
  local copies, waits for them, and re-layouts  7.16 us (8%)
    ppermute x26, starting transfers between devices, swap(): lax.ppermute(value, axis, [(s, s ^ mask) for s in range(lax.axis_size(axi...  30.3 us
    ppermute x26, waiting for transfers between devices, swap(): lax.ppermute(value, axis, [(s, s ^ mask) for s in range(lax.axis_size(axi...  27.2 us
    unnamed x26, local copies, waits for them, and re-layouts  7.16 us
    ppermute x1, waiting for transfers between devices, slope_z(): above = lax.ppermute(pot[0], 'gz', [(i + 1, i) for i in range(size - 1)])  4.28 us
    pallas_call x2, Pallas kernels, forward_half(): pl.pallas_call(forward_half_kernel, in_specs=[pl.BlockSpec(memory_space=S...  3.99 us
    pallas_call x1, Pallas kernels, middle_half(): pl.pallas_call(middle_half_kernel, grid=(kx // tile,), in_specs=[pl.Block...  3.78 us
    ppermute x1, starting transfers between devices, slope_z(): below = lax.ppermute(pot[-1], 'gz', [(i, i + 1) for i in range(size - 1)])  3.34 us
    pallas_call x2, Pallas kernels, inverse_x_half(): pl.pallas_call(inverse_x_half_kernel, in_specs=[pl.BlockSpec(memory_space...  2.66 us
  transfers between devices with their start and end apart: 28, of which 14 were waited for; matrix products, arithmetic and copies ran while one was open for 0% of the time, Pallas kernels for 9%

profile of v2, /device:TPU:0, one launch (start us, length us, event | category | flops | bytes accessed | tf_op | source)
XLA Modules:
  0.0 89.4 jit_solution(7170433008577627941)
XLA Ops:
  0.6 4.1 %collective-permute-start.6 = (f32[2,64,256]{2,1,0:T(8,128)}, f32[2,64,256]{2,1,0:T(8,128)S(1)}, u32[]{:S(2)}, u32[]{:S(2)}) collective-permute-start(f32[2,64,256]{2,1,0:T(8,128)} %refs_0_.1), channel_id=1, source_target_pairs={{0,16},{4,20},{8,24},{12,28},{16,0},{20,4},{24,8},{28,12},{1,17},{... | collective-permute-start | bytes 393224 | tf_op jit(solution)/shard_map/ppermute | solution.py:474
  4.7 1.5 %collective-permute-start.1 = (f32[2,64,256]{2,1,0:T(8,128)}, f32[2,64,256]{2,1,0:T(8,128)S(1)}, u32[]{:S(2)}, u32[]{:S(2)}) collective-permute-start(f32[2,64,256]{2,1,0:T(8,128)} %refs_0_.1), channel_id=1, source_target_pairs={{0,2},{1,3},{2,0},{3,1},{4,6},{5,7},{6,4},{7,5},{8,10},{9,11},{10,... | collective-permute-start | bytes 393224 | tf_op jit(solution)/shard_map/ppermute | solution.py:474
  6.2 5.0 %collective-permute-done.6.refs_0_ = f32[2,64,256]{2,1,0:T(8,128)S(1)} collective-permute-done((f32[2,64,256]{2,1,0:T(8,128)}, f32[2,64,256]{2,1,0:T(8,128)S(1)}, u32[]{:S(2)}, u32[]{:S(2)}) %collective-permute-start.6) | collective-permute-done | bytes 131104 | tf_op jit(solution)/shard_map/ppermute | solution.py:474
  11.2 1.5 %collective-permute-start.8 = (f32[2,64,256]{2,1,0:T(8,128)S(1)}, f32[2,64,256]{2,1,0:T(8,128)S(1)}, u32[]{:S(2)}, u32[]{:S(2)}) collective-permute-start(f32[2,64,256]{2,1,0:T(8,128)S(1)} %collective-permute-done.6.refs_0_), channel_id=1, source_target_pairs={{0,2},{1,3},{2,0},{3,1},{4,6},{5,7},{6,4},{7,5},{8,10},{9,11},{10,... | collective-permute-start | bytes 393224 | tf_op jit(solution)/shard_map/ppermute | solution.py:474
  13.4 2.8 %collective-permute-done.8.refs_2_ = f32[2,64,256]{2,1,0:T(8,128)S(1)} collective-permute-done((f32[2,64,256]{2,1,0:T(8,128)S(1)}, f32[2,64,256]{2,1,0:T(8,128)S(1)}, u32[]{:S(2)}, u32[]{:S(2)}) %collective-permute-start.8) | collective-permute-done | bytes 131104 | tf_op jit(solution)/shard_map/ppermute | solution.py:474
  21.3 2.0 %forward_half.2 = (f32[2,64,256]{2,1,0:T(8,128)S(1)}, f32[2,64,256]{2,1,0:T(8,128)S(1)}, f32[2,64,256]{2,1,0:T(8,128)S(1)}, f32[2,64,256]{2,1,0:T(8,128)S(1)}) custom-call(s32[3]{0:T(128)S(1)} %pad_add_fusion.at_ref, f32[2,64,256]{2,1,0:T(8,128)S(1)} %copy-done.12, f32[2,64,256]{2,1,0:T(8,128)S(1)} %collective-permute-done.refs_1_, ...), custom_call_target="tpu_custom_call" | custom-call | flops 603979776 | bytes 3145728 | tf_op jit(solution)/shard_map/forward_half/pallas_call | solution.py:316
  23.3 1.6 %collective-permute-start.3 = (f32[2,64,256]{2,1,0:T(8,128)S(1)}, f32[2,64,256]{2,1,0:T(8,128)S(1)}, u32[]{:S(2)}, u32[]{:S(2)}) collective-permute-start(f32[2,64,256]{2,1,0:T(8,128)S(1)} %get-tuple-element.32), channel_id=1, source_target_pairs={{0,4},{4,0},{8,12},{12,8},{16,20},{20,16},{24,28},{28,24},{1,5},{5... | collective-permute-start | bytes 393224 | tf_op jit(solution)/shard_map/ppermute | solution.py:474
  29.0 2.0 %forward_half.3 = (f32[2,64,256]{2,1,0:T(8,128)S(1)}, f32[2,64,256]{2,1,0:T(8,128)S(1)}, f32[2,64,256]{2,1,0:T(8,128)S(1)}, f32[2,64,256]{2,1,0:T(8,128)S(1)}) custom-call(s32[3]{0:T(128)S(1)} %pad_add_fusion.at_ref, f32[2,64,256]{2,1,0:T(8,128)S(1)} %collective-permute-done.6.refs_0_, f32[2,64,256]{2,1,0:T(8,128)S(1)} %collective-permute-done.7.refs_1_, ...), custom_call_target="tpu_custom_call" | custom-call | flops 603979776 | bytes 3145728 | tf_op jit(solution)/shard_map/forward_half/pallas_call | solution.py:316
  31.0 1.6 %collective-permute-start.10 = (f32[2,64,256]{2,1,0:T(8,128)S(1)}, f32[2,64,256]{2,1,0:T(8,128)S(1)}, u32[]{:S(2)}, u32[]{:S(2)}) collective-permute-start(f32[2,64,256]{2,1,0:T(8,128)S(1)} %get-tuple-element.36), channel_id=1, source_target_pairs={{0,4},{4,0},{8,12},{12,8},{16,20},{20,16},{24,28},{28,24},{1,5},{5... | collective-permute-start | bytes 393224 | tf_op jit(solution)/shard_map/ppermute | solution.py:474
  34.6 1.6 %collective-permute-done.10.refs_5_ = f32[2,64,256]{2,1,0:T(8,128)S(1)} collective-permute-done((f32[2,64,256]{2,1,0:T(8,128)S(1)}, f32[2,64,256]{2,1,0:T(8,128)S(1)}, u32[]{:S(2)}, u32[]{:S(2)}) %collective-permute-start.10) | collective-permute-done | bytes 131104 | tf_op jit(solution)/shard_map/ppermute | solution.py:474
  36.1 2.7 %collective-permute-done.11.refs_6_ = f32[2,64,256]{2,1,0:T(8,128)S(1)} collective-permute-done((f32[2,64,256]{2,1,0:T(8,128)S(1)}, f32[2,64,256]{2,1,0:T(8,128)S(1)}, u32[]{:S(2)}, u32[]{:S(2)}) %collective-permute-start.11) | collective-permute-done | bytes 131104 | tf_op jit(solution)/shard_map/ppermute | solution.py:474
  38.8 1.5 %collective-permute-done.12.refs_7_ = f32[2,64,256]{2,1,0:T(8,128)S(1)} collective-permute-done((f32[2,64,256]{2,1,0:T(8,128)S(1)}, f32[2,64,256]{2,1,0:T(8,128)S(1)}, u32[]{:S(2)}, u32[]{:S(2)}) %collective-permute-start.12) | collective-permute-done | bytes 131104 | tf_op jit(solution)/shard_map/ppermute | solution.py:474
  40.3 3.8 %middle_half.1 = (f32[2,64,256]{2,1,0:T(8,128)S(1)}, f32[2,64,256]{2,1,0:T(8,128)S(1)}, f32[2,64,256]{2,1,0:T(8,128)S(1)}, f32[2,64,256]{2,1,0:T(8,128)S(1)}, f3...) custom-call(s32[3]{0:T(128)S(1)} %pad_add_fusion.at_ref, ...), custom_call_target="tpu_custom_call" | custom-call | flops 491520000 | bytes 6291456 | tf_op jit(solution)/shard_map/middle_half/pallas_call | solution.py:353
  51.3 2.8 %collective-permute-start.15 = (f32[2,64,256]{2,1,0:T(8,128)S(1)}, f32[2,64,256]{2,1,0:T(8,128)S(1)}, u32[]{:S(2)}, u32[]{:S(2)}) collective-permute-start(f32[2,64,256]{2,1,0:T(8,128)S(1)} %get-tuple-element.42), channel_id=1, source_target_pairs={{0,12},{4,8},{8,4},{12,0},{16,28},{20,24},{24,20},{28,16},{1,13},{... | collective-permute-start | bytes 393224 | tf_op jit(solution)/shard_map/ppermute | solution.py:474
  56.4 1.6 %collective-permute-start.23 = (f32[2,72,256]{2,1,0:T(8,128)S(1)}, f32[2,72,256]{2,1,0:T(8,128)S(1)}, u32[]{:S(2)}, u32[]{:S(2)}) collective-permute-start(f32[2,72,256]{2,1,0:T(8,128)S(1)} %get-tuple-element.53), channel_id=1, source_target_pairs={{0,2},{1,3},{2,0},{3,1},{4,6},{5,7},{6,4},{7,5},{8,10},{9,11},{10,... | collective-permute-start | bytes 442376 | tf_op jit(solution)/shard_map/ppermute | solution.py:474
  60.0 1.6 %collective-permute-start.17 = (f32[2,72,256]{2,1,0:T(8,128)S(1)}, f32[2,72,256]{2,1,0:T(8,128)S(1)}, u32[]{:S(2)}, u32[]{:S(2)}) collective-permute-start(f32[2,72,256]{2,1,0:T(8,128)S(1)} %get-tuple-element.45), channel_id=1, source_target_pairs={{0,2},{1,3},{2,0},{3,1},{4,6},{5,7},{6,4},{7,5},{8,10},{9,11},{10,... | collective-permute-start | bytes 442376 | tf_op jit(solution)/shard_map/ppermute | solution.py:474
  61.6 1.5 %collective-permute-done.23.refs_2_ = f32[2,72,256]{2,1,0:T(8,128)S(1)} collective-permute-done((f32[2,72,256]{2,1,0:T(8,128)S(1)}, f32[2,72,256]{2,1,0:T(8,128)S(1)}, u32[]{:S(2)}, u32[]{:S(2)}) %collective-permute-start.23) | collective-permute-done | bytes 147488 | tf_op jit(solution)/shard_map/ppermute | solution.py:474
  63.1 2.3 %collective-permute-done.24.refs_3_ = f32[2,72,256]{2,1,0:T(8,128)S(1)} collective-permute-done((f32[2,72,256]{2,1,0:T(8,128)S(1)}, f32[2,72,256]{2,1,0:T(8,128)S(1)}, u32[]{:S(2)}, u32[]{:S(2)}) %collective-permute-start.24) | collective-permute-done | bytes 147488 | tf_op jit(solution)/shard_map/ppermute | solution.py:474
  66.6 2.7 %collective-permute-start.25 = (f32[2,72,256]{2,1,0:T(8,128)S(1)}, f32[2,72,256]{2,1,0:T(8,128)S(1)}, u32[]{:S(2)}, u32[]{:S(2)}) collective-permute-start(f32[2,72,256]{2,1,0:T(8,128)S(1)} %inverse_y_partial.1), channel_id=1, source_target_pairs={{0,16},{4,20},{8,24},{12,28},{16,0},{20,4},{24,8},{28,12},{1,17},{... | collective-permute-start | bytes 442376 | tf_op jit(solution)/shard_map/ppermute | solution.py:474
  69.4 2.3 %collective-permute-done.18.refs_3_ = f32[2,72,256]{2,1,0:T(8,128)S(1)} collective-permute-done((f32[2,72,256]{2,1,0:T(8,128)S(1)}, f32[2,72,256]{2,1,0:T(8,128)S(1)}, u32[]{:S(2)}, u32[]{:S(2)}) %collective-permute-start.18) | collective-permute-done | bytes 147488 | tf_op jit(solution)/shard_map/ppermute | solution.py:474
  71.7 5.5 %collective-permute-done.25.refs_4_ = f32[2,72,256]{2,1,0:T(8,128)S(1)} collective-permute-done((f32[2,72,256]{2,1,0:T(8,128)S(1)}, f32[2,72,256]{2,1,0:T(8,128)S(1)}, u32[]{:S(2)}, u32[]{:S(2)}) %collective-permute-start.25) | collective-permute-done | bytes 147488 | tf_op jit(solution)/shard_map/ppermute | solution.py:474
  77.2 2.0 %inverse_y_half.1 = (f32[64,256]{1,0:T(8,128)S(1)}, f32[64,256]{1,0:T(8,128)S(1)}, f32[2,64,256]{2,1,0:T(8,128)}, f32[2,64,256]{2,1,0:T(8,128)}) custom-call(s32[3]{0:T(128)S(1)} %pad_add_fusion.at_ref, f32[2,72,256]{2,1,0:T(8,128)S(1)} %get-tuple-element.43.refs_0_, f32[2,72,256]{2,1,0:T(8,128)S(1)} %collective-permute-done.16.refs_1_, ...), custom_call_target="tpu_custom_call" | custom-call | flops 226492416 | bytes 2179072 | tf_op jit(solution)/shard_map/inverse_y_half/pallas_call | solution.py:462
  79.1 3.3 %collective-permute-start.27 = (f32[64,256]{1,0:T(8,128)S(1)}, f32[64,256]{1,0:T(8,128)S(1)}, u32[]{:S(2)}, u32[]{:S(2)}) collective-permute-start(f32[64,256]{1,0:T(8,128)S(1)} %get-tuple-element.57), channel_id=1, source_target_pairs={{0,4},{4,8},{8,12},{12,16},{16,20},{20,24},{24,28},{1,5},{5,9},{9,... | collective-permute-start | bytes 196616 | tf_op jit(solution)/shard_map/ppermute | solution.py:255
  84.4 4.3 %collective-permute-done.26 = f32[64,256]{1,0:T(8,128)S(1)} collective-permute-done((f32[64,256]{1,0:T(8,128)S(1)}, f32[64,256]{1,0:T(8,128)S(1)}, u32[]{:S(2)}, u32[]{:S(2)}) %collective-permute-start.26) | collective-permute-done | bytes 65568 | tf_op jit(solution)/shard_map/ppermute | solution.py:256
  (70 shorter events, 27.1 us)
Async XLA Ops:
  0.6 10.6 %collective-permute-start.6 = (f32[2,64,256]{2,1,0:T(8,128)}, f32[2,64,256]{2,1,0:T(8,128)S(1)}, u32[]{:S(2)}, u32[]{:S(2)}) collective-permute-start(f32[2,64,256]{2,1,0:T(8,128)} %refs_0_.1), channel_id=1, source_target_pairs={{0,16},{4,20},{8,24},{12,28},{16,0},{20,4},{24,8},{28,12},{1,17},{... | collective-permute-start | bytes 393224 | tf_op jit(solution)/shard_map/ppermute | solution.py:474
  4.7 8.1 %collective-permute-start.1 = (f32[2,64,256]{2,1,0:T(8,128)}, f32[2,64,256]{2,1,0:T(8,128)S(1)}, u32[]{:S(2)}, u32[]{:S(2)}) collective-permute-start(f32[2,64,256]{2,1,0:T(8,128)} %refs_0_.1), channel_id=1, source_target_pairs={{0,2},{1,3},{2,0},{3,1},{4,6},{5,7},{6,4},{7,5},{8,10},{9,11},{10,... | collective-permute-start | bytes 393224 | tf_op jit(solution)/shard_map/ppermute | solution.py:474
  13.4 13.5 %collective-permute-start.7 = (f32[2,64,256]{2,1,0:T(8,128)S(1)}, f32[2,64,256]{2,1,0:T(8,128)S(1)}, u32[]{:S(2)}, u32[]{:S(2)}) collective-permute-start(f32[2,64,256]{2,1,0:T(8,128)S(1)} %collective-permute-done.6.refs_0_), channel_id=1, source_target_pairs={{0,1},{1,0},{2,3},{3,2},{4,5},{5,4},{6,7},{7,6},{8,9},{9,8},{10,11... | collective-permute-start | bytes 393224 | tf_op jit(solution)/shard_map/ppermute | solution.py:474
  16.2 10.7 %collective-permute-start.9 = (f32[2,64,256]{2,1,0:T(8,128)S(1)}, f32[2,64,256]{2,1,0:T(8,128)S(1)}, u32[]{:S(2)}, u32[]{:S(2)}) collective-permute-start(f32[2,64,256]{2,1,0:T(8,128)S(1)} %collective-permute-done.8.refs_2_), channel_id=1, source_target_pairs={{0,1},{1,0},{2,3},{3,2},{4,5},{5,4},{6,7},{7,6},{8,9},{9,8},{10,11... | collective-permute-start | bytes 393224 | tf_op jit(solution)/shard_map/ppermute | solution.py:474
  23.3 10.5 %collective-permute-start.3 = (f32[2,64,256]{2,1,0:T(8,128)S(1)}, f32[2,64,256]{2,1,0:T(8,128)S(1)}, u32[]{:S(2)}, u32[]{:S(2)}) collective-permute-start(f32[2,64,256]{2,1,0:T(8,128)S(1)} %get-tuple-element.32), channel_id=1, source_target_pairs={{0,4},{4,0},{8,12},{12,8},{16,20},{20,16},{24,28},{28,24},{1,5},{5... | collective-permute-start | bytes 393224 | tf_op jit(solution)/shard_map/ppermute | solution.py:474
  25.0 9.6 %collective-permute-start.4 = (f32[2,64,256]{2,1,0:T(8,128)S(1)}, f32[2,64,256]{2,1,0:T(8,128)S(1)}, u32[]{:S(2)}, u32[]{:S(2)}) collective-permute-start(f32[2,64,256]{2,1,0:T(8,128)S(1)} %get-tuple-element.33), channel_id=1, source_target_pairs={{0,8},{4,12},{8,0},{12,4},{16,24},{20,28},{24,16},{28,20},{1,9},{5... | collective-permute-start | bytes 393224 | tf_op jit(solution)/shard_map/ppermute | solution.py:474
  26.2 8.4 %collective-permute-start.5 = (f32[2,64,256]{2,1,0:T(8,128)S(1)}, f32[2,64,256]{2,1,0:T(8,128)S(1)}, u32[]{:S(2)}, u32[]{:S(2)}) collective-permute-start(f32[2,64,256]{2,1,0:T(8,128)S(1)} %get-tuple-element.34), channel_id=1, source_target_pairs={{0,12},{4,8},{8,4},{12,0},{16,28},{20,24},{24,20},{28,16},{1,13},{... | collective-permute-start | bytes 393224 | tf_op jit(solution)/shard_map/ppermute | solution.py:474
  32.6 6.2 %collective-permute-start.11 = (f32[2,64,256]{2,1,0:T(8,128)S(1)}, f32[2,64,256]{2,1,0:T(8,128)S(1)}, u32[]{:S(2)}, u32[]{:S(2)}) collective-permute-start(f32[2,64,256]{2,1,0:T(8,128)S(1)} %get-tuple-element.37), channel_id=1, source_target_pairs={{0,8},{4,12},{8,0},{12,4},{16,24},{20,28},{24,16},{28,20},{1,9},{5... | collective-permute-start | bytes 393224 | tf_op jit(solution)/shard_map/ppermute | solution.py:474
  33.9 6.4 %collective-permute-start.12 = (f32[2,64,256]{2,1,0:T(8,128)S(1)}, f32[2,64,256]{2,1,0:T(8,128)S(1)}, u32[]{:S(2)}, u32[]{:S(2)}) collective-permute-start(f32[2,64,256]{2,1,0:T(8,128)S(1)} %get-tuple-element.38), channel_id=1, source_target_pairs={{0,12},{4,8},{8,4},{12,0},{16,28},{20,24},{24,20},{28,16},{1,13},{... | collective-permute-start | bytes 393224 | tf_op jit(solution)/shard_map/ppermute | solution.py:474
  44.1 7.2 %collective-permute-start.19 = (f32[2,64,256]{2,1,0:T(8,128)S(1)}, f32[2,64,256]{2,1,0:T(8,128)S(1)}, u32[]{:S(2)}, u32[]{:S(2)}) collective-permute-start(f32[2,64,256]{2,1,0:T(8,128)S(1)} %get-tuple-element.48), channel_id=1, source_target_pairs={{0,4},{4,0},{8,12},{12,8},{16,20},{20,16},{24,28},{28,24},{1,5},{5... | collective-permute-start | bytes 393224 | tf_op jit(solution)/shard_map/ppermute | solution.py:474
  45.5 8.6 %collective-permute-start.20 = (f32[2,64,256]{2,1,0:T(8,128)S(1)}, f32[2,64,256]{2,1,0:T(8,128)S(1)}, u32[]{:S(2)}, u32[]{:S(2)}) collective-permute-start(f32[2,64,256]{2,1,0:T(8,128)S(1)} %get-tuple-element.49), channel_id=1, source_target_pairs={{0,8},{4,12},{8,0},{12,4},{16,24},{20,28},{24,16},{28,20},{1,9},{5... | collective-permute-start | bytes 393224 | tf_op jit(solution)/shard_map/ppermute | solution.py:474
  46.8 8.2 %collective-permute-start.21 = (f32[2,64,256]{2,1,0:T(8,128)S(1)}, f32[2,64,256]{2,1,0:T(8,128)S(1)}, u32[]{:S(2)}, u32[]{:S(2)}) collective-permute-start(f32[2,64,256]{2,1,0:T(8,128)S(1)} %get-tuple-element.50), channel_id=1, source_target_pairs={{0,12},{4,8},{8,4},{12,0},{16,28},{20,24},{24,20},{28,16},{1,13},{... | collective-permute-start | bytes 393224 | tf_op jit(solution)/shard_map/ppermute | solution.py:474
  47.6 10.3 %collective-permute-start.13 = (f32[2,64,256]{2,1,0:T(8,128)S(1)}, f32[2,64,256]{2,1,0:T(8,128)S(1)}, u32[]{:S(2)}, u32[]{:S(2)}) collective-permute-start(f32[2,64,256]{2,1,0:T(8,128)S(1)} %get-tuple-element.40), channel_id=1, source_target_pairs={{0,4},{4,0},{8,12},{12,8},{16,20},{20,16},{24,28},{28,24},{1,5},{5... | collective-permute-start | bytes 393224 | tf_op jit(solution)/shard_map/ppermute | solution.py:474
  49.0 9.2 %collective-permute-start.14 = (f32[2,64,256]{2,1,0:T(8,128)S(1)}, f32[2,64,256]{2,1,0:T(8,128)S(1)}, u32[]{:S(2)}, u32[]{:S(2)}) collective-permute-start(f32[2,64,256]{2,1,0:T(8,128)S(1)} %get-tuple-element.41), channel_id=1, source_target_pairs={{0,8},{4,12},{8,0},{12,4},{16,24},{20,28},{24,16},{28,20},{1,9},{5... | collective-permute-start | bytes 393224 | tf_op jit(solution)/shard_map/ppermute | solution.py:474
  51.3 6.9 %collective-permute-start.15 = (f32[2,64,256]{2,1,0:T(8,128)S(1)}, f32[2,64,256]{2,1,0:T(8,128)S(1)}, u32[]{:S(2)}, u32[]{:S(2)}) collective-permute-start(f32[2,64,256]{2,1,0:T(8,128)S(1)} %get-tuple-element.42), channel_id=1, source_target_pairs={{0,12},{4,8},{8,4},{12,0},{16,28},{20,24},{24,20},{28,16},{1,13},{... | collective-permute-start | bytes 393224 | tf_op jit(solution)/shard_map/ppermute | solution.py:474
  56.3 5.3 %collective-permute-start.22 = (f32[2,72,256]{2,1,0:T(8,128)S(1)}, f32[2,72,256]{2,1,0:T(8,128)S(1)}, u32[]{:S(2)}, u32[]{:S(2)}) collective-permute-start(f32[2,72,256]{2,1,0:T(8,128)S(1)} %get-tuple-element.52), channel_id=1, source_target_pairs={{0,1},{1,0},{2,3},{3,2},{4,5},{5,4},{6,7},{7,6},{8,9},{9,8},{10,11... | collective-permute-start | bytes 442376 | tf_op jit(solution)/shard_map/ppermute | solution.py:474
  56.4 6.7 %collective-permute-start.23 = (f32[2,72,256]{2,1,0:T(8,128)S(1)}, f32[2,72,256]{2,1,0:T(8,128)S(1)}, u32[]{:S(2)}, u32[]{:S(2)}) collective-permute-start(f32[2,72,256]{2,1,0:T(8,128)S(1)} %get-tuple-element.53), channel_id=1, source_target_pairs={{0,2},{1,3},{2,0},{3,1},{4,6},{5,7},{6,4},{7,5},{8,10},{9,11},{10,... | collective-permute-start | bytes 442376 | tf_op jit(solution)/shard_map/ppermute | solution.py:474
  58.0 7.4 %collective-permute-start.24 = (f32[2,72,256]{2,1,0:T(8,128)S(1)}, f32[2,72,256]{2,1,0:T(8,128)S(1)}, u32[]{:S(2)}, u32[]{:S(2)}) collective-permute-start(f32[2,72,256]{2,1,0:T(8,128)S(1)} %get-tuple-element.54), channel_id=1, source_target_pairs={{0,3},{1,2},{2,1},{3,0},{4,7},{5,6},{6,5},{7,4},{8,11},{9,10},{10,... | collective-permute-start | bytes 442376 | tf_op jit(solution)/shard_map/ppermute | solution.py:474
  59.6 9.6 %collective-permute-start.16 = (f32[2,72,256]{2,1,0:T(8,128)S(1)}, f32[2,72,256]{2,1,0:T(8,128)S(1)}, u32[]{:S(2)}, u32[]{:S(2)}) collective-permute-start(f32[2,72,256]{2,1,0:T(8,128)S(1)} %get-tuple-element.44), channel_id=1, source_target_pairs={{0,1},{1,0},{2,3},{3,2},{4,5},{5,4},{6,7},{7,6},{8,9},{9,8},{10,11... | collective-permute-start | bytes 442376 | tf_op jit(solution)/shard_map/ppermute | solution.py:474
  60.0 9.4 %collective-permute-start.17 = (f32[2,72,256]{2,1,0:T(8,128)S(1)}, f32[2,72,256]{2,1,0:T(8,128)S(1)}, u32[]{:S(2)}, u32[]{:S(2)}) collective-permute-start(f32[2,72,256]{2,1,0:T(8,128)S(1)} %get-tuple-element.45), channel_id=1, source_target_pairs={{0,2},{1,3},{2,0},{3,1},{4,6},{5,7},{6,4},{7,5},{8,10},{9,11},{10,... | collective-permute-start | bytes 442376 | tf_op jit(solution)/shard_map/ppermute | solution.py:474
  61.6 10.1 %collective-permute-start.18 = (f32[2,72,256]{2,1,0:T(8,128)S(1)}, f32[2,72,256]{2,1,0:T(8,128)S(1)}, u32[]{:S(2)}, u32[]{:S(2)}) collective-permute-start(f32[2,72,256]{2,1,0:T(8,128)S(1)} %get-tuple-element.46), channel_id=1, source_target_pairs={{0,3},{1,2},{2,1},{3,0},{4,7},{5,6},{6,5},{7,4},{8,11},{9,10},{10,... | collective-permute-start | bytes 442376 | tf_op jit(solution)/shard_map/ppermute | solution.py:474
  66.6 10.6 %collective-permute-start.25 = (f32[2,72,256]{2,1,0:T(8,128)S(1)}, f32[2,72,256]{2,1,0:T(8,128)S(1)}, u32[]{:S(2)}, u32[]{:S(2)}) collective-permute-start(f32[2,72,256]{2,1,0:T(8,128)S(1)} %inverse_y_partial.1), channel_id=1, source_target_pairs={{0,16},{4,20},{8,24},{12,28},{16,0},{20,4},{24,8},{28,12},{1,17},{... | collective-permute-start | bytes 442376 | tf_op jit(solution)/shard_map/ppermute | solution.py:474
  79.1 5.2 %collective-permute-start.27 = (f32[64,256]{1,0:T(8,128)S(1)}, f32[64,256]{1,0:T(8,128)S(1)}, u32[]{:S(2)}, u32[]{:S(2)}) collective-permute-start(f32[64,256]{1,0:T(8,128)S(1)} %get-tuple-element.57), channel_id=1, source_target_pairs={{0,4},{4,8},{8,12},{12,16},{16,20},{20,24},{24,28},{1,5},{5,9},{9,... | collective-permute-start | bytes 196616 | tf_op jit(solution)/shard_map/ppermute | solution.py:255
  82.5 6.2 %collective-permute-start.26 = (f32[64,256]{1,0:T(8,128)S(1)}, f32[64,256]{1,0:T(8,128)S(1)}, u32[]{:S(2)}, u32[]{:S(2)}) collective-permute-start(f32[64,256]{1,0:T(8,128)S(1)} %get-tuple-element.58), channel_id=1, source_target_pairs={{4,0},{8,4},{12,8},{16,12},{20,16},{24,20},{28,24},{5,1},{9,5},{13... | collective-permute-start | bytes 196616 | tf_op jit(solution)/shard_map/ppermute | solution.py:256
  (17 other events, 102.6 us)

commit v3 on v2

--- a/solution.py
+++ b/solution.py
@@ -56,17 +56,6 @@
 def inverse_table(space):
     angle = angles(space, 2 * space).T
     return halves(np.concatenate([np.cos(angle), np.sin(angle)], axis=1))
-
-
-def half_inverse_table(space, parts):
-    angle = angles(space, 2 * space).T
-    count = space // parts
-    rows = []
-    for start in range(0, space, count):
-        rows += [*range(start, start + count), max(start - 1, 0), min(start + count, space - 1)]
-        rows += [start] * 6
-    angle = angle[np.array(rows)].reshape(len(rows), 2, space).transpose(1, 0, 2)
-    return halves(np.concatenate([np.cos(angle), np.sin(angle)], axis=2))
 
 
 def times(value, turns, length):
@@ -131,15 +120,9 @@
     )(rows, *table_y, *table_x)
 
 
-def middle_kernel(f_ref, g_ref, h_ref, out_ref):
-    slabs = f_ref.shape[1]
-    depth = f_ref.shape[0] * slabs
+def through_z(field, green, image_green):
+    depth = len(field)
     length = 2 * depth
-    half = f_ref.shape[3] // 2
-    field = [
-        (f_ref[z // slabs, z % slabs, :, :half], f_ref[z // slabs, z % slabs, :, half:])
-        for z in range(depth)
-    ]
     even = fft(field, -1)
     odd = fft([times(v, -z, length) for z, v in enumerate(field)], -1)
     spec = [v for pair in zip(even, odd) for v in pair]
@@ -147,7 +130,7 @@
     for k in range(length):
         re, im = spec[k]
         mre, mim = times(spec[-k % length], -k * (depth - 1), length)
-        gre, gim, hre, him = g_ref[0, k], g_ref[1, k], h_ref[0, k], h_ref[1, k]
+        (gre, gim), (hre, him) = green(k), image_green(k)
         product.append(
             (
                 gre * re - gim * im + hre * mre - him * mim,
@@ -156,10 +139,18 @@
         )
     even = fft(product[0::2], 1)
     odd = fft(product[1::2], 1)
-    for z in range(depth):
-        re, im = add(even[z], times(odd[z], z, length))
-        out_ref[z // slabs, z % slabs, :, :half] = re
-        out_ref[z // slabs, z % slabs, :, half:] = im
+    return [add(even[z], times(odd[z], z, length)) for z in range(depth)]
+
+
+def middle_kernel(f_ref, g_ref, h_ref, out_ref):
+    slabs = f_ref.shape[1]
+    half = f_ref.shape[3] // 2
+    at = [(z // slabs, z % slabs) for z in range(f_ref.shape[0] * slabs)]
+    field = [(f_ref[a, b, :, :half], f_ref[a, b, :, half:]) for a, b in at]
+    both = lambda ref: lambda k: (ref[0, k], ref[1, k])
+    for (a, b), (re, im) in zip(at, through_z(field, both(g_ref), both(h_ref))):
+        out_ref[a, b, :, :half] = re
+        out_ref[a, b, :, half:] = im
 
 
 def middle(field, green, image_green):
@@ -272,15 +263,89 @@
     return jnp.stack([lax.axis_index("gx"), mine // half, mine % half]).astype(jnp.int32)
 
 
+def turn_table(space):
+    rows = np.concatenate([np.arange(0, 2 * space, 8), np.arange(8)])
+    angle = np.outer(rows, np.arange(space)) % (2 * space) * (math.pi / space)
+    return np.concatenate([np.cos(angle), np.sin(angle)], axis=1).astype(np.float32)
+
+
+def tables_kernel(space, parts, at_ref, turn_ref, density_ref, *outs):
+    outs[8][...] = density_ref[...]
+    me, side = at_ref[0], at_ref[1]
+    coarse = 2 * space // 8
+    cos, sin = turn_ref[coarse:, :space], turn_ref[coarse:, space:]
+    odd = lax.broadcasted_iota(jnp.int32, cos.shape, 0) % 2 == 1
+    sign = jnp.where(odd & (side == 1), -1.0, 1.0)
+    flip_cos, flip_sin = cos * sign, sin * sign
+
+    def turned_by(row, cos, sin):
+        c, s = turn_ref[pl.ds(row, 1), :space], turn_ref[pl.ds(row, 1), space:]
+        return c * cos - s * sin, c * sin + s * cos
+
+    def put(pair, at, lanes, values):
+        for ref, value in zip(pair, split(jnp.concatenate(values, axis=0))):
+            ref[at : at + 16, lanes] = value
+
+    every = slice(0, space)
+    first, second = slice(0, space), slice(space, 2 * space)
+    count = space // parts
+    freq = 2 * space // parts
+    for k in range(2):
+        base = (me ^ k) * (freq // 8)
+        pair = outs[2 * k : 2 * k + 2]
+        for row in range(0, freq, 16):
+            two = [turned_by(base + row // 8 + i, cos, sin) for i in range(2)]
+            put(pair, row, every, [v[0] for v in two])
+            put(pair, freq + row, every, [-v[1] for v in two])
+    pair = outs[4:6]
+    for row in range(0, space, 16):
+        two = [turned_by(side * (space // 8) + row // 8 + i, cos, sin) for i in range(2)]
+        put(pair, row, first, [v[0] for v in two])
+        put(pair, row, second, [-v[1] for v in two])
+    tiles = []
+    which = lax.broadcasted_iota(jnp.int32, cos.shape, 0)
+    for part in range(parts):
+        start = part * count
+        tiles += [turned_by(row // 8, flip_cos, flip_sin) for row in range(start, start + count, 8)]
+        edge = []
+        for row in (max(start - 1, 0), min(start + count, space - 1)):
+            fine = row % 8
+            edge.append(turned_by(row // 8, flip_cos[fine : fine + 1], flip_sin[fine : fine + 1]))
+        tiles.append(tuple(jnp.where(which == 0, edge[0][i], edge[1][i]) for i in range(2)))
+    for row in range(0, 8 * len(tiles), 16):
+        two = tiles[row // 8 : row // 8 + 2]
+        put(outs[6:8], row, first, [v[0] for v in two])
+        put(outs[6:], row, second, [v[1] for v in two])
+
+
+def tables(at, density, parts):
+    space = density.shape[2]
+    turn = turn_table(space)
+    high = lambda *shape: [jax.ShapeDtypeStruct(shape, jnp.bfloat16)] * 2
+    shapes = high(4 * space // parts, space) * 2 + high(space, 2 * space)
+    shapes += high(space + 8 * parts, 2 * space)
+    shapes += [jax.ShapeDtypeStruct(density.shape, density.dtype)]
+    out = pl.pallas_call(
+        functools.partial(tables_kernel, space, parts),
+        in_specs=[pl.BlockSpec(memory_space=SMEM)] + pieces_spec(2),
+        out_specs=pieces_spec(len(shapes)),
+        out_shape=shapes,
+        compiler_params=pltpu.CompilerParams(vmem_limit_bytes=LIMIT),
+        cost_estimate=cost(0, (turn, *shapes)),
+        name="tables",
+    )(at, turn, density)
+    return out[8], *[out[i : i + 2] for i in range(0, 8, 2)]
+
+
 def forward_half_kernel(at_ref, *refs):
     parts = lax.axis_size("gx")
     group = lax.axis_size("gz") // 2
-    me, side, member = at_ref[0], at_ref[1], at_ref[2]
+    me, member = at_ref[0], at_ref[2]
     rows, refs = refs[:parts], refs[parts:]
     yh_ref, yl_ref, th_ref, tl_ref, *refs = refs
     outs, (high_ref, low_ref, res_ref) = refs[:group], refs[group:]
-    table_y = (yh_ref[me], yl_ref[me])
-    table_x = (th_ref[side], tl_ref[side])
+    table_y = (yh_ref[...], yl_ref[...])
+    table_x = (th_ref[...], tl_ref[...])
     count = rows[0].shape[1]
     width = count * parts
     for z in range(rows[0].shape[0]):
@@ -309,7 +374,7 @@
 def forward_half(at, rows, table_y, table_x, group):
     slabs, count, height = rows[0].shape
     width = count * len(rows)
-    wide = table_y[0].shape[1]
+    wide = table_y[0].shape[0]
     kx = width // group
     shape = jax.ShapeDtypeStruct((slabs, kx, wide), jnp.float32)
     ins = (*rows, *table_y, *table_x)
@@ -334,30 +399,38 @@
     side, member = at_ref[1], at_ref[2]
     ins, (g_ref, h_ref), refs = refs[: 2 * group], refs[2 * group : 2 * group + 2], refs[2 * group + 2 :]
     outs, (in_ref, out_ref) = refs[: 2 * group], refs[2 * group :]
-    for k in range(2 * group):
-        slab = (side ^ (k // group)) * group + (member ^ (k % group))
-        in_ref[slab] = ins[k][...]
-    middle_kernel(in_ref, g_ref, h_ref, out_ref)
-    for k in range(2 * group):
-        slab = (side ^ (k // group)) * group + (member ^ (k % group))
-        outs[k][...] = out_ref[slab]
+    slabs, kx, wide = ins[0].shape
+    half = wide // 2
+    place = [(side ^ (k // group)) * group + (member ^ (k % group)) for k in range(2 * group)]
+    at = [(z // slabs, z % slabs) for z in range(2 * group * slabs)]
+
+    def tile(i, carry):
+        rows = pl.ds(pl.multiple_of(8 * i, 8), 8)
+        for k, slab in enumerate(place):
+            in_ref[slab] = ins[k][:, rows, :]
+        field = [(in_ref[a, b, :, :half], in_ref[a, b, :, half:]) for a, b in at]
+        both = lambda ref: lambda k: (ref[0, k, rows, :], ref[1, k, rows, :])
+        for (a, b), (re, im) in zip(at, through_z(field, both(g_ref), both(h_ref))):
+            out_ref[a, b, :, :half] = re
+            out_ref[a, b, :, half:] = im
+        for k, slab in enumerate(place):
+            outs[k][:, rows, :] = out_ref[slab]
+        return carry
+
+    lax.fori_loop(0, kx // 8, tile, 0)
 
 
 def middle_half(at, field, green, image_green):
     slabs, kx, wide = field[0].shape
-    tile = 8
-    spec = pl.BlockSpec((slabs, tile, wide), lambda i: (0, i, 0))
-    gspec = pl.BlockSpec((*green.shape[:2], tile, green.shape[3]), lambda i: (0, 0, i, 0))
     ins = (*field, green, image_green)
     shape = jax.ShapeDtypeStruct(field[0].shape, jnp.float32)
     return pl.pallas_call(
         middle_half_kernel,
-        grid=(kx // tile,),
-        in_specs=[pl.BlockSpec(memory_space=SMEM)] + [spec] * len(field) + [gspec, gspec],
-        out_specs=[spec] * len(field),
+        in_specs=[pl.BlockSpec(memory_space=SMEM)] + pieces_spec(len(ins)),
+        out_specs=pieces_spec(len(field)),
         out_shape=[shape] * len(field),
-        scratch_shapes=[VMEM((len(field), slabs, tile, wide), jnp.float32)] * 2,
-        cost_estimate=cost(30000 * kx * wide, (*ins, *[shape] * len(field))),
+        scratch_shapes=[VMEM((len(field), slabs, 8, wide), jnp.float32)] * 2,
+        cost_estimate=cost(0, (*ins, *[shape] * len(field))),
         compiler_params=pltpu.CompilerParams(vmem_limit_bytes=LIMIT),
         name="middle_half",
     )(at, *ins)
@@ -366,10 +439,10 @@
 def inverse_x_half_kernel(at_ref, *refs):
     parts = lax.axis_size("gx")
     group = lax.axis_size("gz") // 2
-    me, side, member = at_ref[0], at_ref[1], at_ref[2]
+    me, member = at_ref[0], at_ref[2]
     ins, (th_ref, tl_ref), refs = refs[:group], refs[group : group + 2], refs[group + 2 :]
-    outs, (high_ref, low_ref, res_ref) = refs[:parts], refs[parts:]
-    table = (th_ref[side], tl_ref[side])
+    outs, (high_ref, low_ref, res_ref) = refs[:2], refs[2:]
+    table = (th_ref[...], tl_ref[...])
     _, kx, wide = ins[0].shape
     wide //= 2
     for z in range(ins[0].shape[0]):
@@ -382,108 +455,130 @@
         res = product3(table, (high_ref[z], low_ref[z]), ((1,), (0,)))
         res_ref[z] = res.reshape(res_ref.shape[1:])
         for k in range(parts):
-            outs[k][z] = res_ref[z, me ^ k]
+            outs[k % 2][k // 2, z] = res_ref[z, me ^ k]
 
 
 def inverse_x_half(at, field, table, parts):
     slabs, kx, wide = field[0].shape
     width = len(field) * kx
     count = width // parts + 8
-    shape = jax.ShapeDtypeStruct((slabs, count, wide), jnp.float32)
+    shape = jax.ShapeDtypeStruct((parts // 2, slabs, count, wide), jnp.float32)
     ins = (*field, *table)
     return pl.pallas_call(
         inverse_x_half_kernel,
         in_specs=[pl.BlockSpec(memory_space=SMEM)] + pieces_spec(len(ins)),
-        out_specs=pieces_spec(parts),
-        out_shape=[shape] * parts,
+        out_specs=pieces_spec(2),
+        out_shape=[shape] * 2,
         scratch_shapes=[
             VMEM((slabs, 2 * width, wide), jnp.bfloat16),
             VMEM((slabs, 2 * width, wide), jnp.bfloat16),
             VMEM((slabs, parts, count, wide), jnp.float32),
         ],
-        cost_estimate=cost(12 * slabs * parts * count * width * wide, (*ins, *[shape] * parts)),
+        cost_estimate=cost(12 * slabs * parts * count * width * wide, (*ins, *[shape] * 2)),
         compiler_params=pltpu.CompilerParams(vmem_limit_bytes=LIMIT),
         name="inverse_x_half",
     )(at, *ins)
 
 
-def rows_of(ins, th_ref, tl_ref, me, z):
+def inverse_y_partial_kernel(keep_ref, near_ref, *refs):
+    outs = refs[4:]
     total = None
-    for k, ref in enumerate(ins):
-        term = product3(split(ref[z]), (th_ref[me ^ k], tl_ref[me ^ k]), ((1,), (0,)))
+    for k, ref in enumerate((keep_ref, near_ref)):
+        rows = ref[...].reshape(-1, ref.shape[3])
+        table = (refs[2 * k][...], refs[2 * k + 1][...])
+        term = product3(split(rows), table, ((1,), (0,)))
         total = term if total is None else total + term
-    return total
-
-
-def inverse_y_partial_kernel(at_ref, *refs):
-    parts = lax.axis_size("gx")
-    ins, (th_ref, tl_ref, out_ref) = refs[:parts], refs[parts:]
-    me = at_ref[0]
-    for z in range(out_ref.shape[0]):
-        out_ref[z] = rows_of(ins, th_ref, tl_ref, me, z)
-
-
-def inverse_y_partial(at, rows, table):
-    slabs, count, wide = rows[0].shape
-    shape = jax.ShapeDtypeStruct((slabs, count, table[0].shape[2]), jnp.float32)
-    ins = (*rows, *table)
+    total = total.reshape(len(outs), *outs[0].shape)
+    for k, ref in enumerate(outs):
+        ref[...] = total[k]
+
+
+def inverse_y_partial(keep, near, table):
+    chips, slabs, count, wide = keep.shape
+    shape = jax.ShapeDtypeStruct((slabs, count, table[0].shape[1]), jnp.float32)
+    ins = (keep, near, *table)
     return pl.pallas_call(
         inverse_y_partial_kernel,
-        in_specs=[pl.BlockSpec(memory_space=SMEM)] + pieces_spec(len(ins)),
-        out_specs=pl.BlockSpec(memory_space=VMEM),
-        out_shape=shape,
-        cost_estimate=cost(6 * slabs * count * wide * len(rows) * shape.shape[2], (*ins, shape)),
+        in_specs=pieces_spec(len(ins)),
+        out_specs=pieces_spec(chips),
+        out_shape=[shape] * chips,
+        cost_estimate=cost(12 * chips * slabs * count * wide * shape.shape[2], (*ins, *[shape] * chips)),
         compiler_params=pltpu.CompilerParams(vmem_limit_bytes=LIMIT),
         name="inverse_y_partial",
-    )(at, *ins)
-
-
-def inverse_y_half_kernel(scale, at_ref, *refs):
+    )(*ins)
+
+
+def combine_kernel(scale, at_ref, mine_ref, near_ref, other_ref, first_ref, second_ref, rows_ref):
+    odd = at_ref[2] % 2 == 1
+    count = first_ref.shape[0]
+    low = ((mine_ref[0] + near_ref[0]) + other_ref[0]) * scale
+    high = ((mine_ref[1] + near_ref[1]) + other_ref[1]) * scale
+    first_ref[...] = jnp.where(odd, low[:count], high[:count])
+    second_ref[...] = jnp.where(odd, high[:count], low[:count])
+    rows_ref[0] = low[count:]
+    rows_ref[1] = high[count:]
+
+
+def combine(at, mine, near, other, scale):
+    slabs, count, height = mine.shape
+    one = jax.ShapeDtypeStruct((count - 8, height), jnp.float32)
+    shapes = [one, one, jax.ShapeDtypeStruct((slabs, 8, height), jnp.float32)]
+    return pl.pallas_call(
+        functools.partial(combine_kernel, scale),
+        in_specs=[pl.BlockSpec(memory_space=SMEM)] + pieces_spec(3),
+        out_specs=pieces_spec(3),
+        out_shape=shapes,
+        compiler_params=pltpu.CompilerParams(vmem_limit_bytes=LIMIT),
+        cost_estimate=cost(0, (mine, near, other, *shapes)),
+        name="combine",
+    )(at, mine, near, other)
+
+
+def slopes_kernel(at_ref, first_ref, second_ref, rows_ref, gx_ref, gy_ref):
     parts = lax.axis_size("gx")
-    ins, (other_ref, th_ref, tl_ref, low_ref, high_ref, gx_ref, gy_ref) = refs[:parts], refs[parts:]
-    me = at_ref[0]
-    slabs = gx_ref.shape[0]
-    for z in range(slabs):
-        total = (rows_of(ins, th_ref, tl_ref, me, z) + other_ref[z]) * scale
-        main = differences(total, me, parts, gx_ref.at[z], gy_ref.at[z])
-        if z == 0:
-            low_ref[...] = main
-        if z == slabs - 1:
-            high_ref[...] = main
-
-
-def inverse_y_half(at, rows, other, table, scale):
-    slabs, count, wide = rows[0].shape
-    height = table[0].shape[2]
-    full = jax.ShapeDtypeStruct((slabs, count - 8, height), jnp.float32)
-    one = jax.ShapeDtypeStruct((count - 8, height), jnp.float32)
-    ins = (*rows, other, *table)
-    shapes = [one, one, full, full]
-    return pl.pallas_call(
-        functools.partial(inverse_y_half_kernel, scale),
-        in_specs=[pl.BlockSpec(memory_space=SMEM)] + pieces_spec(len(ins)),
-        out_specs=pieces_spec(4),
-        out_shape=shapes,
-        cost_estimate=cost(6 * slabs * count * wide * len(rows) * height, (*ins, *shapes)),
+    odd = at_ref[2] % 2 == 1
+    first, second = first_ref[...], second_ref[...]
+    for z, main in enumerate((jnp.where(odd, first, second), jnp.where(odd, second, first))):
+        total = jnp.concatenate([main, rows_ref[z]], axis=0)
+        differences(total, at_ref[0], parts, gx_ref.at[z], gy_ref.at[z])
+
+
+def slopes(at, first, second, rows):
+    shape = jax.ShapeDtypeStruct((2, *first.shape), jnp.float32)
+    return pl.pallas_call(
+        slopes_kernel,
+        in_specs=[pl.BlockSpec(memory_space=SMEM)] + pieces_spec(3),
+        out_specs=pieces_spec(2),
+        out_shape=[shape, shape],
         compiler_params=pltpu.CompilerParams(vmem_limit_bytes=LIMIT),
-        name="inverse_y_half",
-    )(at, *ins)
+        cost_estimate=cost(0, (first, second, rows, shape, shape)),
+        name="slopes",
+    )(at, first, second, rows)
+
+
+def slope_z_pairs(first, second):
+    size, mine = lax.axis_size("gz"), lax.axis_index("gz")
+    odd, start, end = mine % 2 == 1, mine == 0, mine == size - 1
+    near = swap(first, "gz", 1)
+    pairs = [(i, i + 1) for i in range(1, size - 1, 2)]
+    far = lax.ppermute(second, "gz", pairs + [(b, a) for a, b in pairs])
+    low, high = jnp.where(odd, first, second), jnp.where(odd, second, first)
+    below, above = jnp.where(odd, near, far), jnp.where(odd, far, near)
+    bottom = (high - jnp.where(start, low, below)) * jnp.where(start, 1.0, 0.5)
+    top = (jnp.where(end, high, above) - low) * jnp.where(end, 1.0, 0.5)
+    return jnp.stack([bottom, top])
 
 
 def swap(value, axis, mask):
     return lax.ppermute(value, axis, [(s, s ^ mask) for s in range(lax.axis_size(axis))])
 
 
-def gather_rows(own):
-    pieces = [own]
-    for k in range(1, lax.axis_size("gx")):
-        low = k & -k
-        pieces.append(swap(pieces[k - low], "gx", low))
-    return pieces
-
-
 def exchange(pieces, axis):
     return [pieces[0]] + [swap(p, axis, k) for k, p in enumerate(pieces) if k > 0]
+
+
+def after(value, *others):
+    return lax.optimization_barrier((value, others))[0]
 
 
 def halves_device(density, green, image_green):
@@ -491,31 +586,40 @@
     gz, gx = lax.axis_size("gz"), lax.axis_size("gx")
     group = gz // 2
     width = density.shape[1] * gx
-    column = column_table(height, gx)
-    ahead = [t.reshape(2, width, 2 * width) for t in forward_table(width)]
-    back = half_inverse_table(width, gx)
     at = place()
     other = swap(density, "gz", group)
-    field = []
-    for raw in (density, other):
-        pieces = forward_half(at, gather_rows(raw), column, ahead, group)
-        field += exchange(pieces, "gz")
+    raw = exchange([density] * gx, "gx")
+    local, near_y, far_y, ahead, back = tables(at, density, gx)
+    other = after(other, near_y)
+    low, high = swap(other, "gx", 1), swap(other, "gx", 2)
+    field = forward_half(at, [local, *raw[1:]], near_y, ahead, group)
+    raw = [other, low, high, swap(after(high, field), "gx", 1)]
+    field = exchange(field, "gz")
+    field += exchange(forward_half(at, raw, near_y, ahead, group), "gz")
     field = middle_half(at, field, green, image_green)
-    part = inverse_x_half(at, exchange(field[group:], "gz"), back, gx)
-    part = inverse_y_partial(at, exchange(part, "gx"), column)
+    own, far = field[:group], field[group:]
+    column = (*near_y, *far_y)
+    keep, give = inverse_x_half(at, exchange(far, "gz"), back, gx)
+    own = exchange(after(own, give), "gz")
+    part, give = inverse_y_partial(keep, swap(give, "gx", 1), column)
+    part = part + swap(give, "gx", 2)
+    own = after(own, part)
+    keep, give = inverse_x_half(at, own, back, gx)
+    keep = after(keep, part)
     part = swap(part, "gz", group)
-    rows = inverse_x_half(at, exchange(field[:group], "gz"), back, gx)
+    mine, give = inverse_y_partial(keep, swap(give, "gx", 1), column)
     scale = 1.0 / (8.0 * slabs * gz * width * height)
-    low, high, grad_x, grad_y = inverse_y_half(at, exchange(rows, "gx"), part, column, scale)
-    return grad_x, grad_y, slope_z(low, high)
+    first, second, rows = combine(at, mine, swap(give, "gx", 2), part, scale)
+    grad_z = slope_z_pairs(first, second)
+    return *slopes(at, first, second, rows), grad_z
 
 
 def per_device(density, green, image_green):
-    slabs, _, height = density.shape
-    if lax.axis_size("gz") <= 8 and slabs == 2:
+    slabs, count, height = density.shape
+    width = count * lax.axis_size("gx")
+    if lax.axis_size("gz") == 8 and lax.axis_size("gx") == 4 and slabs == 2 and width == height:
         return halves_device(density, green, image_green)
     gz, gx = lax.axis_size("gz"), lax.axis_size("gx")
-    width = density.shape[1] * gx
     depth = slabs * gz
     column = column_table(height, gx)
     me = lax.axis_index("gx")

time: 89.9 us -> 78.1 us (0.87)
  the two profiles are of different devices: /device:TPU:0 before, /device:TPU:8 now
where the time goes in v3:
time: 78.1 us; the launch traced here: 77.2 us
  waiting for transfers between devices  30.8 us (39%)
  starting transfers between devices  30.2 us (39%)
  Pallas kernels  12.9 us (17%)
  local copies, waits for them, and re-layouts  1.82 us (2%)
  other arithmetic  0.79 us (1%)
    ppermute x25, waiting for transfers between devices, swap(): lax.ppermute(value, axis, [(s, s ^ mask) for s in range(lax.axis_size(axi...  28.5 us
    ppermute x25, starting transfers between devices, swap(): lax.ppermute(value, axis, [(s, s ^ mask) for s in range(lax.axis_size(axi...  26.8 us
    pallas_call x2, Pallas kernels, forward_half(): pl.pallas_call(forward_half_kernel, in_specs=[pl.BlockSpec(memory_space=S...  3.98 us
    ppermute x1, starting transfers between devices, slope_z_pairs(): far = lax.ppermute(second, 'gz', pairs + [(b, a) for a, b in pairs])  3.37 us
    pallas_call x2, Pallas kernels, inverse_x_half(): pl.pallas_call(inverse_x_half_kernel, in_specs=[pl.BlockSpec(memory_space...  2.66 us
    pallas_call x1, Pallas kernels, middle_half(): pl.pallas_call(middle_half_kernel, in_specs=[pl.BlockSpec(memory_space=SM...  2.55 us
    ppermute x1, waiting for transfers between devices, slope_z_pairs(): far = lax.ppermute(second, 'gz', pairs + [(b, a) for a, b in pairs])  2.3 us
    unnamed x8, local copies, waits for them, and re-layouts  1.82 us
  transfers between devices with their start and end apart: 26, of which 17 were waited for; matrix products, arithmetic and copies ran while one was open for 0% of the time, Pallas kernels for 9%

profile of v3, /device:TPU:8, one launch (start us, length us, event | category | flops | bytes accessed | tf_op | source)
XLA Modules:
  0.0 77.2 jit_solution(10869818816035479073)
XLA Ops:
  0.6 2.7 %collective-permute-start.6 = (f32[2,64,256]{2,1,0:T(8,128)}, f32[2,64,256]{2,1,0:T(8,128)S(1)}, u32[]{:S(2)}, u32[]{:S(2)}) collective-permute-start(f32[2,64,256]{2,1,0:T(8,128)} %density_ref.1), channel_id=1, source_target_pairs={{0,16},{4,20},{8,24},{12,28},{16,0},{20,4},{24,8},{28,12},{1,17},{... | collective-permute-start | bytes 393224 | tf_op jit(solution)/shard_map/ppermute | solution.py:573
  11.8 2.0 %forward_half.2 = (f32[2,64,256]{2,1,0:T(8,128)S(1)}, f32[2,64,256]{2,1,0:T(8,128)S(1)}, f32[2,64,256]{2,1,0:T(8,128)S(1)}, f32[2,64,256]{2,1,0:T(8,128)S(1)}) custom-call(s32[3]{0:T(128)S(1)} %pad_add_fusion.at_ref, f32[2,64,256]{2,1,0:T(8,128)S(1)} %get-tuple-element.52.refs_0_, f32[2,64,256]{2,1,0:T(8,128)S(1)} %collective-permute-done.refs_1_, ...), custom_call_target="tpu_custom_call" | custom-call | flops 603979776 | bytes 1835008 | tf_op jit(solution)/shard_map/forward_half/pallas_call | solution.py:381
  15.0 1.5 %collective-permute-start.3 = (f32[2,64,256]{2,1,0:T(8,128)S(1)}, f32[2,64,256]{2,1,0:T(8,128)S(1)}, u32[]{:S(2)}, u32[]{:S(2)}) collective-permute-start(f32[2,64,256]{2,1,0:T(8,128)S(1)} %get-tuple-element.58), channel_id=1, source_target_pairs={{0,4},{4,0},{8,12},{12,8},{16,20},{20,16},{24,28},{28,24},{1,5},{5... | collective-permute-start | bytes 393224 | tf_op jit(solution)/shard_map/ppermute | solution.py:573
  17.0 1.5 %collective-permute-start.5 = (f32[2,64,256]{2,1,0:T(8,128)S(1)}, f32[2,64,256]{2,1,0:T(8,128)S(1)}, u32[]{:S(2)}, u32[]{:S(2)}) collective-permute-start(f32[2,64,256]{2,1,0:T(8,128)S(1)} %get-tuple-element.60), channel_id=1, source_target_pairs={{0,12},{4,8},{8,4},{12,0},{16,28},{20,24},{24,20},{28,16},{1,13},{... | collective-permute-start | bytes 393224 | tf_op jit(solution)/shard_map/ppermute | solution.py:573
  18.5 2.0 %forward_half.3 = (f32[2,64,256]{2,1,0:T(8,128)S(1)}, f32[2,64,256]{2,1,0:T(8,128)S(1)}, f32[2,64,256]{2,1,0:T(8,128)S(1)}, f32[2,64,256]{2,1,0:T(8,128)S(1)}) custom-call(s32[3]{0:T(128)S(1)} %pad_add_fusion.at_ref, f32[2,64,256]{2,1,0:T(8,128)S(1)} %collective-permute-done.6.refs_0_, f32[2,64,256]{2,1,0:T(8,128)S(1)} %collective-permute-done.7.refs_1_, ...), custom_call_target="tpu_custom_call" | custom-call | flops 603979776 | bytes 1835008 | tf_op jit(solution)/shard_map/forward_half/pallas_call | solution.py:381
  20.5 1.6 %collective-permute-start.10 = (f32[2,64,256]{2,1,0:T(8,128)S(1)}, f32[2,64,256]{2,1,0:T(8,128)S(1)}, u32[]{:S(2)}, u32[]{:S(2)}) collective-permute-start(f32[2,64,256]{2,1,0:T(8,128)S(1)} %get-tuple-element.64), channel_id=1, source_target_pairs={{0,4},{4,0},{8,12},{12,8},{16,20},{20,16},{24,28},{28,24},{1,5},{5... | collective-permute-start | bytes 393224 | tf_op jit(solution)/shard_map/ppermute | solution.py:573
  22.6 1.5 %collective-permute-start.12 = (f32[2,64,256]{2,1,0:T(8,128)S(1)}, f32[2,64,256]{2,1,0:T(8,128)S(1)}, u32[]{:S(2)}, u32[]{:S(2)}) collective-permute-start(f32[2,64,256]{2,1,0:T(8,128)S(1)} %get-tuple-element.66), channel_id=1, source_target_pairs={{0,12},{4,8},{8,4},{12,0},{16,28},{20,24},{24,20},{28,16},{1,13},{... | collective-permute-start | bytes 393224 | tf_op jit(solution)/shard_map/ppermute | solution.py:573
  24.1 1.5 %collective-permute-done.5.refs_3_ = f32[2,64,256]{2,1,0:T(8,128)S(1)} collective-permute-done((f32[2,64,256]{2,1,0:T(8,128)S(1)}, f32[2,64,256]{2,1,0:T(8,128)S(1)}, u32[]{:S(2)}, u32[]{:S(2)}) %collective-permute-start.5) | collective-permute-done | bytes 131104 | tf_op jit(solution)/shard_map/ppermute | solution.py:573
  25.6 2.8 %collective-permute-done.10.refs_5_ = f32[2,64,256]{2,1,0:T(8,128)S(1)} collective-permute-done((f32[2,64,256]{2,1,0:T(8,128)S(1)}, f32[2,64,256]{2,1,0:T(8,128)S(1)}, u32[]{:S(2)}, u32[]{:S(2)}) %collective-permute-start.10) | collective-permute-done | bytes 131104 | tf_op jit(solution)/shard_map/ppermute | solution.py:573
  28.5 2.0 %collective-permute-done.12.refs_7_ = f32[2,64,256]{2,1,0:T(8,128)S(1)} collective-permute-done((f32[2,64,256]{2,1,0:T(8,128)S(1)}, f32[2,64,256]{2,1,0:T(8,128)S(1)}, u32[]{:S(2)}, u32[]{:S(2)}) %collective-permute-start.12) | collective-permute-done | bytes 131104 | tf_op jit(solution)/shard_map/ppermute | solution.py:573
  30.6 2.6 %middle_half.1 = (f32[2,64,256]{2,1,0:T(8,128)S(1)}, f32[2,64,256]{2,1,0:T(8,128)S(1)}, f32[2,64,256]{2,1,0:T(8,128)S(1)}, f32[2,64,256]{2,1,0:T(8,128)S(1)}, f3...) custom-call(s32[3]{0:T(128)S(1)} %pad_add_fusion.at_ref, ...), custom_call_target="tpu_custom_call" | custom-call | bytes 6291456 | tf_op jit(solution)/shard_map/middle_half/pallas_call | solution.py:427
  33.1 1.6 %collective-permute-start.13 = (f32[2,64,256]{2,1,0:T(8,128)S(1)}, f32[2,64,256]{2,1,0:T(8,128)S(1)}, u32[]{:S(2)}, u32[]{:S(2)}) collective-permute-start(f32[2,64,256]{2,1,0:T(8,128)S(1)} %get-tuple-element.72), channel_id=1, source_target_pairs={{0,4},{4,0},{8,12},{12,8},{16,20},{20,16},{24,28},{28,24},{1,5},{5... | collective-permute-start | bytes 393224 | tf_op jit(solution)/shard_map/ppermute | solution.py:573
  36.7 2.4 %collective-permute-done.13.refs_1_ = f32[2,64,256]{2,1,0:T(8,128)S(1)} collective-permute-done((f32[2,64,256]{2,1,0:T(8,128)S(1)}, f32[2,64,256]{2,1,0:T(8,128)S(1)}, u32[]{:S(2)}, u32[]{:S(2)}) %collective-permute-start.13) | collective-permute-done | bytes 131104 | tf_op jit(solution)/shard_map/ppermute | solution.py:573
  39.0 1.6 %collective-permute-done.14.refs_2_ = f32[2,64,256]{2,1,0:T(8,128)S(1)} collective-permute-done((f32[2,64,256]{2,1,0:T(8,128)S(1)}, f32[2,64,256]{2,1,0:T(8,128)S(1)}, u32[]{:S(2)}, u32[]{:S(2)}) %collective-permute-start.14) | collective-permute-done | bytes 131104 | tf_op jit(solution)/shard_map/ppermute | solution.py:573
  43.4 1.6 %collective-permute-done.19.near_ref = f32[2,2,72,256]{3,2,1,0:T(8,128)S(1)} collective-permute-done((f32[2,2,72,256]{3,2,1,0:T(8,128)S(1)}, f32[2,2,72,256]{3,2,1,0:T(8,128)S(1)}, u32[]{:S(2)}, u32[]{:S(2)}) %collective-permute-start.19) | collective-permute-done | bytes 294944 | tf_op jit(solution)/shard_map/ppermute | solution.py:573
  45.4 1.6 %collective-permute-start.20 = (f32[2,72,256]{2,1,0:T(8,128)S(1)}, f32[2,72,256]{2,1,0:T(8,128)S(1)}, u32[]{:S(2)}, u32[]{:S(2)}) collective-permute-start(f32[2,72,256]{2,1,0:T(8,128)S(1)} %get-tuple-element.86), channel_id=1, source_target_pairs={{0,2},{1,3},{2,0},{3,1},{4,6},{5,7},{6,4},{7,5},{8,10},{9,11},{10,... | collective-permute-start | bytes 442376 | tf_op jit(solution)/shard_map/ppermute | solution.py:573
  46.9 1.5 %collective-permute-start.16 = (f32[2,64,256]{2,1,0:T(8,128)S(1)}, f32[2,64,256]{2,1,0:T(8,128)S(1)}, u32[]{:S(2)}, u32[]{:S(2)}) collective-permute-start(f32[2,64,256]{2,1,0:T(8,128)S(1)} %get-tuple-element.79), channel_id=1, source_target_pairs={{0,4},{4,0},{8,12},{12,8},{16,20},{20,16},{24,28},{28,24},{1,5},{5... | collective-permute-start | bytes 393224 | tf_op jit(solution)/shard_map/ppermute | solution.py:573
  48.9 1.5 %collective-permute-start.18 = (f32[2,64,256]{2,1,0:T(8,128)S(1)}, f32[2,64,256]{2,1,0:T(8,128)S(1)}, u32[]{:S(2)}, u32[]{:S(2)}) collective-permute-start(f32[2,64,256]{2,1,0:T(8,128)S(1)} %get-tuple-element.81), channel_id=1, source_target_pairs={{0,12},{4,8},{8,4},{12,0},{16,28},{20,24},{24,20},{28,16},{1,13},{... | collective-permute-start | bytes 393224 | tf_op jit(solution)/shard_map/ppermute | solution.py:573
  52.5 2.4 %collective-permute-done.17.refs_2_ = f32[2,64,256]{2,1,0:T(8,128)S(1)} collective-permute-done((f32[2,64,256]{2,1,0:T(8,128)S(1)}, f32[2,64,256]{2,1,0:T(8,128)S(1)}, u32[]{:S(2)}, u32[]{:S(2)}) %collective-permute-start.17) | collective-permute-done | bytes 131104 | tf_op jit(solution)/shard_map/ppermute | solution.py:573
  57.6 2.8 %collective-permute-start.23 = (f32[2,72,256]{2,1,0:T(8,128)S(1)}, f32[2,72,256]{2,1,0:T(8,128)S(1)}, u32[]{:S(2)}, u32[]{:S(2)}) collective-permute-start(f32[2,72,256]{2,1,0:T(8,128)S(1)} %add.12), channel_id=1, source_target_pairs={{0,16},{4,20},{8,24},{12,28},{16,0},{20,4},{24,8},{28,12},{1,17},{... | collective-permute-start | bytes 442376 | tf_op jit(solution)/shard_map/ppermute | solution.py:573
  61.4 5.9 %collective-permute-done.23.other_ref = f32[2,72,256]{2,1,0:T(8,128)S(1)} collective-permute-done((f32[2,72,256]{2,1,0:T(8,128)S(1)}, f32[2,72,256]{2,1,0:T(8,128)S(1)}, u32[]{:S(2)}, u32[]{:S(2)}) %collective-permute-start.23) | collective-permute-done | bytes 147488 | tf_op jit(solution)/shard_map/ppermute | solution.py:573
  67.9 1.6 %collective-permute-start.24 = (f32[64,256]{1,0:T(8,128)S(1)}, f32[64,256]{1,0:T(8,128)S(1)}, u32[]{:S(2)}, u32[]{:S(2)}) collective-permute-start(f32[64,256]{1,0:T(8,128)S(1)} %get-tuple-element.96.first_ref), channel_id=1, source_target_pairs={{0,4},{4,0},{8,12},{12,8},{16,20},{20,16},{24,28},{28,24},{1,5},{5... | collective-permute-start | bytes 196616 | tf_op jit(solution)/shard_map/ppermute | solution.py:573
  69.5 3.4 %collective-permute-start.25 = (f32[64,256]{1,0:T(8,128)S(1)}, f32[64,256]{1,0:T(8,128)S(1)}, u32[]{:S(2)}, u32[]{:S(2)}) collective-permute-start(f32[64,256]{1,0:T(8,128)S(1)} %get-tuple-element.97.second_ref), channel_id=1, source_target_pairs={{4,8},{12,16},{20,24},{8,4},{16,12},{24,20},{5,9},{13,17},{21,25},... | collective-permute-start | bytes 196616 | tf_op jit(solution)/shard_map/ppermute | solution.py:564
  74.2 2.3 %collective-permute-done.25 = f32[64,256]{1,0:T(8,128)S(1)} collective-permute-done((f32[64,256]{1,0:T(8,128)S(1)}, f32[64,256]{1,0:T(8,128)S(1)}, u32[]{:S(2)}, u32[]{:S(2)}) %collective-permute-start.25) | collective-permute-done | bytes 65568 | tf_op jit(solution)/shard_map/ppermute | solution.py:564
  (50 shorter events, 24.6 us)
Async XLA Ops:
  0.6 8.4 %collective-permute-start.6 = (f32[2,64,256]{2,1,0:T(8,128)}, f32[2,64,256]{2,1,0:T(8,128)S(1)}, u32[]{:S(2)}, u32[]{:S(2)}) collective-permute-start(f32[2,64,256]{2,1,0:T(8,128)} %density_ref.1), channel_id=1, source_target_pairs={{0,16},{4,20},{8,24},{12,28},{16,0},{20,4},{24,8},{28,12},{1,17},{... | collective-permute-start | bytes 393224 | tf_op jit(solution)/shard_map/ppermute | solution.py:573
  3.3 7.3 %collective-permute-start = (f32[2,64,256]{2,1,0:T(8,128)}, f32[2,64,256]{2,1,0:T(8,128)S(1)}, u32[]{:S(2)}, u32[]{:S(2)}) collective-permute-start(f32[2,64,256]{2,1,0:T(8,128)} %density_ref.1), channel_id=1, source_target_pairs={{0,1},{1,0},{2,3},{3,2},{4,5},{5,4},{6,7},{7,6},{8,9},{9,8},{10,11... | collective-permute-start | bytes 393224 | tf_op jit(solution)/shard_map/ppermute | solution.py:573
  3.3 7.3 %collective-permute-start.1 = (f32[2,64,256]{2,1,0:T(8,128)}, f32[2,64,256]{2,1,0:T(8,128)S(1)}, u32[]{:S(2)}, u32[]{:S(2)}) collective-permute-start(f32[2,64,256]{2,1,0:T(8,128)} %density_ref.1), channel_id=1, source_target_pairs={{0,2},{1,3},{2,0},{3,1},{4,6},{5,7},{6,4},{7,5},{8,10},{9,11},{10,... | collective-permute-start | bytes 393224 | tf_op jit(solution)/shard_map/ppermute | solution.py:573
  4.8 7.0 %collective-permute-start.2 = (f32[2,64,256]{2,1,0:T(8,128)}, f32[2,64,256]{2,1,0:T(8,128)S(1)}, u32[]{:S(2)}, u32[]{:S(2)}) collective-permute-start(f32[2,64,256]{2,1,0:T(8,128)} %density_ref.1), channel_id=1, source_target_pairs={{0,3},{1,2},{2,1},{3,0},{4,7},{5,6},{6,5},{7,4},{8,11},{9,10},{10,... | collective-permute-start | bytes 393224 | tf_op jit(solution)/shard_map/ppermute | solution.py:573
  9.1 6.0 %collective-permute-start.8 = (f32[2,64,256]{2,1,0:T(8,128)S(1)}, f32[2,64,256]{2,1,0:T(8,128)S(1)}, u32[]{:S(2)}, u32[]{:S(2)}) collective-permute-start(f32[2,64,256]{2,1,0:T(8,128)S(1)} %collective-permute-done.6.refs_0_), channel_id=1, source_target_pairs={{0,2},{1,3},{2,0},{3,1},{4,6},{5,7},{6,4},{7,5},{8,10},{9,11},{10,... | collective-permute-start | bytes 393224 | tf_op jit(solution)/shard_map/ppermute | solution.py:573
  10.5 8.0 %collective-permute-start.7 = (f32[2,64,256]{2,1,0:T(8,128)S(1)}, f32[2,64,256]{2,1,0:T(8,128)S(1)}, u32[]{:S(2)}, u32[]{:S(2)}) collective-permute-start(f32[2,64,256]{2,1,0:T(8,128)S(1)} %collective-permute-done.6.refs_0_), channel_id=1, source_target_pairs={{0,1},{1,0},{2,3},{3,2},{4,5},{5,4},{6,7},{7,6},{8,9},{9,8},{10,11... | collective-permute-start | bytes 393224 | tf_op jit(solution)/shard_map/ppermute | solution.py:573
  15.0 3.5 %collective-permute-start.9 = (f32[2,64,256]{2,1,0:T(8,128)S(1)}, f32[2,64,256]{2,1,0:T(8,128)S(1)}, u32[]{:S(2)}, u32[]{:S(2)}) collective-permute-start(f32[2,64,256]{2,1,0:T(8,128)S(1)} %collective-permute-done.8.refs_2_), channel_id=1, source_target_pairs={{0,1},{1,0},{2,3},{3,2},{4,5},{5,4},{6,7},{7,6},{8,9},{9,8},{10,11... | collective-permute-start | bytes 393224 | tf_op jit(solution)/shard_map/ppermute | solution.py:573
  15.0 7.5 %collective-permute-start.3 = (f32[2,64,256]{2,1,0:T(8,128)S(1)}, f32[2,64,256]{2,1,0:T(8,128)S(1)}, u32[]{:S(2)}, u32[]{:S(2)}) collective-permute-start(f32[2,64,256]{2,1,0:T(8,128)S(1)} %get-tuple-element.58), channel_id=1, source_target_pairs={{0,4},{4,0},{8,12},{12,8},{16,20},{20,16},{24,28},{28,24},{1,5},{5... | collective-permute-start | bytes 393224 | tf_op jit(solution)/shard_map/ppermute | solution.py:573
  16.5 7.5 %collective-permute-start.4 = (f32[2,64,256]{2,1,0:T(8,128)S(1)}, f32[2,64,256]{2,1,0:T(8,128)S(1)}, u32[]{:S(2)}, u32[]{:S(2)}) collective-permute-start(f32[2,64,256]{2,1,0:T(8,128)S(1)} %get-tuple-element.59), channel_id=1, source_target_pairs={{0,8},{4,12},{8,0},{12,4},{16,24},{20,28},{24,16},{28,20},{1,9},{5... | collective-permute-start | bytes 393224 | tf_op jit(solution)/shard_map/ppermute | solution.py:573
  17.0 8.6 %collective-permute-start.5 = (f32[2,64,256]{2,1,0:T(8,128)S(1)}, f32[2,64,256]{2,1,0:T(8,128)S(1)}, u32[]{:S(2)}, u32[]{:S(2)}) collective-permute-start(f32[2,64,256]{2,1,0:T(8,128)S(1)} %get-tuple-element.60), channel_id=1, source_target_pairs={{0,12},{4,8},{8,4},{12,0},{16,28},{20,24},{24,20},{28,16},{1,13},{... | collective-permute-start | bytes 393224 | tf_op jit(solution)/shard_map/ppermute | solution.py:573
  20.5 7.9 %collective-permute-start.10 = (f32[2,64,256]{2,1,0:T(8,128)S(1)}, f32[2,64,256]{2,1,0:T(8,128)S(1)}, u32[]{:S(2)}, u32[]{:S(2)}) collective-permute-start(f32[2,64,256]{2,1,0:T(8,128)S(1)} %get-tuple-element.64), channel_id=1, source_target_pairs={{0,4},{4,0},{8,12},{12,8},{16,20},{20,16},{24,28},{28,24},{1,5},{5... | collective-permute-start | bytes 393224 | tf_op jit(solution)/shard_map/ppermute | solution.py:573
  22.1 6.4 %collective-permute-start.11 = (f32[2,64,256]{2,1,0:T(8,128)S(1)}, f32[2,64,256]{2,1,0:T(8,128)S(1)}, u32[]{:S(2)}, u32[]{:S(2)}) collective-permute-start(f32[2,64,256]{2,1,0:T(8,128)S(1)} %get-tuple-element.65), channel_id=1, source_target_pairs={{0,8},{4,12},{8,0},{12,4},{16,24},{20,28},{24,16},{28,20},{1,9},{5... | collective-permute-start | bytes 393224 | tf_op jit(solution)/shard_map/ppermute | solution.py:573
  22.6 8.0 %collective-permute-start.12 = (f32[2,64,256]{2,1,0:T(8,128)S(1)}, f32[2,64,256]{2,1,0:T(8,128)S(1)}, u32[]{:S(2)}, u32[]{:S(2)}) collective-permute-start(f32[2,64,256]{2,1,0:T(8,128)S(1)} %get-tuple-element.66), channel_id=1, source_target_pairs={{0,12},{4,8},{8,4},{12,0},{16,28},{20,24},{24,20},{28,16},{1,13},{... | collective-permute-start | bytes 393224 | tf_op jit(solution)/shard_map/ppermute | solution.py:573
  33.1 5.9 %collective-permute-start.13 = (f32[2,64,256]{2,1,0:T(8,128)S(1)}, f32[2,64,256]{2,1,0:T(8,128)S(1)}, u32[]{:S(2)}, u32[]{:S(2)}) collective-permute-start(f32[2,64,256]{2,1,0:T(8,128)S(1)} %get-tuple-element.72), channel_id=1, source_target_pairs={{0,4},{4,0},{8,12},{12,8},{16,20},{20,16},{24,28},{28,24},{1,5},{5... | collective-permute-start | bytes 393224 | tf_op jit(solution)/shard_map/ppermute | solution.py:573
  34.7 5.9 %collective-permute-start.14 = (f32[2,64,256]{2,1,0:T(8,128)S(1)}, f32[2,64,256]{2,1,0:T(8,128)S(1)}, u32[]{:S(2)}, u32[]{:S(2)}) collective-permute-start(f32[2,64,256]{2,1,0:T(8,128)S(1)} %get-tuple-element.73), channel_id=1, source_target_pairs={{0,8},{4,12},{8,0},{12,4},{16,24},{20,28},{24,16},{28,20},{1,9},{5... | collective-permute-start | bytes 393224 | tf_op jit(solution)/shard_map/ppermute | solution.py:573
  35.1 6.8 %collective-permute-start.15 = (f32[2,64,256]{2,1,0:T(8,128)S(1)}, f32[2,64,256]{2,1,0:T(8,128)S(1)}, u32[]{:S(2)}, u32[]{:S(2)}) collective-permute-start(f32[2,64,256]{2,1,0:T(8,128)S(1)} %get-tuple-element.74), channel_id=1, source_target_pairs={{0,12},{4,8},{8,4},{12,0},{16,28},{20,24},{24,20},{28,16},{1,13},{... | collective-permute-start | bytes 393224 | tf_op jit(solution)/shard_map/ppermute | solution.py:573
  45.4 6.0 %collective-permute-start.20 = (f32[2,72,256]{2,1,0:T(8,128)S(1)}, f32[2,72,256]{2,1,0:T(8,128)S(1)}, u32[]{:S(2)}, u32[]{:S(2)}) collective-permute-start(f32[2,72,256]{2,1,0:T(8,128)S(1)} %get-tuple-element.86), channel_id=1, source_target_pairs={{0,2},{1,3},{2,0},{3,1},{4,6},{5,7},{6,4},{7,5},{8,10},{9,11},{10,... | collective-permute-start | bytes 442376 | tf_op jit(solution)/shard_map/ppermute | solution.py:573
  46.9 5.5 %collective-permute-start.16 = (f32[2,64,256]{2,1,0:T(8,128)S(1)}, f32[2,64,256]{2,1,0:T(8,128)S(1)}, u32[]{:S(2)}, u32[]{:S(2)}) collective-permute-start(f32[2,64,256]{2,1,0:T(8,128)S(1)} %get-tuple-element.79), channel_id=1, source_target_pairs={{0,4},{4,0},{8,12},{12,8},{16,20},{20,16},{24,28},{28,24},{1,5},{5... | collective-permute-start | bytes 393224 | tf_op jit(solution)/shard_map/ppermute | solution.py:573
  48.5 6.4 %collective-permute-start.17 = (f32[2,64,256]{2,1,0:T(8,128)S(1)}, f32[2,64,256]{2,1,0:T(8,128)S(1)}, u32[]{:S(2)}, u32[]{:S(2)}) collective-permute-start(f32[2,64,256]{2,1,0:T(8,128)S(1)} %get-tuple-element.80), channel_id=1, source_target_pairs={{0,8},{4,12},{8,0},{12,4},{16,24},{20,28},{24,16},{28,20},{1,9},{5... | collective-permute-start | bytes 393224 | tf_op jit(solution)/shard_map/ppermute | solution.py:573
  48.9 7.3 %collective-permute-start.18 = (f32[2,64,256]{2,1,0:T(8,128)S(1)}, f32[2,64,256]{2,1,0:T(8,128)S(1)}, u32[]{:S(2)}, u32[]{:S(2)}) collective-permute-start(f32[2,64,256]{2,1,0:T(8,128)S(1)} %get-tuple-element.81), channel_id=1, source_target_pairs={{0,12},{4,8},{8,4},{12,0},{16,28},{20,24},{24,20},{28,16},{1,13},{... | collective-permute-start | bytes 393224 | tf_op jit(solution)/shard_map/ppermute | solution.py:573
  57.6 9.7 %collective-permute-start.23 = (f32[2,72,256]{2,1,0:T(8,128)S(1)}, f32[2,72,256]{2,1,0:T(8,128)S(1)}, u32[]{:S(2)}, u32[]{:S(2)}) collective-permute-start(f32[2,72,256]{2,1,0:T(8,128)S(1)} %add.12), channel_id=1, source_target_pairs={{0,16},{4,20},{8,24},{12,28},{16,0},{20,4},{24,8},{28,12},{1,17},{... | collective-permute-start | bytes 442376 | tf_op jit(solution)/shard_map/ppermute | solution.py:573
  60.8 6.5 %collective-permute-start.22 = (f32[2,72,256]{2,1,0:T(8,128)S(1)}, f32[2,72,256]{2,1,0:T(8,128)S(1)}, u32[]{:S(2)}, u32[]{:S(2)}) collective-permute-start(f32[2,72,256]{2,1,0:T(8,128)S(1)} %get-tuple-element.95), channel_id=1, source_target_pairs={{0,2},{1,3},{2,0},{3,1},{4,6},{5,7},{6,4},{7,5},{8,10},{9,11},{10,... | collective-permute-start | bytes 442376 | tf_op jit(solution)/shard_map/ppermute | solution.py:573
  67.9 6.3 %collective-permute-start.24 = (f32[64,256]{1,0:T(8,128)S(1)}, f32[64,256]{1,0:T(8,128)S(1)}, u32[]{:S(2)}, u32[]{:S(2)}) collective-permute-start(f32[64,256]{1,0:T(8,128)S(1)} %get-tuple-element.96.first_ref), channel_id=1, source_target_pairs={{0,4},{4,0},{8,12},{12,8},{16,20},{20,16},{24,28},{28,24},{1,5},{5... | collective-permute-start | bytes 196616 | tf_op jit(solution)/shard_map/ppermute | solution.py:573
  69.5 7.0 %collective-permute-start.25 = (f32[64,256]{1,0:T(8,128)S(1)}, f32[64,256]{1,0:T(8,128)S(1)}, u32[]{:S(2)}, u32[]{:S(2)}) collective-permute-start(f32[64,256]{1,0:T(8,128)S(1)} %get-tuple-element.97.second_ref), channel_id=1, source_target_pairs={{4,8},{12,16},{20,24},{8,4},{16,12},{24,20},{5,9},{13,17},{21,25},... | collective-permute-start | bytes 196616 | tf_op jit(solution)/shard_map/ppermute | solution.py:564
  (6 other events, 43.8 us)

commit v4 on v3

--- a/solution.py
+++ b/solution.py
@@ -441,7 +441,7 @@
     group = lax.axis_size("gz") // 2
     me, member = at_ref[0], at_ref[2]
     ins, (th_ref, tl_ref), refs = refs[:group], refs[group : group + 2], refs[group + 2 :]
-    outs, (high_ref, low_ref, res_ref) = refs[:2], refs[2:]
+    outs, (high_ref, low_ref, res_ref) = refs[:parts], refs[parts:]
     table = (th_ref[...], tl_ref[...])
     _, kx, wide = ins[0].shape
     wide //= 2
@@ -455,83 +455,68 @@
         res = product3(table, (high_ref[z], low_ref[z]), ((1,), (0,)))
         res_ref[z] = res.reshape(res_ref.shape[1:])
         for k in range(parts):
-            outs[k % 2][k // 2, z] = res_ref[z, me ^ k]
+            outs[k][z] = res_ref[z, me ^ k]
 
 
 def inverse_x_half(at, field, table, parts):
     slabs, kx, wide = field[0].shape
     width = len(field) * kx
     count = width // parts + 8
-    shape = jax.ShapeDtypeStruct((parts // 2, slabs, count, wide), jnp.float32)
+    shape = jax.ShapeDtypeStruct((slabs, count, wide), jnp.float32)
     ins = (*field, *table)
     return pl.pallas_call(
         inverse_x_half_kernel,
         in_specs=[pl.BlockSpec(memory_space=SMEM)] + pieces_spec(len(ins)),
-        out_specs=pieces_spec(2),
-        out_shape=[shape] * 2,
+        out_specs=pieces_spec(parts),
+        out_shape=[shape] * parts,
         scratch_shapes=[
             VMEM((slabs, 2 * width, wide), jnp.bfloat16),
             VMEM((slabs, 2 * width, wide), jnp.bfloat16),
             VMEM((slabs, parts, count, wide), jnp.float32),
         ],
-        cost_estimate=cost(12 * slabs * parts * count * width * wide, (*ins, *[shape] * 2)),
+        cost_estimate=cost(12 * slabs * parts * count * width * wide, (*ins, *[shape] * parts)),
         compiler_params=pltpu.CompilerParams(vmem_limit_bytes=LIMIT),
         name="inverse_x_half",
     )(at, *ins)
 
 
-def inverse_y_partial_kernel(keep_ref, near_ref, *refs):
-    outs = refs[4:]
+def inverse_y_partial_kernel(chips, *refs):
+    slabs, count, wide = refs[0].shape
     total = None
-    for k, ref in enumerate((keep_ref, near_ref)):
-        rows = ref[...].reshape(-1, ref.shape[3])
-        table = (refs[2 * k][...], refs[2 * k + 1][...])
+    outs, refs = refs[-chips:], refs[:-chips]
+    for k, ins in enumerate((refs[:chips], refs[chips:-4])):
+        rows = jnp.concatenate([r[...].reshape(-1, wide) for r in ins], axis=0)
+        table = [r[...] for r in refs[len(refs) - 4 :][2 * k : 2 * k + 2]]
         term = product3(split(rows), table, ((1,), (0,)))
         total = term if total is None else total + term
-    total = total.reshape(len(outs), *outs[0].shape)
+    total = total.reshape(chips, slabs, count, -1)
     for k, ref in enumerate(outs):
         ref[...] = total[k]
 
 
 def inverse_y_partial(keep, near, table):
-    chips, slabs, count, wide = keep.shape
+    slabs, count, wide = keep[0].shape
     shape = jax.ShapeDtypeStruct((slabs, count, table[0].shape[1]), jnp.float32)
-    ins = (keep, near, *table)
-    return pl.pallas_call(
-        inverse_y_partial_kernel,
+    ins = (*keep, *near, *table)
+    return pl.pallas_call(
+        functools.partial(inverse_y_partial_kernel, len(keep)),
         in_specs=pieces_spec(len(ins)),
-        out_specs=pieces_spec(chips),
-        out_shape=[shape] * chips,
-        cost_estimate=cost(12 * chips * slabs * count * wide * shape.shape[2], (*ins, *[shape] * chips)),
+        out_specs=pieces_spec(len(keep)),
+        out_shape=[shape] * len(keep),
+        cost_estimate=cost(12 * len(keep) * slabs * count * wide * shape.shape[2], (*ins, shape)),
         compiler_params=pltpu.CompilerParams(vmem_limit_bytes=LIMIT),
         name="inverse_y_partial",
     )(*ins)
 
 
-def combine_kernel(scale, at_ref, mine_ref, near_ref, other_ref, first_ref, second_ref, rows_ref):
-    odd = at_ref[2] % 2 == 1
-    count = first_ref.shape[0]
-    low = ((mine_ref[0] + near_ref[0]) + other_ref[0]) * scale
-    high = ((mine_ref[1] + near_ref[1]) + other_ref[1]) * scale
-    first_ref[...] = jnp.where(odd, low[:count], high[:count])
-    second_ref[...] = jnp.where(odd, high[:count], low[:count])
-    rows_ref[0] = low[count:]
-    rows_ref[1] = high[count:]
-
-
-def combine(at, mine, near, other, scale):
-    slabs, count, height = mine.shape
-    one = jax.ShapeDtypeStruct((count - 8, height), jnp.float32)
-    shapes = [one, one, jax.ShapeDtypeStruct((slabs, 8, height), jnp.float32)]
-    return pl.pallas_call(
-        functools.partial(combine_kernel, scale),
-        in_specs=[pl.BlockSpec(memory_space=SMEM)] + pieces_spec(3),
-        out_specs=pieces_spec(3),
-        out_shape=shapes,
-        compiler_params=pltpu.CompilerParams(vmem_limit_bytes=LIMIT),
-        cost_estimate=cost(0, (mine, near, other, *shapes)),
-        name="combine",
-    )(at, mine, near, other)
+def combine(mine, near, scale):
+    total = (mine + near) * scale
+    count = total.shape[1] - 8
+    low, high = total[0], total[1]
+    odd = lax.axis_index("gz") % 2 == 1
+    first = jnp.where(odd, low[:count], high[:count])
+    second = jnp.where(odd, high[:count], low[:count])
+    return first, second, total[:, count:]
 
 
 def slopes_kernel(at_ref, first_ref, second_ref, rows_ref, gx_ref, gy_ref):
@@ -579,6 +564,14 @@
 
 def after(value, *others):
     return lax.optimization_barrier((value, others))[0]
+
+
+def sums_y(rows, column, cut):
+    near = rows[1::2]
+    if cut:
+        near = [r[z] for r in near for z in range(r.shape[0])]
+    near = [swap(r, "gx", 1) for r in near]
+    return inverse_y_partial(rows[0::2], near, column)
 
 
 def halves_device(density, green, image_green):
@@ -599,17 +592,14 @@
     field = middle_half(at, field, green, image_green)
     own, far = field[:group], field[group:]
     column = (*near_y, *far_y)
-    keep, give = inverse_x_half(at, exchange(far, "gz"), back, gx)
-    own = exchange(after(own, give), "gz")
-    part, give = inverse_y_partial(keep, swap(give, "gx", 1), column)
+    far, own = exchange(far, "gz"), exchange(own, "gz")
+    part, give = sums_y(inverse_x_half(at, far, back, gx), column, True)
     part = part + swap(give, "gx", 2)
-    own = after(own, part)
-    keep, give = inverse_x_half(at, own, back, gx)
-    keep = after(keep, part)
-    part = swap(part, "gz", group)
-    mine, give = inverse_y_partial(keep, swap(give, "gx", 1), column)
+    rows = inverse_x_half(at, own, back, gx)
+    mine, give = sums_y((after(rows[0], part), *rows[1:]), column, False)
+    mine = after(mine + swap(part, "gz", group))
     scale = 1.0 / (8.0 * slabs * gz * width * height)
-    first, second, rows = combine(at, mine, swap(give, "gx", 2), part, scale)
+    first, second, rows = combine(mine, swap(give, "gx", 2), scale)
     grad_z = slope_z_pairs(first, second)
     return *slopes(at, first, second, rows), grad_z
 

time: 78.1 us -> 73.6 us (0.942)
  waiting for transfers between devices: 30.8 us -> 24.7 us
  starting transfers between devices: 30.2 us -> 32.1 us
    ppermute x25 -> x29, waiting for transfers between devices: 28.5 us -> 22 us  [swap(): lax.ppermute(value, axis, [(s, s ^ mask) for s in range(lax.axis_size(axi...]
    ppermute x25 -> x29, starting transfers between devices: 26.8 us -> 29.2 us  [swap(): lax.ppermute(value, axis, [(s, s ^ mask) for s in range(lax.axis_size(axi...]
  transfers between devices with their start and end apart: 26 -> 30, of which waited for: 17 -> 17; matrix products, arithmetic and copies ran while one was open for 0% -> 0% of each run, Pallas kernels for 9% -> 13%
where the time goes in v4:
time: 73.6 us; the launch traced here: 72.6 us
  starting transfers between devices  32.1 us (44%)
  waiting for transfers between devices  24.7 us (34%)
  Pallas kernels  12.3 us (17%)
  local copies, waits for them, and re-layouts  1.85 us (3%)
  other arithmetic  0.84 us (1%)
  between operations  0.8 us (1%)
    ppermute x29, starting transfers between devices, swap(): lax.ppermute(value, axis, [(s, s ^ mask) for s in range(lax.axis_size(axi...  29.2 us
    ppermute x29, waiting for transfers between devices, swap(): lax.ppermute(value, axis, [(s, s ^ mask) for s in range(lax.axis_size(axi...  22 us
    pallas_call x2, Pallas kernels, forward_half(): pl.pallas_call(forward_half_kernel, in_specs=[pl.BlockSpec(memory_space=S...  3.98 us
    ppermute x1, starting transfers between devices, slope_z_pairs(): far = lax.ppermute(second, 'gz', pairs + [(b, a) for a, b in pairs])  2.93 us
    ppermute x1, waiting for transfers between devices, slope_z_pairs(): far = lax.ppermute(second, 'gz', pairs + [(b, a) for a, b in pairs])  2.74 us
    pallas_call x2, Pallas kernels, inverse_x_half(): pl.pallas_call(inverse_x_half_kernel, in_specs=[pl.BlockSpec(memory_space...  2.68 us
    pallas_call x1, Pallas kernels, middle_half(): pl.pallas_call(middle_half_kernel, in_specs=[pl.BlockSpec(memory_space=SM...  2.55 us
    unnamed x8, local copies, waits for them, and re-layouts  1.82 us
  transfers between devices with their start and end apart: 30, of which 17 were waited for; matrix products, arithmetic and copies ran while one was open for 0% of the time, Pallas kernels for 13%

profile of v4, /device:TPU:8, one launch (start us, length us, event | category | flops | bytes accessed | tf_op | source)
XLA Modules:
  0.0 72.6 jit_solution(3178823632092666894)
XLA Ops:
  0.6 2.7 %collective-permute-start.6 = (f32[2,64,256]{2,1,0:T(8,128)}, f32[2,64,256]{2,1,0:T(8,128)S(1)}, u32[]{:S(2)}, u32[]{:S(2)}) collective-permute-start(f32[2,64,256]{2,1,0:T(8,128)} %density_ref.1), channel_id=1, source_target_pairs={{0,16},{4,20},{8,24},{12,28},{16,0},{20,4},{24,8},{28,12},{1,17},{... | collective-permute-start | bytes 393224 | tf_op jit(solution)/shard_map/ppermute | solution.py:558
  3.3 1.5 %collective-permute-start.1 = (f32[2,64,256]{2,1,0:T(8,128)}, f32[2,64,256]{2,1,0:T(8,128)S(1)}, u32[]{:S(2)}, u32[]{:S(2)}) collective-permute-start(f32[2,64,256]{2,1,0:T(8,128)} %density_ref.1), channel_id=1, source_target_pairs={{0,2},{1,3},{2,0},{3,1},{4,6},{5,7},{6,4},{7,5},{8,10},{9,11},{10,... | collective-permute-start | bytes 393224 | tf_op jit(solution)/shard_map/ppermute | solution.py:558
  11.8 2.0 %forward_half.2 = (f32[2,64,256]{2,1,0:T(8,128)S(1)}, f32[2,64,256]{2,1,0:T(8,128)S(1)}, f32[2,64,256]{2,1,0:T(8,128)S(1)}, f32[2,64,256]{2,1,0:T(8,128)S(1)}) custom-call(s32[3]{0:T(128)S(1)} %pad_add_fusion.at_ref, f32[2,64,256]{2,1,0:T(8,128)S(1)} %get-tuple-element.45.refs_0_, f32[2,64,256]{2,1,0:T(8,128)S(1)} %collective-permute-done.refs_1_, ...), custom_call_target="tpu_custom_call" | custom-call | flops 603979776 | bytes 1835008 | tf_op jit(solution)/shard_map/forward_half/pallas_call | solution.py:381
  15.0 1.5 %collective-permute-start.3 = (f32[2,64,256]{2,1,0:T(8,128)S(1)}, f32[2,64,256]{2,1,0:T(8,128)S(1)}, u32[]{:S(2)}, u32[]{:S(2)}) collective-permute-start(f32[2,64,256]{2,1,0:T(8,128)S(1)} %get-tuple-element.51), channel_id=1, source_target_pairs={{0,4},{4,0},{8,12},{12,8},{16,20},{20,16},{24,28},{28,24},{1,5},{5... | collective-permute-start | bytes 393224 | tf_op jit(solution)/shard_map/ppermute | solution.py:558
  17.0 1.5 %collective-permute-start.5 = (f32[2,64,256]{2,1,0:T(8,128)S(1)}, f32[2,64,256]{2,1,0:T(8,128)S(1)}, u32[]{:S(2)}, u32[]{:S(2)}) collective-permute-start(f32[2,64,256]{2,1,0:T(8,128)S(1)} %get-tuple-element.53), channel_id=1, source_target_pairs={{0,12},{4,8},{8,4},{12,0},{16,28},{20,24},{24,20},{28,16},{1,13},{... | collective-permute-start | bytes 393224 | tf_op jit(solution)/shard_map/ppermute | solution.py:558
  18.5 2.0 %forward_half.3 = (f32[2,64,256]{2,1,0:T(8,128)S(1)}, f32[2,64,256]{2,1,0:T(8,128)S(1)}, f32[2,64,256]{2,1,0:T(8,128)S(1)}, f32[2,64,256]{2,1,0:T(8,128)S(1)}) custom-call(s32[3]{0:T(128)S(1)} %pad_add_fusion.at_ref, f32[2,64,256]{2,1,0:T(8,128)S(1)} %collective-permute-done.6.refs_0_, f32[2,64,256]{2,1,0:T(8,128)S(1)} %collective-permute-done.7.refs_1_, ...), custom_call_target="tpu_custom_call" | custom-call | flops 603979776 | bytes 1835008 | tf_op jit(solution)/shard_map/forward_half/pallas_call | solution.py:381
  20.5 1.6 %collective-permute-start.10 = (f32[2,64,256]{2,1,0:T(8,128)S(1)}, f32[2,64,256]{2,1,0:T(8,128)S(1)}, u32[]{:S(2)}, u32[]{:S(2)}) collective-permute-start(f32[2,64,256]{2,1,0:T(8,128)S(1)} %get-tuple-element.57), channel_id=1, source_target_pairs={{0,4},{4,0},{8,12},{12,8},{16,20},{20,16},{24,28},{28,24},{1,5},{5... | collective-permute-start | bytes 393224 | tf_op jit(solution)/shard_map/ppermute | solution.py:558
  22.6 1.5 %collective-permute-start.12 = (f32[2,64,256]{2,1,0:T(8,128)S(1)}, f32[2,64,256]{2,1,0:T(8,128)S(1)}, u32[]{:S(2)}, u32[]{:S(2)}) collective-permute-start(f32[2,64,256]{2,1,0:T(8,128)S(1)} %get-tuple-element.59), channel_id=1, source_target_pairs={{0,12},{4,8},{8,4},{12,0},{16,28},{20,24},{24,20},{28,16},{1,13},{... | collective-permute-start | bytes 393224 | tf_op jit(solution)/shard_map/ppermute | solution.py:558
  24.1 1.5 %collective-permute-done.5.refs_3_ = f32[2,64,256]{2,1,0:T(8,128)S(1)} collective-permute-done((f32[2,64,256]{2,1,0:T(8,128)S(1)}, f32[2,64,256]{2,1,0:T(8,128)S(1)}, u32[]{:S(2)}, u32[]{:S(2)}) %collective-permute-start.5) | collective-permute-done | bytes 131104 | tf_op jit(solution)/shard_map/ppermute | solution.py:558
  25.6 2.8 %collective-permute-done.10.refs_5_ = f32[2,64,256]{2,1,0:T(8,128)S(1)} collective-permute-done((f32[2,64,256]{2,1,0:T(8,128)S(1)}, f32[2,64,256]{2,1,0:T(8,128)S(1)}, u32[]{:S(2)}, u32[]{:S(2)}) %collective-permute-start.10) | collective-permute-done | bytes 131104 | tf_op jit(solution)/shard_map/ppermute | solution.py:558
  28.5 2.0 %collective-permute-done.12.refs_7_ = f32[2,64,256]{2,1,0:T(8,128)S(1)} collective-permute-done((f32[2,64,256]{2,1,0:T(8,128)S(1)}, f32[2,64,256]{2,1,0:T(8,128)S(1)}, u32[]{:S(2)}, u32[]{:S(2)}) %collective-permute-start.12) | collective-permute-done | bytes 131104 | tf_op jit(solution)/shard_map/ppermute | solution.py:558
  30.6 2.6 %middle_half.1 = (f32[2,64,256]{2,1,0:T(8,128)S(1)}, f32[2,64,256]{2,1,0:T(8,128)S(1)}, f32[2,64,256]{2,1,0:T(8,128)S(1)}, f32[2,64,256]{2,1,0:T(8,128)S(1)}, f3...) custom-call(s32[3]{0:T(128)S(1)} %pad_add_fusion.at_ref, ...), custom_call_target="tpu_custom_call" | custom-call | bytes 6291456 | tf_op jit(solution)/shard_map/middle_half/pallas_call | solution.py:427
  33.1 1.6 %collective-permute-start.16 = (f32[2,64,256]{2,1,0:T(8,128)S(1)}, f32[2,64,256]{2,1,0:T(8,128)S(1)}, u32[]{:S(2)}, u32[]{:S(2)}) collective-permute-start(f32[2,64,256]{2,1,0:T(8,128)S(1)} %get-tuple-element.68), channel_id=1, source_target_pairs={{0,4},{4,0},{8,12},{12,8},{16,20},{20,16},{24,28},{28,24},{1,5},{5... | collective-permute-start | bytes 393224 | tf_op jit(solution)/shard_map/ppermute | solution.py:558
  35.1 1.5 %collective-permute-start.18 = (f32[2,64,256]{2,1,0:T(8,128)S(1)}, f32[2,64,256]{2,1,0:T(8,128)S(1)}, u32[]{:S(2)}, u32[]{:S(2)}) collective-permute-start(f32[2,64,256]{2,1,0:T(8,128)S(1)} %get-tuple-element.70), channel_id=1, source_target_pairs={{0,12},{4,8},{8,4},{12,0},{16,28},{20,24},{24,20},{28,16},{1,13},{... | collective-permute-start | bytes 393224 | tf_op jit(solution)/shard_map/ppermute | solution.py:558
  36.7 1.5 %collective-permute-start.13 = (f32[2,64,256]{2,1,0:T(8,128)S(1)}, f32[2,64,256]{2,1,0:T(8,128)S(1)}, u32[]{:S(2)}, u32[]{:S(2)}) collective-permute-start(f32[2,64,256]{2,1,0:T(8,128)S(1)} %get-tuple-element.61), channel_id=1, source_target_pairs={{0,4},{4,0},{8,12},{12,8},{16,20},{20,16},{24,28},{28,24},{1,5},{5... | collective-permute-start | bytes 393224 | tf_op jit(solution)/shard_map/ppermute | solution.py:558
  41.1 2.8 %collective-permute-done.18.refs_3_ = f32[2,64,256]{2,1,0:T(8,128)S(1)} collective-permute-done((f32[2,64,256]{2,1,0:T(8,128)S(1)}, f32[2,64,256]{2,1,0:T(8,128)S(1)}, u32[]{:S(2)}, u32[]{:S(2)}) %collective-permute-start.18) | collective-permute-done | bytes 131104 | tf_op jit(solution)/shard_map/ppermute | solution.py:558
  48.5 1.6 %collective-permute-start.23 = (f32[2,72,256]{2,1,0:T(8,128)S(1)}, f32[2,72,256]{2,1,0:T(8,128)S(1)}, u32[]{:S(2)}, u32[]{:S(2)}) collective-permute-start(f32[2,72,256]{2,1,0:T(8,128)S(1)} %get-tuple-element.78), channel_id=1, source_target_pairs={{0,2},{1,3},{2,0},{3,1},{4,6},{5,7},{6,4},{7,5},{8,10},{9,11},{10,... | collective-permute-start | bytes 442376 | tf_op jit(solution)/shard_map/ppermute | solution.py:558
  52.0 2.7 %collective-permute-done.23 = f32[2,72,256]{2,1,0:T(8,128)S(1)} collective-permute-done((f32[2,72,256]{2,1,0:T(8,128)S(1)}, f32[2,72,256]{2,1,0:T(8,128)S(1)}, u32[]{:S(2)}, u32[]{:S(2)}) %collective-permute-start.23) | collective-permute-done | bytes 147488 | tf_op jit(solution)/shard_map/ppermute | solution.py:558
  54.7 2.8 %collective-permute-start.26 = (f32[2,72,256]{2,1,0:T(8,128)S(1)}, f32[2,72,256]{2,1,0:T(8,128)S(1)}, u32[]{:S(2)}, u32[]{:S(2)}) collective-permute-start(f32[2,72,256]{2,1,0:T(8,128)S(1)} %add.20), channel_id=1, source_target_pairs={{0,16},{4,20},{8,24},{12,28},{16,0},{20,4},{24,8},{28,12},{1,17},{... | collective-permute-start | bytes 442376 | tf_op jit(solution)/shard_map/ppermute | solution.py:558
  58.0 1.5 %collective-permute-start.27 = (f32[2,72,256]{2,1,0:T(8,128)S(1)}, f32[2,72,256]{2,1,0:T(8,128)S(1)}, u32[]{:S(2)}, u32[]{:S(2)}) collective-permute-start(f32[2,72,256]{2,1,0:T(8,128)S(1)} %get-tuple-element.84), channel_id=1, source_target_pairs={{0,2},{1,3},{2,0},{3,1},{4,6},{5,7},{6,4},{7,5},{8,10},{9,11},{10,... | collective-permute-start | bytes 442376 | tf_op jit(solution)/shard_map/ppermute | solution.py:558
  59.5 3.5 %collective-permute-done.26 = f32[2,72,256]{2,1,0:T(8,128)S(1)} collective-permute-done((f32[2,72,256]{2,1,0:T(8,128)S(1)}, f32[2,72,256]{2,1,0:T(8,128)S(1)}, u32[]{:S(2)}, u32[]{:S(2)}) %collective-permute-start.26) | collective-permute-done | bytes 147488 | tf_op jit(solution)/shard_map/ppermute | solution.py:558
  63.2 1.7 %collective-permute-start.28 = (f32[64,256]{1,0:T(8,128)S(1)}, f32[64,256]{1,0:T(8,128)S(1)}, u32[]{:S(2)}, u32[]{:S(2)}) collective-permute-start(f32[64,256]{1,0:T(8,128)S(1)} %get-tuple-element.90.first_ref), channel_id=1, source_target_pairs={{0,4},{4,0},{8,12},{12,8},{16,20},{20,16},{24,28},{28,24},{1,5},{5... | collective-permute-start | bytes 196616 | tf_op jit(solution)/shard_map/ppermute | solution.py:558
  64.9 2.9 %collective-permute-start.29 = (f32[64,256]{1,0:T(8,128)S(1)}, f32[64,256]{1,0:T(8,128)S(1)}, u32[]{:S(2)}, u32[]{:S(2)}) collective-permute-start(f32[64,256]{1,0:T(8,128)S(1)} %get-tuple-element.89.second_ref), channel_id=1, source_target_pairs={{4,8},{12,16},{20,24},{8,4},{16,12},{24,20},{5,9},{13,17},{21,25},... | collective-permute-start | bytes 196616 | tf_op jit(solution)/shard_map/ppermute | solution.py:549
  69.2 2.7 %collective-permute-done.29 = f32[64,256]{1,0:T(8,128)S(1)} collective-permute-done((f32[64,256]{1,0:T(8,128)S(1)}, f32[64,256]{1,0:T(8,128)S(1)}, u32[]{:S(2)}, u32[]{:S(2)}) %collective-permute-start.29) | collective-permute-done | bytes 65568 | tf_op jit(solution)/shard_map/ppermute | solution.py:549
  (63 shorter events, 21.7 us)
Async XLA Ops:
  0.6 8.4 %collective-permute-start.6 = (f32[2,64,256]{2,1,0:T(8,128)}, f32[2,64,256]{2,1,0:T(8,128)S(1)}, u32[]{:S(2)}, u32[]{:S(2)}) collective-permute-start(f32[2,64,256]{2,1,0:T(8,128)} %density_ref.1), channel_id=1, source_target_pairs={{0,16},{4,20},{8,24},{12,28},{16,0},{20,4},{24,8},{28,12},{1,17},{... | collective-permute-start | bytes 393224 | tf_op jit(solution)/shard_map/ppermute | solution.py:558
  3.3 7.3 %collective-permute-start = (f32[2,64,256]{2,1,0:T(8,128)}, f32[2,64,256]{2,1,0:T(8,128)S(1)}, u32[]{:S(2)}, u32[]{:S(2)}) collective-permute-start(f32[2,64,256]{2,1,0:T(8,128)} %density_ref.1), channel_id=1, source_target_pairs={{0,1},{1,0},{2,3},{3,2},{4,5},{5,4},{6,7},{7,6},{8,9},{9,8},{10,11... | collective-permute-start | bytes 393224 | tf_op jit(solution)/shard_map/ppermute | solution.py:558
  3.3 7.3 %collective-permute-start.1 = (f32[2,64,256]{2,1,0:T(8,128)}, f32[2,64,256]{2,1,0:T(8,128)S(1)}, u32[]{:S(2)}, u32[]{:S(2)}) collective-permute-start(f32[2,64,256]{2,1,0:T(8,128)} %density_ref.1), channel_id=1, source_target_pairs={{0,2},{1,3},{2,0},{3,1},{4,6},{5,7},{6,4},{7,5},{8,10},{9,11},{10,... | collective-permute-start | bytes 393224 | tf_op jit(solution)/shard_map/ppermute | solution.py:558
  4.8 7.0 %collective-permute-start.2 = (f32[2,64,256]{2,1,0:T(8,128)}, f32[2,64,256]{2,1,0:T(8,128)S(1)}, u32[]{:S(2)}, u32[]{:S(2)}) collective-permute-start(f32[2,64,256]{2,1,0:T(8,128)} %density_ref.1), channel_id=1, source_target_pairs={{0,3},{1,2},{2,1},{3,0},{4,7},{5,6},{6,5},{7,4},{8,11},{9,10},{10,... | collective-permute-start | bytes 393224 | tf_op jit(solution)/shard_map/ppermute | solution.py:558
  9.1 6.0 %collective-permute-start.8 = (f32[2,64,256]{2,1,0:T(8,128)S(1)}, f32[2,64,256]{2,1,0:T(8,128)S(1)}, u32[]{:S(2)}, u32[]{:S(2)}) collective-permute-start(f32[2,64,256]{2,1,0:T(8,128)S(1)} %collective-permute-done.6.refs_0_), channel_id=1, source_target_pairs={{0,2},{1,3},{2,0},{3,1},{4,6},{5,7},{6,4},{7,5},{8,10},{9,11},{10,... | collective-permute-start | bytes 393224 | tf_op jit(solution)/shard_map/ppermute | solution.py:558
  10.5 8.0 %collective-permute-start.7 = (f32[2,64,256]{2,1,0:T(8,128)S(1)}, f32[2,64,256]{2,1,0:T(8,128)S(1)}, u32[]{:S(2)}, u32[]{:S(2)}) collective-permute-start(f32[2,64,256]{2,1,0:T(8,128)S(1)} %collective-permute-done.6.refs_0_), channel_id=1, source_target_pairs={{0,1},{1,0},{2,3},{3,2},{4,5},{5,4},{6,7},{7,6},{8,9},{9,8},{10,11... | collective-permute-start | bytes 393224 | tf_op jit(solution)/shard_map/ppermute | solution.py:558
  15.0 7.5 %collective-permute-start.3 = (f32[2,64,256]{2,1,0:T(8,128)S(1)}, f32[2,64,256]{2,1,0:T(8,128)S(1)}, u32[]{:S(2)}, u32[]{:S(2)}) collective-permute-start(f32[2,64,256]{2,1,0:T(8,128)S(1)} %get-tuple-element.51), channel_id=1, source_target_pairs={{0,4},{4,0},{8,12},{12,8},{16,20},{20,16},{24,28},{28,24},{1,5},{5... | collective-permute-start | bytes 393224 | tf_op jit(solution)/shard_map/ppermute | solution.py:558
  16.5 7.5 %collective-permute-start.4 = (f32[2,64,256]{2,1,0:T(8,128)S(1)}, f32[2,64,256]{2,1,0:T(8,128)S(1)}, u32[]{:S(2)}, u32[]{:S(2)}) collective-permute-start(f32[2,64,256]{2,1,0:T(8,128)S(1)} %get-tuple-element.52), channel_id=1, source_target_pairs={{0,8},{4,12},{8,0},{12,4},{16,24},{20,28},{24,16},{28,20},{1,9},{5... | collective-permute-start | bytes 393224 | tf_op jit(solution)/shard_map/ppermute | solution.py:558
  17.0 8.6 %collective-permute-start.5 = (f32[2,64,256]{2,1,0:T(8,128)S(1)}, f32[2,64,256]{2,1,0:T(8,128)S(1)}, u32[]{:S(2)}, u32[]{:S(2)}) collective-permute-start(f32[2,64,256]{2,1,0:T(8,128)S(1)} %get-tuple-element.53), channel_id=1, source_target_pairs={{0,12},{4,8},{8,4},{12,0},{16,28},{20,24},{24,20},{28,16},{1,13},{... | collective-permute-start | bytes 393224 | tf_op jit(solution)/shard_map/ppermute | solution.py:558
  20.5 7.9 %collective-permute-start.10 = (f32[2,64,256]{2,1,0:T(8,128)S(1)}, f32[2,64,256]{2,1,0:T(8,128)S(1)}, u32[]{:S(2)}, u32[]{:S(2)}) collective-permute-start(f32[2,64,256]{2,1,0:T(8,128)S(1)} %get-tuple-element.57), channel_id=1, source_target_pairs={{0,4},{4,0},{8,12},{12,8},{16,20},{20,16},{24,28},{28,24},{1,5},{5... | collective-permute-start | bytes 393224 | tf_op jit(solution)/shard_map/ppermute | solution.py:558
  22.1 6.4 %collective-permute-start.11 = (f32[2,64,256]{2,1,0:T(8,128)S(1)}, f32[2,64,256]{2,1,0:T(8,128)S(1)}, u32[]{:S(2)}, u32[]{:S(2)}) collective-permute-start(f32[2,64,256]{2,1,0:T(8,128)S(1)} %get-tuple-element.58), channel_id=1, source_target_pairs={{0,8},{4,12},{8,0},{12,4},{16,24},{20,28},{24,16},{28,20},{1,9},{5... | collective-permute-start | bytes 393224 | tf_op jit(solution)/shard_map/ppermute | solution.py:558
  22.6 8.0 %collective-permute-start.12 = (f32[2,64,256]{2,1,0:T(8,128)S(1)}, f32[2,64,256]{2,1,0:T(8,128)S(1)}, u32[]{:S(2)}, u32[]{:S(2)}) collective-permute-start(f32[2,64,256]{2,1,0:T(8,128)S(1)} %get-tuple-element.59), channel_id=1, source_target_pairs={{0,12},{4,8},{8,4},{12,0},{16,28},{20,24},{24,20},{28,16},{1,13},{... | collective-permute-start | bytes 393224 | tf_op jit(solution)/shard_map/ppermute | solution.py:558
  33.1 6.5 %collective-permute-start.16 = (f32[2,64,256]{2,1,0:T(8,128)S(1)}, f32[2,64,256]{2,1,0:T(8,128)S(1)}, u32[]{:S(2)}, u32[]{:S(2)}) collective-permute-start(f32[2,64,256]{2,1,0:T(8,128)S(1)} %get-tuple-element.68), channel_id=1, source_target_pairs={{0,4},{4,0},{8,12},{12,8},{16,20},{20,16},{24,28},{28,24},{1,5},{5... | collective-permute-start | bytes 393224 | tf_op jit(solution)/shard_map/ppermute | solution.py:558
  34.7 6.4 %collective-permute-start.17 = (f32[2,64,256]{2,1,0:T(8,128)S(1)}, f32[2,64,256]{2,1,0:T(8,128)S(1)}, u32[]{:S(2)}, u32[]{:S(2)}) collective-permute-start(f32[2,64,256]{2,1,0:T(8,128)S(1)} %get-tuple-element.69), channel_id=1, source_target_pairs={{0,8},{4,12},{8,0},{12,4},{16,24},{20,28},{24,16},{28,20},{1,9},{5... | collective-permute-start | bytes 393224 | tf_op jit(solution)/shard_map/ppermute | solution.py:558
  35.1 8.8 %collective-permute-start.18 = (f32[2,64,256]{2,1,0:T(8,128)S(1)}, f32[2,64,256]{2,1,0:T(8,128)S(1)}, u32[]{:S(2)}, u32[]{:S(2)}) collective-permute-start(f32[2,64,256]{2,1,0:T(8,128)S(1)} %get-tuple-element.70), channel_id=1, source_target_pairs={{0,12},{4,8},{8,4},{12,0},{16,28},{20,24},{24,20},{28,16},{1,13},{... | collective-permute-start | bytes 393224 | tf_op jit(solution)/shard_map/ppermute | solution.py:558
  36.7 13.4 %collective-permute-start.13 = (f32[2,64,256]{2,1,0:T(8,128)S(1)}, f32[2,64,256]{2,1,0:T(8,128)S(1)}, u32[]{:S(2)}, u32[]{:S(2)}) collective-permute-start(f32[2,64,256]{2,1,0:T(8,128)S(1)} %get-tuple-element.61), channel_id=1, source_target_pairs={{0,4},{4,0},{8,12},{12,8},{16,20},{20,16},{24,28},{28,24},{1,5},{5... | collective-permute-start | bytes 393224 | tf_op jit(solution)/shard_map/ppermute | solution.py:558
  38.2 11.9 %collective-permute-start.14 = (f32[2,64,256]{2,1,0:T(8,128)S(1)}, f32[2,64,256]{2,1,0:T(8,128)S(1)}, u32[]{:S(2)}, u32[]{:S(2)}) collective-permute-start(f32[2,64,256]{2,1,0:T(8,128)S(1)} %get-tuple-element.62), channel_id=1, source_target_pairs={{0,8},{4,12},{8,0},{12,4},{16,24},{20,28},{24,16},{28,20},{1,9},{5... | collective-permute-start | bytes 393224 | tf_op jit(solution)/shard_map/ppermute | solution.py:558
  39.7 10.4 %collective-permute-start.15 = (f32[2,64,256]{2,1,0:T(8,128)S(1)}, f32[2,64,256]{2,1,0:T(8,128)S(1)}, u32[]{:S(2)}, u32[]{:S(2)}) collective-permute-start(f32[2,64,256]{2,1,0:T(8,128)S(1)} %get-tuple-element.63), channel_id=1, source_target_pairs={{0,12},{4,8},{8,4},{12,0},{16,28},{20,24},{24,20},{28,16},{1,13},{... | collective-permute-start | bytes 393224 | tf_op jit(solution)/shard_map/ppermute | solution.py:558
  48.5 6.2 %collective-permute-start.23 = (f32[2,72,256]{2,1,0:T(8,128)S(1)}, f32[2,72,256]{2,1,0:T(8,128)S(1)}, u32[]{:S(2)}, u32[]{:S(2)}) collective-permute-start(f32[2,72,256]{2,1,0:T(8,128)S(1)} %get-tuple-element.78), channel_id=1, source_target_pairs={{0,2},{1,3},{2,0},{3,1},{4,6},{5,7},{6,4},{7,5},{8,10},{9,11},{10,... | collective-permute-start | bytes 442376 | tf_op jit(solution)/shard_map/ppermute | solution.py:558
  51.4 6.1 %collective-permute-start.24 = (f32[2,72,256]{2,1,0:T(8,128)S(1)}, f32[2,72,256]{2,1,0:T(8,128)S(1)}, u32[]{:S(2)}, u32[]{:S(2)}) collective-permute-start(f32[2,72,256]{2,1,0:T(8,128)S(1)} %get-tuple-element.81), channel_id=1, source_target_pairs={{0,1},{1,0},{2,3},{3,2},{4,5},{5,4},{6,7},{7,6},{8,9},{9,8},{10,11... | collective-permute-start | bytes 442376 | tf_op jit(solution)/shard_map/ppermute | solution.py:558
  51.6 6.0 %collective-permute-start.25 = (f32[2,72,256]{2,1,0:T(8,128)S(1)}, f32[2,72,256]{2,1,0:T(8,128)S(1)}, u32[]{:S(2)}, u32[]{:S(2)}) collective-permute-start(f32[2,72,256]{2,1,0:T(8,128)S(1)} %get-tuple-element.82), channel_id=1, source_target_pairs={{0,1},{1,0},{2,3},{3,2},{4,5},{5,4},{6,7},{7,6},{8,9},{9,8},{10,11... | collective-permute-start | bytes 442376 | tf_op jit(solution)/shard_map/ppermute | solution.py:558
  54.7 8.3 %collective-permute-start.26 = (f32[2,72,256]{2,1,0:T(8,128)S(1)}, f32[2,72,256]{2,1,0:T(8,128)S(1)}, u32[]{:S(2)}, u32[]{:S(2)}) collective-permute-start(f32[2,72,256]{2,1,0:T(8,128)S(1)} %add.20), channel_id=1, source_target_pairs={{0,16},{4,20},{8,24},{12,28},{16,0},{20,4},{24,8},{28,12},{1,17},{... | collective-permute-start | bytes 442376 | tf_op jit(solution)/shard_map/ppermute | solution.py:558
  63.2 6.0 %collective-permute-start.28 = (f32[64,256]{1,0:T(8,128)S(1)}, f32[64,256]{1,0:T(8,128)S(1)}, u32[]{:S(2)}, u32[]{:S(2)}) collective-permute-start(f32[64,256]{1,0:T(8,128)S(1)} %get-tuple-element.90.first_ref), channel_id=1, source_target_pairs={{0,4},{4,0},{8,12},{12,8},{16,20},{20,16},{24,28},{28,24},{1,5},{5... | collective-permute-start | bytes 196616 | tf_op jit(solution)/shard_map/ppermute | solution.py:558
  64.9 7.0 %collective-permute-start.29 = (f32[64,256]{1,0:T(8,128)S(1)}, f32[64,256]{1,0:T(8,128)S(1)}, u32[]{:S(2)}, u32[]{:S(2)}) collective-permute-start(f32[64,256]{1,0:T(8,128)S(1)} %get-tuple-element.89.second_ref), channel_id=1, source_target_pairs={{4,8},{12,16},{20,24},{8,4},{16,12},{24,20},{5,9},{13,17},{21,25},... | collective-permute-start | bytes 196616 | tf_op jit(solution)/shard_map/ppermute | solution.py:549
  (10 other events, 53.2 us)

commit v5 on v4

--- a/solution.py
+++ b/solution.py
@@ -269,17 +269,35 @@
     return np.concatenate([np.cos(angle), np.sin(angle)], axis=1).astype(np.float32)
 
 
-def tables_kernel(space, parts, at_ref, turn_ref, density_ref, *outs):
+def shuffled(value, index, block):
+    wide = value.shape[1]
+    while block < wide:
+        if block % 128 == 0:
+            parts = [value[:, i : i + block] for i in range(0, wide, block)]
+            pairs = [parts[i ^ 1] for i in range(len(parts))]
+        else:
+            parts = [value[:, i : i + 2 * block] for i in range(0, wide, 2 * block)]
+            pairs = [pltpu.roll(p, block, 1) for p in parts]
+        value = jnp.where(index % 2 == 1, jnp.concatenate(pairs, axis=1), value)
+        index, block = index // 2, 2 * block
+    return value
+
+
+def tables_kernel(space, parts, group, at_ref, turn_ref, density_ref, *refs):
+    outs, (x_ref, k_ref) = refs[:9], refs[9:]
     outs[8][...] = density_ref[...]
-    me, side = at_ref[0], at_ref[1]
+    me, side, member = at_ref[0], at_ref[1], at_ref[2]
     coarse = 2 * space // 8
-    cos, sin = turn_ref[coarse:, :space], turn_ref[coarse:, space:]
-    odd = lax.broadcasted_iota(jnp.int32, cos.shape, 0) % 2 == 1
-    sign = jnp.where(odd & (side == 1), -1.0, 1.0)
-    flip_cos, flip_sin = cos * sign, sin * sign
-
-    def turned_by(row, cos, sin):
-        c, s = turn_ref[pl.ds(row, 1), :space], turn_ref[pl.ds(row, 1), space:]
+    count, block = space // parts, space // group
+    for half in (slice(0, space), slice(space, 2 * space)):
+        x_ref[:, half] = shuffled(turn_ref[:, half], me, count)
+        k_ref[:, half] = shuffled(turn_ref[:, half], member, block)
+
+    def fine(ref):
+        return ref[coarse:, :space], ref[coarse:, space:]
+
+    def turned_by(ref, row, cos, sin):
+        c, s = ref[pl.ds(row, 1), :space], ref[pl.ds(row, 1), space:]
         return c * cos - s * sin, c * sin + s * cos
 
     def put(pair, at, lanes, values):
@@ -288,37 +306,45 @@
 
     every = slice(0, space)
     first, second = slice(0, space), slice(space, 2 * space)
-    count = space // parts
     freq = 2 * space // parts
     for k in range(2):
         base = (me ^ k) * (freq // 8)
         pair = outs[2 * k : 2 * k + 2]
         for row in range(0, freq, 16):
-            two = [turned_by(base + row // 8 + i, cos, sin) for i in range(2)]
+            two = [turned_by(turn_ref, base + row // 8 + i, *fine(turn_ref)) for i in range(2)]
             put(pair, row, every, [v[0] for v in two])
             put(pair, freq + row, every, [-v[1] for v in two])
-    pair = outs[4:6]
     for row in range(0, space, 16):
-        two = [turned_by(side * (space // 8) + row // 8 + i, cos, sin) for i in range(2)]
-        put(pair, row, first, [v[0] for v in two])
-        put(pair, row, second, [-v[1] for v in two])
+        base = side * (space // 8) + (member ^ (row // block)) * (block // 8) + row % block // 8
+        two = [turned_by(x_ref, base + i, *fine(x_ref)) for i in range(2)]
+        put(outs[4:6], row, first, [v[0] for v in two])
+        put(outs[4:6], row, second, [-v[1] for v in two])
     tiles = []
+    cos, sin = fine(k_ref)
     which = lax.broadcasted_iota(jnp.int32, cos.shape, 0)
-    for part in range(parts):
-        start = part * count
-        tiles += [turned_by(row // 8, flip_cos, flip_sin) for row in range(start, start + count, 8)]
-        edge = []
-        for row in (max(start - 1, 0), min(start + count, space - 1)):
-            fine = row % 8
-            edge.append(turned_by(row // 8, flip_cos[fine : fine + 1], flip_sin[fine : fine + 1]))
-        tiles.append(tuple(jnp.where(which == 0, edge[0][i], edge[1][i]) for i in range(2)))
+    sign = jnp.where((which % 2 == 1) & (side == 1), -1.0, 1.0)
+    cos, sin = cos * sign, sin * sign
+    for k in range(parts):
+        part = me ^ k
+        base = part * (count // 8)
+        tiles += [turned_by(k_ref, base + i, cos, sin) for i in range(count // 8)]
+        start, end = part == 0, part == parts - 1
+        edges = []
+        for near, step, inside, outside in ((start, -1, 7, 0), (end, count // 8, 0, 7)):
+            row = jnp.where(near, base if step < 0 else base + step - 1, base + step)
+            edges.append(
+                turned_by(
+                    k_ref, row, *[jnp.where(near, v[outside : outside + 1], v[inside : inside + 1]) for v in (cos, sin)]
+                )
+            )
+        tiles.append(tuple(jnp.where(which == 0, edges[0][i], edges[1][i]) for i in range(2)))
     for row in range(0, 8 * len(tiles), 16):
         two = tiles[row // 8 : row // 8 + 2]
         put(outs[6:8], row, first, [v[0] for v in two])
-        put(outs[6:], row, second, [v[1] for v in two])
-
-
-def tables(at, density, parts):
+        put(outs[6:8], row, second, [v[1] for v in two])
+
+
+def tables(at, density, parts, group):
     space = density.shape[2]
     turn = turn_table(space)
     high = lambda *shape: [jax.ShapeDtypeStruct(shape, jnp.bfloat16)] * 2
@@ -326,10 +352,11 @@
     shapes += high(space + 8 * parts, 2 * space)
     shapes += [jax.ShapeDtypeStruct(density.shape, density.dtype)]
     out = pl.pallas_call(
-        functools.partial(tables_kernel, space, parts),
+        functools.partial(tables_kernel, space, parts, group),
         in_specs=[pl.BlockSpec(memory_space=SMEM)] + pieces_spec(2),
         out_specs=pieces_spec(len(shapes)),
         out_shape=shapes,
+        scratch_shapes=[VMEM(turn.shape, jnp.float32)] * 2,
         compiler_params=pltpu.CompilerParams(vmem_limit_bytes=LIMIT),
         cost_estimate=cost(0, (turn, *shapes)),
         name="tables",
@@ -337,33 +364,23 @@
     return out[8], *[out[i : i + 2] for i in range(0, 8, 2)]
 
 
-def forward_half_kernel(at_ref, *refs):
+def turned_halves(value):
+    return tuple(turned(v) for v in split(value))
+
+
+def forward_half_kernel(*refs):
     parts = lax.axis_size("gx")
-    group = lax.axis_size("gz") // 2
-    me, member = at_ref[0], at_ref[2]
     rows, refs = refs[:parts], refs[parts:]
-    yh_ref, yl_ref, th_ref, tl_ref, *refs = refs
-    outs, (high_ref, low_ref, res_ref) = refs[:group], refs[group:]
+    yh_ref, yl_ref, th_ref, tl_ref, *outs = refs
     table_y = (yh_ref[...], yl_ref[...])
     table_x = (th_ref[...], tl_ref[...])
-    count = rows[0].shape[1]
-    width = count * parts
+    kx = outs[0].shape[1]
     for z in range(rows[0].shape[0]):
         both = jnp.concatenate([r[z] for r in rows], axis=0)
         spec = product3(split(both), table_y, ((1,), (1,)))
-        wide = spec.shape[1] // 2
-        high, low = split(spec)
-        for k in range(parts):
-            start = pl.multiple_of((me ^ k) * count, count)
-            for ref, value in ((high_ref, high), (low_ref, low)):
-                value = value[k * count : (k + 1) * count]
-                ref[z, pl.ds(start, count), :] = value
-                ref[z, pl.ds(width + start, count), :wide] = -value[:, wide:]
-                ref[z, pl.ds(width + start, count), wide:] = value[:, :wide]
-        res = product3(table_x, (high_ref[z], low_ref[z]), ((1,), (0,)))
-        res_ref[z] = res.reshape(res_ref.shape[1:])
-        for k in range(group):
-            outs[k][z] = res_ref[z, member ^ k]
+        res = product3(table_x, turned_halves(spec), ((1,), (0,)))
+        for k, ref in enumerate(outs):
+            ref[z] = res[k * kx : (k + 1) * kx]
 
 
 def cost(flops, arrays):
@@ -371,27 +388,21 @@
     return pl.CostEstimate(flops=flops, bytes_accessed=size, transcendentals=0)
 
 
-def forward_half(at, rows, table_y, table_x, group):
+def forward_half(rows, table_y, table_x, group):
     slabs, count, height = rows[0].shape
     width = count * len(rows)
     wide = table_y[0].shape[0]
-    kx = width // group
-    shape = jax.ShapeDtypeStruct((slabs, kx, wide), jnp.float32)
+    shape = jax.ShapeDtypeStruct((slabs, width // group, wide), jnp.float32)
     ins = (*rows, *table_y, *table_x)
     return pl.pallas_call(
         forward_half_kernel,
-        in_specs=[pl.BlockSpec(memory_space=SMEM)] + pieces_spec(len(ins)),
+        in_specs=pieces_spec(len(ins)),
         out_specs=pieces_spec(group),
         out_shape=[shape] * group,
-        scratch_shapes=[
-            VMEM((slabs, 2 * width, wide), jnp.bfloat16),
-            VMEM((slabs, 2 * width, wide), jnp.bfloat16),
-            VMEM((slabs, group, kx, wide), jnp.float32),
-        ],
+        compiler_params=pltpu.CompilerParams(vmem_limit_bytes=LIMIT),
         cost_estimate=cost(6 * slabs * width * wide * (height + 2 * width), (*ins, *[shape] * group)),
-        compiler_params=pltpu.CompilerParams(vmem_limit_bytes=LIMIT),
         name="forward_half",
-    )(at, *ins)
+    )(*ins)
 
 
 def middle_half_kernel(at_ref, *refs):
@@ -436,29 +447,19 @@
     )(at, *ins)
 
 
-def inverse_x_half_kernel(at_ref, *refs):
-    parts = lax.axis_size("gx")
+def inverse_x_half_kernel(*refs):
     group = lax.axis_size("gz") // 2
-    me, member = at_ref[0], at_ref[2]
-    ins, (th_ref, tl_ref), refs = refs[:group], refs[group : group + 2], refs[group + 2 :]
-    outs, (high_ref, low_ref, res_ref) = refs[:parts], refs[parts:]
+    ins, (th_ref, tl_ref), outs = refs[:group], refs[group : group + 2], refs[group + 2 :]
     table = (th_ref[...], tl_ref[...])
-    _, kx, wide = ins[0].shape
-    wide //= 2
+    count = outs[0].shape[1]
     for z in range(ins[0].shape[0]):
-        for k in range(group):
-            start = pl.multiple_of((member ^ k) * kx, kx)
-            for ref, value in zip((high_ref, low_ref), split(ins[k][z])):
-                ref[z, pl.ds(start, kx), :] = value
-                ref[z, pl.ds(group * kx + start, kx), :wide] = -value[:, wide:]
-                ref[z, pl.ds(group * kx + start, kx), wide:] = value[:, :wide]
-        res = product3(table, (high_ref[z], low_ref[z]), ((1,), (0,)))
-        res_ref[z] = res.reshape(res_ref.shape[1:])
-        for k in range(parts):
-            outs[k][z] = res_ref[z, me ^ k]
-
-
-def inverse_x_half(at, field, table, parts):
+        field = jnp.concatenate([r[z] for r in ins], axis=0)
+        res = product3(table, turned_halves(field), ((1,), (0,)))
+        for k, ref in enumerate(outs):
+            ref[z] = res[k * count : (k + 1) * count]
+
+
+def inverse_x_half(field, table, parts):
     slabs, kx, wide = field[0].shape
     width = len(field) * kx
     count = width // parts + 8
@@ -466,18 +467,13 @@
     ins = (*field, *table)
     return pl.pallas_call(
         inverse_x_half_kernel,
-        in_specs=[pl.BlockSpec(memory_space=SMEM)] + pieces_spec(len(ins)),
+        in_specs=pieces_spec(len(ins)),
         out_specs=pieces_spec(parts),
         out_shape=[shape] * parts,
-        scratch_shapes=[
-            VMEM((slabs, 2 * width, wide), jnp.bfloat16),
-            VMEM((slabs, 2 * width, wide), jnp.bfloat16),
-            VMEM((slabs, parts, count, wide), jnp.float32),
-        ],
         cost_estimate=cost(12 * slabs * parts * count * width * wide, (*ins, *[shape] * parts)),
         compiler_params=pltpu.CompilerParams(vmem_limit_bytes=LIMIT),
         name="inverse_x_half",
-    )(at, *ins)
+    )(*ins)
 
 
 def inverse_y_partial_kernel(chips, *refs):
@@ -582,20 +578,19 @@
     at = place()
     other = swap(density, "gz", group)
     raw = exchange([density] * gx, "gx")
-    local, near_y, far_y, ahead, back = tables(at, density, gx)
+    local, near_y, far_y, ahead, back = tables(at, density, gx, group)
     other = after(other, near_y)
-    low, high = swap(other, "gx", 1), swap(other, "gx", 2)
-    field = forward_half(at, [local, *raw[1:]], near_y, ahead, group)
-    raw = [other, low, high, swap(after(high, field), "gx", 1)]
+    field = forward_half([local, *raw[1:]], near_y, ahead, group)
+    raw = exchange([other] * gx, "gx")
     field = exchange(field, "gz")
-    field += exchange(forward_half(at, raw, near_y, ahead, group), "gz")
+    field += exchange(forward_half(raw, near_y, ahead, group), "gz")
     field = middle_half(at, field, green, image_green)
     own, far = field[:group], field[group:]
     column = (*near_y, *far_y)
     far, own = exchange(far, "gz"), exchange(own, "gz")
-    part, give = sums_y(inverse_x_half(at, far, back, gx), column, True)
+    part, give = sums_y(inverse_x_half(far, back, gx), column, True)
     part = part + swap(give, "gx", 2)
-    rows = inverse_x_half(at, own, back, gx)
+    rows = inverse_x_half(own, back, gx)
     mine, give = sums_y((after(rows[0], part), *rows[1:]), column, False)
     mine = after(mine + swap(part, "gz", group))
     scale = 1.0 / (8.0 * slabs * gz * width * height)
@@ -607,7 +602,7 @@
 def per_device(density, green, image_green):
     slabs, count, height = density.shape
     width = count * lax.axis_size("gx")
-    if lax.axis_size("gz") == 8 and lax.axis_size("gx") == 4 and slabs == 2 and width == height:
+    if lax.axis_size("gz") == 8 and lax.axis_size("gx") == 4 and slabs == 2 and width == height == 256:
         return halves_device(density, green, image_green)
     gz, gx = lax.axis_size("gz"), lax.axis_size("gx")
     depth = slabs * gz

time: 73.6 us -> 71.5 us (0.971)
  starting transfers between devices: 32.1 us -> 35.5 us
  waiting for transfers between devices: 24.7 us -> 21.9 us
  Pallas kernels: 12.3 us -> 9.74 us
    ppermute x29, starting transfers between devices: 29.2 us -> 32 us  [swap(): lax.ppermute(value, axis, [(s, s ^ mask) for s in range(lax.axis_size(axi...]
    pallas_call x5, Pallas kernels: 7.59 us -> 5.04 us  [the longest x2 2.7 us: forward_half(): pl.pallas_call(forward_half_kernel, in_specs=pieces_spec(len(ins)), out_s...]
    ppermute x29, waiting for transfers between devices: 22 us -> 19.6 us  [swap(): lax.ppermute(value, axis, [(s, s ^ mask) for s in range(lax.axis_size(axi...]
  transfers between devices with their start and end apart: 30 -> 30, of which waited for: 17 -> 15; matrix products, arithmetic and copies ran while one was open for 0% -> 0% of each run, Pallas kernels for 13% -> 10%
where the time goes in v5:
time: 71.5 us; the launch traced here: 70.6 us
  starting transfers between devices  35.5 us (50%)
  waiting for transfers between devices  21.9 us (31%)
  Pallas kernels  9.74 us (14%)
  local copies, waits for them, and re-layouts  1.85 us (3%)
  other arithmetic  0.84 us (1%)
  between operations  0.79 us (1%)
    ppermute x29, starting transfers between devices, swap(): lax.ppermute(value, axis, [(s, s ^ mask) for s in range(lax.axis_size(axi...  32 us
    ppermute x29, waiting for transfers between devices, swap(): lax.ppermute(value, axis, [(s, s ^ mask) for s in range(lax.axis_size(axi...  19.6 us
    ppermute x1, starting transfers between devices, slope_z_pairs(): far = lax.ppermute(second, 'gz', pairs + [(b, a) for a, b in pairs])  3.42 us
    pallas_call x2, Pallas kernels, forward_half(): pl.pallas_call(forward_half_kernel, in_specs=pieces_spec(len(ins)), out_s...  2.7 us
    pallas_call x1, Pallas kernels, middle_half(): pl.pallas_call(middle_half_kernel, in_specs=[pl.BlockSpec(memory_space=SM...  2.54 us
    ppermute x1, waiting for transfers between devices, slope_z_pairs(): far = lax.ppermute(second, 'gz', pairs + [(b, a) for a, b in pairs])  2.24 us
    unnamed x8, local copies, waits for them, and re-layouts  1.82 us
  transfers between devices with their start and end apart: 30, of which 15 were waited for; matrix products, arithmetic and copies ran while one was open for 0% of the time, Pallas kernels for 10%

profile of v5, /device:TPU:8, one launch (start us, length us, event | category | flops | bytes accessed | tf_op | source)
XLA Modules:
  0.0 70.6 jit_solution(6548510575763764084)
XLA Ops:
  0.6 2.7 %collective-permute-start.6 = (f32[2,64,256]{2,1,0:T(8,128)}, f32[2,64,256]{2,1,0:T(8,128)S(1)}, u32[]{:S(2)}, u32[]{:S(2)}) collective-permute-start(f32[2,64,256]{2,1,0:T(8,128)} %density_ref.1), channel_id=1, source_target_pairs={{0,16},{4,20},{8,24},{12,28},{16,0},{20,4},{24,8},{28,12},{1,17},{... | collective-permute-start | bytes 393224 | tf_op jit(solution)/shard_map/ppermute | solution.py:554
  3.3 1.5 %collective-permute-start.1 = (f32[2,64,256]{2,1,0:T(8,128)}, f32[2,64,256]{2,1,0:T(8,128)S(1)}, u32[]{:S(2)}, u32[]{:S(2)}) collective-permute-start(f32[2,64,256]{2,1,0:T(8,128)} %density_ref.1), channel_id=1, source_target_pairs={{0,2},{1,3},{2,0},{3,1},{4,6},{5,7},{6,4},{7,5},{8,10},{9,11},{10,... | collective-permute-start | bytes 393224 | tf_op jit(solution)/shard_map/ppermute | solution.py:554
  9.1 1.5 %collective-permute-start.8 = (f32[2,64,256]{2,1,0:T(8,128)S(1)}, f32[2,64,256]{2,1,0:T(8,128)S(1)}, u32[]{:S(2)}, u32[]{:S(2)}) collective-permute-start(f32[2,64,256]{2,1,0:T(8,128)S(1)} %collective-permute-done.6.refs_0_), channel_id=1, source_target_pairs={{0,2},{1,3},{2,0},{3,1},{4,6},{5,7},{6,4},{7,5},{8,10},{9,11},{10,... | collective-permute-start | bytes 393224 | tf_op jit(solution)/shard_map/ppermute | solution.py:554
  11.8 1.4 %forward_half.2 = (f32[2,64,256]{2,1,0:T(8,128)S(1)}, f32[2,64,256]{2,1,0:T(8,128)S(1)}, f32[2,64,256]{2,1,0:T(8,128)S(1)}, f32[2,64,256]{2,1,0:T(8,128)S(1)}) custom-call(f32[2,64,256]{2,1,0:T(8,128)S(1)} %get-tuple-element.44.refs_0_, f32[2,64,256]{2,1,0:T(8,128)S(1)} %collective-permute-done.refs_1_, f32[2,64,256]{2,1,0:T(8,128)S(1)} %collective-permute-done.1.refs_2_, ...), custom_call_target="tpu_custom_call" | custom-call | flops 603979776 | bytes 1835008 | tf_op jit(solution)/shard_map/forward_half/pallas_call | solution.py:397
  13.2 1.6 %collective-permute-start.3 = (f32[2,64,256]{2,1,0:T(8,128)S(1)}, f32[2,64,256]{2,1,0:T(8,128)S(1)}, u32[]{:S(2)}, u32[]{:S(2)}) collective-permute-start(f32[2,64,256]{2,1,0:T(8,128)S(1)} %get-tuple-element.50), channel_id=1, source_target_pairs={{0,4},{4,0},{8,12},{12,8},{16,20},{20,16},{24,28},{28,24},{1,5},{5... | collective-permute-start | bytes 393224 | tf_op jit(solution)/shard_map/ppermute | solution.py:554
  15.2 1.5 %collective-permute-start.5 = (f32[2,64,256]{2,1,0:T(8,128)S(1)}, f32[2,64,256]{2,1,0:T(8,128)S(1)}, u32[]{:S(2)}, u32[]{:S(2)}) collective-permute-start(f32[2,64,256]{2,1,0:T(8,128)S(1)} %get-tuple-element.52), channel_id=1, source_target_pairs={{0,12},{4,8},{8,4},{12,0},{16,28},{20,24},{24,20},{28,16},{1,13},{... | collective-permute-start | bytes 393224 | tf_op jit(solution)/shard_map/ppermute | solution.py:554
  17.5 1.3 %forward_half.3 = (f32[2,64,256]{2,1,0:T(8,128)S(1)}, f32[2,64,256]{2,1,0:T(8,128)S(1)}, f32[2,64,256]{2,1,0:T(8,128)S(1)}, f32[2,64,256]{2,1,0:T(8,128)S(1)}) custom-call(f32[2,64,256]{2,1,0:T(8,128)S(1)} %collective-permute-done.6.refs_0_, f32[2,64,256]{2,1,0:T(8,128)S(1)} %collective-permute-done.7.refs_1_, ...), custom_call_target="tpu_custom_call" | custom-call | flops 603979776 | bytes 1835008 | tf_op jit(solution)/shard_map/forward_half/pallas_call | solution.py:397
  18.8 1.6 %collective-permute-start.10 = (f32[2,64,256]{2,1,0:T(8,128)S(1)}, f32[2,64,256]{2,1,0:T(8,128)S(1)}, u32[]{:S(2)}, u32[]{:S(2)}) collective-permute-start(f32[2,64,256]{2,1,0:T(8,128)S(1)} %get-tuple-element.55), channel_id=1, source_target_pairs={{0,4},{4,0},{8,12},{12,8},{16,20},{20,16},{24,28},{28,24},{1,5},{5... | collective-permute-start | bytes 393224 | tf_op jit(solution)/shard_map/ppermute | solution.py:554
  22.9 3.2 %collective-permute-done.10.refs_5_ = f32[2,64,256]{2,1,0:T(8,128)S(1)} collective-permute-done((f32[2,64,256]{2,1,0:T(8,128)S(1)}, f32[2,64,256]{2,1,0:T(8,128)S(1)}, u32[]{:S(2)}, u32[]{:S(2)}) %collective-permute-start.10) | collective-permute-done | bytes 131104 | tf_op jit(solution)/shard_map/ppermute | solution.py:554
  26.8 2.0 %collective-permute-done.12.refs_7_ = f32[2,64,256]{2,1,0:T(8,128)S(1)} collective-permute-done((f32[2,64,256]{2,1,0:T(8,128)S(1)}, f32[2,64,256]{2,1,0:T(8,128)S(1)}, u32[]{:S(2)}, u32[]{:S(2)}) %collective-permute-start.12) | collective-permute-done | bytes 131104 | tf_op jit(solution)/shard_map/ppermute | solution.py:554
  28.8 2.5 %middle_half.1 = (f32[2,64,256]{2,1,0:T(8,128)S(1)}, f32[2,64,256]{2,1,0:T(8,128)S(1)}, f32[2,64,256]{2,1,0:T(8,128)S(1)}, f32[2,64,256]{2,1,0:T(8,128)S(1)}, f3...) custom-call(s32[3]{0:T(128)S(1)} %pad_add_fusion.at_ref, ...), custom_call_target="tpu_custom_call" | custom-call | bytes 6291456 | tf_op jit(solution)/shard_map/middle_half/pallas_call | solution.py:438
  31.3 1.6 %collective-permute-start.16 = (f32[2,64,256]{2,1,0:T(8,128)S(1)}, f32[2,64,256]{2,1,0:T(8,128)S(1)}, u32[]{:S(2)}, u32[]{:S(2)}) collective-permute-start(f32[2,64,256]{2,1,0:T(8,128)S(1)} %get-tuple-element.66), channel_id=1, source_target_pairs={{0,4},{4,0},{8,12},{12,8},{16,20},{20,16},{24,28},{28,24},{1,5},{5... | collective-permute-start | bytes 393224 | tf_op jit(solution)/shard_map/ppermute | solution.py:554
  34.9 1.5 %collective-permute-start.13 = (f32[2,64,256]{2,1,0:T(8,128)S(1)}, f32[2,64,256]{2,1,0:T(8,128)S(1)}, u32[]{:S(2)}, u32[]{:S(2)}) collective-permute-start(f32[2,64,256]{2,1,0:T(8,128)S(1)} %get-tuple-element.59), channel_id=1, source_target_pairs={{0,4},{4,0},{8,12},{12,8},{16,20},{20,16},{24,28},{28,24},{1,5},{5... | collective-permute-start | bytes 393224 | tf_op jit(solution)/shard_map/ppermute | solution.py:554
  37.6 2.4 %collective-permute-start.15 = (f32[2,64,256]{2,1,0:T(8,128)S(1)}, f32[2,64,256]{2,1,0:T(8,128)S(1)}, u32[]{:S(2)}, u32[]{:S(2)}) collective-permute-start(f32[2,64,256]{2,1,0:T(8,128)S(1)} %get-tuple-element.61), channel_id=1, source_target_pairs={{0,12},{4,8},{8,4},{12,0},{16,28},{20,24},{24,20},{28,16},{1,13},{... | collective-permute-start | bytes 393224 | tf_op jit(solution)/shard_map/ppermute | solution.py:554
  40.0 2.0 %collective-permute-done.18.refs_3_ = f32[2,64,256]{2,1,0:T(8,128)S(1)} collective-permute-done((f32[2,64,256]{2,1,0:T(8,128)S(1)}, f32[2,64,256]{2,1,0:T(8,128)S(1)}, u32[]{:S(2)}, u32[]{:S(2)}) %collective-permute-start.18) | collective-permute-done | bytes 131104 | tf_op jit(solution)/shard_map/ppermute | solution.py:554
  45.9 1.5 %collective-permute-start.23 = (f32[2,72,256]{2,1,0:T(8,128)S(1)}, f32[2,72,256]{2,1,0:T(8,128)S(1)}, u32[]{:S(2)}, u32[]{:S(2)}) collective-permute-start(f32[2,72,256]{2,1,0:T(8,128)S(1)} %get-tuple-element.76), channel_id=1, source_target_pairs={{0,2},{1,3},{2,0},{3,1},{4,6},{5,7},{6,4},{7,5},{8,10},{9,11},{10,... | collective-permute-start | bytes 442376 | tf_op jit(solution)/shard_map/ppermute | solution.py:554
  48.6 3.4 %collective-permute-done.23 = f32[2,72,256]{2,1,0:T(8,128)S(1)} collective-permute-done((f32[2,72,256]{2,1,0:T(8,128)S(1)}, f32[2,72,256]{2,1,0:T(8,128)S(1)}, u32[]{:S(2)}, u32[]{:S(2)}) %collective-permute-start.23) | collective-permute-done | bytes 147488 | tf_op jit(solution)/shard_map/ppermute | solution.py:554
  52.0 3.5 %collective-permute-start.26 = (f32[2,72,256]{2,1,0:T(8,128)S(1)}, f32[2,72,256]{2,1,0:T(8,128)S(1)}, u32[]{:S(2)}, u32[]{:S(2)}) collective-permute-start(f32[2,72,256]{2,1,0:T(8,128)S(1)} %add.20), channel_id=1, source_target_pairs={{0,16},{4,20},{8,24},{12,28},{16,0},{20,4},{24,8},{28,12},{1,17},{... | collective-permute-start | bytes 442376 | tf_op jit(solution)/shard_map/ppermute | solution.py:554
  55.9 1.6 %collective-permute-start.27 = (f32[2,72,256]{2,1,0:T(8,128)S(1)}, f32[2,72,256]{2,1,0:T(8,128)S(1)}, u32[]{:S(2)}, u32[]{:S(2)}) collective-permute-start(f32[2,72,256]{2,1,0:T(8,128)S(1)} %get-tuple-element.82), channel_id=1, source_target_pairs={{0,2},{1,3},{2,0},{3,1},{4,6},{5,7},{6,4},{7,5},{8,10},{9,11},{10,... | collective-permute-start | bytes 442376 | tf_op jit(solution)/shard_map/ppermute | solution.py:554
  57.5 3.5 %collective-permute-done.26 = f32[2,72,256]{2,1,0:T(8,128)S(1)} collective-permute-done((f32[2,72,256]{2,1,0:T(8,128)S(1)}, f32[2,72,256]{2,1,0:T(8,128)S(1)}, u32[]{:S(2)}, u32[]{:S(2)}) %collective-permute-start.26) | collective-permute-done | bytes 147488 | tf_op jit(solution)/shard_map/ppermute | solution.py:554
  61.2 1.6 %collective-permute-start.28 = (f32[64,256]{1,0:T(8,128)S(1)}, f32[64,256]{1,0:T(8,128)S(1)}, u32[]{:S(2)}, u32[]{:S(2)}) collective-permute-start(f32[64,256]{1,0:T(8,128)S(1)} %get-tuple-element.88.first_ref), channel_id=1, source_target_pairs={{0,4},{4,0},{8,12},{12,8},{16,20},{20,16},{24,28},{28,24},{1,5},{5... | collective-permute-start | bytes 196616 | tf_op jit(solution)/shard_map/ppermute | solution.py:554
  62.8 3.4 %collective-permute-start.29 = (f32[64,256]{1,0:T(8,128)S(1)}, f32[64,256]{1,0:T(8,128)S(1)}, u32[]{:S(2)}, u32[]{:S(2)}) collective-permute-start(f32[64,256]{1,0:T(8,128)S(1)} %get-tuple-element.87.second_ref), channel_id=1, source_target_pairs={{4,8},{12,16},{20,24},{8,4},{16,12},{24,20},{5,9},{13,17},{21,25},... | collective-permute-start | bytes 196616 | tf_op jit(solution)/shard_map/ppermute | solution.py:545
  66.3 1.3 %slopes.1 = (f32[2,64,256]{2,1,0:T(8,128)}, f32[2,64,256]{2,1,0:T(8,128)}) custom-call(s32[3]{0:T(128)S(1)} %pad_add_fusion.at_ref, f32[64,256]{1,0:T(8,128)S(1)} %get-tuple-element.88.first_ref, f32[64,256]{1,0:T(8,128)S(1)} %get-tuple-element.87.second_ref, f32[2,8,256]{2,1,0:T(8,128)S(1)} %slice.38.rows_ref), custom_call_target="tpu_custom_call" | custom-call | bytes 409600 | tf_op jit(solution)/shard_map/slopes/pallas_call | solution.py:529
  67.6 2.2 %collective-permute-done.29 = f32[64,256]{1,0:T(8,128)S(1)} collective-permute-done((f32[64,256]{1,0:T(8,128)S(1)}, f32[64,256]{1,0:T(8,128)S(1)}, u32[]{:S(2)}, u32[]{:S(2)}) %collective-permute-start.29) | collective-permute-done | bytes 65568 | tf_op jit(solution)/shard_map/ppermute | solution.py:545
  (63 shorter events, 19.3 us)
Async XLA Ops:
  0.6 8.4 %collective-permute-start.6 = (f32[2,64,256]{2,1,0:T(8,128)}, f32[2,64,256]{2,1,0:T(8,128)S(1)}, u32[]{:S(2)}, u32[]{:S(2)}) collective-permute-start(f32[2,64,256]{2,1,0:T(8,128)} %density_ref.1), channel_id=1, source_target_pairs={{0,16},{4,20},{8,24},{12,28},{16,0},{20,4},{24,8},{28,12},{1,17},{... | collective-permute-start | bytes 393224 | tf_op jit(solution)/shard_map/ppermute | solution.py:554
  3.3 7.3 %collective-permute-start = (f32[2,64,256]{2,1,0:T(8,128)}, f32[2,64,256]{2,1,0:T(8,128)S(1)}, u32[]{:S(2)}, u32[]{:S(2)}) collective-permute-start(f32[2,64,256]{2,1,0:T(8,128)} %density_ref.1), channel_id=1, source_target_pairs={{0,1},{1,0},{2,3},{3,2},{4,5},{5,4},{6,7},{7,6},{8,9},{9,8},{10,11... | collective-permute-start | bytes 393224 | tf_op jit(solution)/shard_map/ppermute | solution.py:554
  3.3 7.6 %collective-permute-start.1 = (f32[2,64,256]{2,1,0:T(8,128)}, f32[2,64,256]{2,1,0:T(8,128)S(1)}, u32[]{:S(2)}, u32[]{:S(2)}) collective-permute-start(f32[2,64,256]{2,1,0:T(8,128)} %density_ref.1), channel_id=1, source_target_pairs={{0,2},{1,3},{2,0},{3,1},{4,6},{5,7},{6,4},{7,5},{8,10},{9,11},{10,... | collective-permute-start | bytes 393224 | tf_op jit(solution)/shard_map/ppermute | solution.py:554
  4.8 7.0 %collective-permute-start.2 = (f32[2,64,256]{2,1,0:T(8,128)}, f32[2,64,256]{2,1,0:T(8,128)S(1)}, u32[]{:S(2)}, u32[]{:S(2)}) collective-permute-start(f32[2,64,256]{2,1,0:T(8,128)} %density_ref.1), channel_id=1, source_target_pairs={{0,3},{1,2},{2,1},{3,0},{4,7},{5,6},{6,5},{7,4},{8,11},{9,10},{10,... | collective-permute-start | bytes 393224 | tf_op jit(solution)/shard_map/ppermute | solution.py:554
  9.1 6.2 %collective-permute-start.7 = (f32[2,64,256]{2,1,0:T(8,128)S(1)}, f32[2,64,256]{2,1,0:T(8,128)S(1)}, u32[]{:S(2)}, u32[]{:S(2)}) collective-permute-start(f32[2,64,256]{2,1,0:T(8,128)S(1)} %collective-permute-done.6.refs_0_), channel_id=1, source_target_pairs={{0,1},{1,0},{2,3},{3,2},{4,5},{5,4},{6,7},{7,6},{8,9},{9,8},{10,11... | collective-permute-start | bytes 393224 | tf_op jit(solution)/shard_map/ppermute | solution.py:554
  9.1 7.7 %collective-permute-start.8 = (f32[2,64,256]{2,1,0:T(8,128)S(1)}, f32[2,64,256]{2,1,0:T(8,128)S(1)}, u32[]{:S(2)}, u32[]{:S(2)}) collective-permute-start(f32[2,64,256]{2,1,0:T(8,128)S(1)} %collective-permute-done.6.refs_0_), channel_id=1, source_target_pairs={{0,2},{1,3},{2,0},{3,1},{4,6},{5,7},{6,4},{7,5},{8,10},{9,11},{10,... | collective-permute-start | bytes 393224 | tf_op jit(solution)/shard_map/ppermute | solution.py:554
  10.6 6.9 %collective-permute-start.9 = (f32[2,64,256]{2,1,0:T(8,128)S(1)}, f32[2,64,256]{2,1,0:T(8,128)S(1)}, u32[]{:S(2)}, u32[]{:S(2)}) collective-permute-start(f32[2,64,256]{2,1,0:T(8,128)S(1)} %collective-permute-done.6.refs_0_), channel_id=1, source_target_pairs={{0,3},{1,2},{2,1},{3,0},{4,7},{5,6},{6,5},{7,4},{8,11},{9,10},{10,... | collective-permute-start | bytes 393224 | tf_op jit(solution)/shard_map/ppermute | solution.py:554
  13.2 8.4 %collective-permute-start.3 = (f32[2,64,256]{2,1,0:T(8,128)S(1)}, f32[2,64,256]{2,1,0:T(8,128)S(1)}, u32[]{:S(2)}, u32[]{:S(2)}) collective-permute-start(f32[2,64,256]{2,1,0:T(8,128)S(1)} %get-tuple-element.50), channel_id=1, source_target_pairs={{0,4},{4,0},{8,12},{12,8},{16,20},{20,16},{24,28},{28,24},{1,5},{5... | collective-permute-start | bytes 393224 | tf_op jit(solution)/shard_map/ppermute | solution.py:554
  14.8 7.6 %collective-permute-start.4 = (f32[2,64,256]{2,1,0:T(8,128)S(1)}, f32[2,64,256]{2,1,0:T(8,128)S(1)}, u32[]{:S(2)}, u32[]{:S(2)}) collective-permute-start(f32[2,64,256]{2,1,0:T(8,128)S(1)} %get-tuple-element.51), channel_id=1, source_target_pairs={{0,8},{4,12},{8,0},{12,4},{16,24},{20,28},{24,16},{28,20},{1,9},{5... | collective-permute-start | bytes 393224 | tf_op jit(solution)/shard_map/ppermute | solution.py:554
  15.2 7.7 %collective-permute-start.5 = (f32[2,64,256]{2,1,0:T(8,128)S(1)}, f32[2,64,256]{2,1,0:T(8,128)S(1)}, u32[]{:S(2)}, u32[]{:S(2)}) collective-permute-start(f32[2,64,256]{2,1,0:T(8,128)S(1)} %get-tuple-element.52), channel_id=1, source_target_pairs={{0,12},{4,8},{8,4},{12,0},{16,28},{20,24},{24,20},{28,16},{1,13},{... | collective-permute-start | bytes 393224 | tf_op jit(solution)/shard_map/ppermute | solution.py:554
  18.8 7.3 %collective-permute-start.10 = (f32[2,64,256]{2,1,0:T(8,128)S(1)}, f32[2,64,256]{2,1,0:T(8,128)S(1)}, u32[]{:S(2)}, u32[]{:S(2)}) collective-permute-start(f32[2,64,256]{2,1,0:T(8,128)S(1)} %get-tuple-element.55), channel_id=1, source_target_pairs={{0,4},{4,0},{8,12},{12,8},{16,20},{20,16},{24,28},{28,24},{1,5},{5... | collective-permute-start | bytes 393224 | tf_op jit(solution)/shard_map/ppermute | solution.py:554
  20.4 6.3 %collective-permute-start.11 = (f32[2,64,256]{2,1,0:T(8,128)S(1)}, f32[2,64,256]{2,1,0:T(8,128)S(1)}, u32[]{:S(2)}, u32[]{:S(2)}) collective-permute-start(f32[2,64,256]{2,1,0:T(8,128)S(1)} %get-tuple-element.56), channel_id=1, source_target_pairs={{0,8},{4,12},{8,0},{12,4},{16,24},{20,28},{24,16},{28,20},{1,9},{5... | collective-permute-start | bytes 393224 | tf_op jit(solution)/shard_map/ppermute | solution.py:554
  21.6 7.2 %collective-permute-start.12 = (f32[2,64,256]{2,1,0:T(8,128)S(1)}, f32[2,64,256]{2,1,0:T(8,128)S(1)}, u32[]{:S(2)}, u32[]{:S(2)}) collective-permute-start(f32[2,64,256]{2,1,0:T(8,128)S(1)} %get-tuple-element.57), channel_id=1, source_target_pairs={{0,12},{4,8},{8,4},{12,0},{16,28},{20,24},{24,20},{28,16},{1,13},{... | collective-permute-start | bytes 393224 | tf_op jit(solution)/shard_map/ppermute | solution.py:554
  31.3 6.3 %collective-permute-start.16 = (f32[2,64,256]{2,1,0:T(8,128)S(1)}, f32[2,64,256]{2,1,0:T(8,128)S(1)}, u32[]{:S(2)}, u32[]{:S(2)}) collective-permute-start(f32[2,64,256]{2,1,0:T(8,128)S(1)} %get-tuple-element.66), channel_id=1, source_target_pairs={{0,4},{4,0},{8,12},{12,8},{16,20},{20,16},{24,28},{28,24},{1,5},{5... | collective-permute-start | bytes 393224 | tf_op jit(solution)/shard_map/ppermute | solution.py:554
  32.9 7.1 %collective-permute-start.17 = (f32[2,64,256]{2,1,0:T(8,128)S(1)}, f32[2,64,256]{2,1,0:T(8,128)S(1)}, u32[]{:S(2)}, u32[]{:S(2)}) collective-permute-start(f32[2,64,256]{2,1,0:T(8,128)S(1)} %get-tuple-element.67), channel_id=1, source_target_pairs={{0,8},{4,12},{8,0},{12,4},{16,24},{20,28},{24,16},{28,20},{1,9},{5... | collective-permute-start | bytes 393224 | tf_op jit(solution)/shard_map/ppermute | solution.py:554
  34.1 7.9 %collective-permute-start.18 = (f32[2,64,256]{2,1,0:T(8,128)S(1)}, f32[2,64,256]{2,1,0:T(8,128)S(1)}, u32[]{:S(2)}, u32[]{:S(2)}) collective-permute-start(f32[2,64,256]{2,1,0:T(8,128)S(1)} %get-tuple-element.68), channel_id=1, source_target_pairs={{0,12},{4,8},{8,4},{12,0},{16,28},{20,24},{24,20},{28,16},{1,13},{... | collective-permute-start | bytes 393224 | tf_op jit(solution)/shard_map/ppermute | solution.py:554
  34.9 12.5 %collective-permute-start.13 = (f32[2,64,256]{2,1,0:T(8,128)S(1)}, f32[2,64,256]{2,1,0:T(8,128)S(1)}, u32[]{:S(2)}, u32[]{:S(2)}) collective-permute-start(f32[2,64,256]{2,1,0:T(8,128)S(1)} %get-tuple-element.59), channel_id=1, source_target_pairs={{0,4},{4,0},{8,12},{12,8},{16,20},{20,16},{24,28},{28,24},{1,5},{5... | collective-permute-start | bytes 393224 | tf_op jit(solution)/shard_map/ppermute | solution.py:554
  36.4 11.0 %collective-permute-start.14 = (f32[2,64,256]{2,1,0:T(8,128)S(1)}, f32[2,64,256]{2,1,0:T(8,128)S(1)}, u32[]{:S(2)}, u32[]{:S(2)}) collective-permute-start(f32[2,64,256]{2,1,0:T(8,128)S(1)} %get-tuple-element.60), channel_id=1, source_target_pairs={{0,8},{4,12},{8,0},{12,4},{16,24},{20,28},{24,16},{28,20},{1,9},{5... | collective-permute-start | bytes 393224 | tf_op jit(solution)/shard_map/ppermute | solution.py:554
  37.6 9.8 %collective-permute-start.15 = (f32[2,64,256]{2,1,0:T(8,128)S(1)}, f32[2,64,256]{2,1,0:T(8,128)S(1)}, u32[]{:S(2)}, u32[]{:S(2)}) collective-permute-start(f32[2,64,256]{2,1,0:T(8,128)S(1)} %get-tuple-element.61), channel_id=1, source_target_pairs={{0,12},{4,8},{8,4},{12,0},{16,28},{20,24},{24,20},{28,16},{1,13},{... | collective-permute-start | bytes 393224 | tf_op jit(solution)/shard_map/ppermute | solution.py:554
  48.1 7.5 %collective-permute-start.24 = (f32[2,72,256]{2,1,0:T(8,128)S(1)}, f32[2,72,256]{2,1,0:T(8,128)S(1)}, u32[]{:S(2)}, u32[]{:S(2)}) collective-permute-start(f32[2,72,256]{2,1,0:T(8,128)S(1)} %get-tuple-element.79), channel_id=1, source_target_pairs={{0,1},{1,0},{2,3},{3,2},{4,5},{5,4},{6,7},{7,6},{8,9},{9,8},{10,11... | collective-permute-start | bytes 442376 | tf_op jit(solution)/shard_map/ppermute | solution.py:554
  48.2 7.3 %collective-permute-start.25 = (f32[2,72,256]{2,1,0:T(8,128)S(1)}, f32[2,72,256]{2,1,0:T(8,128)S(1)}, u32[]{:S(2)}, u32[]{:S(2)}) collective-permute-start(f32[2,72,256]{2,1,0:T(8,128)S(1)} %get-tuple-element.80), channel_id=1, source_target_pairs={{0,1},{1,0},{2,3},{3,2},{4,5},{5,4},{6,7},{7,6},{8,9},{9,8},{10,11... | collective-permute-start | bytes 442376 | tf_op jit(solution)/shard_map/ppermute | solution.py:554
  52.0 9.0 %collective-permute-start.26 = (f32[2,72,256]{2,1,0:T(8,128)S(1)}, f32[2,72,256]{2,1,0:T(8,128)S(1)}, u32[]{:S(2)}, u32[]{:S(2)}) collective-permute-start(f32[2,72,256]{2,1,0:T(8,128)S(1)} %add.20), channel_id=1, source_target_pairs={{0,16},{4,20},{8,24},{12,28},{16,0},{20,4},{24,8},{28,12},{1,17},{... | collective-permute-start | bytes 442376 | tf_op jit(solution)/shard_map/ppermute | solution.py:554
  61.2 6.5 %collective-permute-start.28 = (f32[64,256]{1,0:T(8,128)S(1)}, f32[64,256]{1,0:T(8,128)S(1)}, u32[]{:S(2)}, u32[]{:S(2)}) collective-permute-start(f32[64,256]{1,0:T(8,128)S(1)} %get-tuple-element.88.first_ref), channel_id=1, source_target_pairs={{0,4},{4,0},{8,12},{12,8},{16,20},{20,16},{24,28},{28,24},{1,5},{5... | collective-permute-start | bytes 196616 | tf_op jit(solution)/shard_map/ppermute | solution.py:554
  62.8 7.0 %collective-permute-start.29 = (f32[64,256]{1,0:T(8,128)S(1)}, f32[64,256]{1,0:T(8,128)S(1)}, u32[]{:S(2)}, u32[]{:S(2)}) collective-permute-start(f32[64,256]{1,0:T(8,128)S(1)} %get-tuple-element.87.second_ref), channel_id=1, source_target_pairs={{4,8},{12,16},{20,24},{8,4},{16,12},{24,20},{5,9},{13,17},{21,25},... | collective-permute-start | bytes 196616 | tf_op jit(solution)/shard_map/ppermute | solution.py:545
  (10 other events, 52.3 us)

commit v6 on v5

--- a/solution.py
+++ b/solution.py
@@ -198,19 +198,17 @@
     )(field, *table)
 
 
-def differences(total, me, parts, gx_ref, gy_ref):
-    count, height = total.shape[0] - 8, total.shape[1]
-    main = total[:count]
+def differences(main, outer, me, parts, gx_ref, gy_ref):
+    count, height = main.shape
     row = lax.broadcasted_iota(jnp.int32, main.shape, 0)
-    before = jnp.where(row == 0, total[count : count + 1], pltpu.roll(main, 1, 0))
-    after = jnp.where(row == count - 1, total[count + 1 : count + 2], pltpu.roll(main, count - 1, 0))
+    before = jnp.where(row == 0, outer[0:1], pltpu.roll(main, 1, 0))
+    after = jnp.where(row == count - 1, outer[1:2], pltpu.roll(main, count - 1, 0))
     edge = ((row == 0) & (me == 0)) | ((row == count - 1) & (me == parts - 1))
     gx_ref[...] = (after - before) * jnp.where(edge, 1.0, 0.5)
     col = lax.broadcasted_iota(jnp.int32, main.shape, 1)
     before = jnp.where(col == 0, main, pltpu.roll(main, 1, 1))
     after = jnp.where(col == height - 1, main, pltpu.roll(main, height - 1, 1))
     gy_ref[...] = (after - before) * jnp.where((col == 0) | (col == height - 1), 1.0, 0.5)
-    return main
 
 
 def inverse_y_kernel(scale, parts, me_ref, s_ref, th_ref, tl_ref, pot_ref, gx_ref, gy_ref):
@@ -223,7 +221,9 @@
             )
             total = term if total is None else total + term
         total = total * scale
-        main = differences(total, me, parts, gx_ref.at[z], gy_ref.at[z])
+        count = total.shape[0] - 8
+        main = total[:count]
+        differences(main, total[count:], me, parts, gx_ref.at[z], gy_ref.at[z])
         pot_ref[z] = main
 
 
@@ -319,7 +319,7 @@
         two = [turned_by(x_ref, base + i, *fine(x_ref)) for i in range(2)]
         put(outs[4:6], row, first, [v[0] for v in two])
         put(outs[4:6], row, second, [-v[1] for v in two])
-    tiles = []
+    tiles, edges = [], []
     cos, sin = fine(k_ref)
     which = lax.broadcasted_iota(jnp.int32, cos.shape, 0)
     sign = jnp.where((which % 2 == 1) & (side == 1), -1.0, 1.0)
@@ -329,7 +329,6 @@
         base = part * (count // 8)
         tiles += [turned_by(k_ref, base + i, cos, sin) for i in range(count // 8)]
         start, end = part == 0, part == parts - 1
-        edges = []
         for near, step, inside, outside in ((start, -1, 7, 0), (end, count // 8, 0, 7)):
             row = jnp.where(near, base if step < 0 else base + step - 1, base + step)
             edges.append(
@@ -337,7 +336,10 @@
                     k_ref, row, *[jnp.where(near, v[outside : outside + 1], v[inside : inside + 1]) for v in (cos, sin)]
                 )
             )
-        tiles.append(tuple(jnp.where(which == 0, edges[0][i], edges[1][i]) for i in range(2)))
+    last = tuple(jnp.broadcast_to(v, cos.shape) for v in edges[0])
+    for i, edge in enumerate(edges[1:]):
+        last = tuple(jnp.where(which == i + 1, e, v) for e, v in zip(edge, last))
+    tiles += [last, last]
     for row in range(0, 8 * len(tiles), 16):
         two = tiles[row // 8 : row // 8 + 2]
         put(outs[6:8], row, first, [v[0] for v in two])
@@ -349,7 +351,7 @@
     turn = turn_table(space)
     high = lambda *shape: [jax.ShapeDtypeStruct(shape, jnp.bfloat16)] * 2
     shapes = high(4 * space // parts, space) * 2 + high(space, 2 * space)
-    shapes += high(space + 8 * parts, 2 * space)
+    shapes += high(space + 16, 2 * space)
     shapes += [jax.ShapeDtypeStruct(density.shape, density.dtype)]
     out = pl.pallas_call(
         functools.partial(tables_kernel, space, parts, group),
@@ -428,7 +430,7 @@
             outs[k][:, rows, :] = out_ref[slab]
         return carry
 
-    lax.fori_loop(0, kx // 8, tile, 0)
+    lax.fori_loop(0, kx // 8, tile, 0, unroll=2)
 
 
 def middle_half(at, field, green, image_green):
@@ -451,55 +453,58 @@
     group = lax.axis_size("gz") // 2
     ins, (th_ref, tl_ref), outs = refs[:group], refs[group : group + 2], refs[group + 2 :]
     table = (th_ref[...], tl_ref[...])
-    count = outs[0].shape[1]
-    for z in range(ins[0].shape[0]):
+    slabs = ins[0].shape[0]
+    count = (outs[0].shape[0] - 8) // slabs
+    inner = count * len(outs)
+    for z in range(slabs):
         field = jnp.concatenate([r[z] for r in ins], axis=0)
         res = product3(table, turned_halves(field), ((1,), (0,)))
         for k, ref in enumerate(outs):
-            ref[z] = res[k * count : (k + 1) * count]
+            ref[z * count : (z + 1) * count] = res[k * count : (k + 1) * count]
+            if z == 0:
+                ref[slabs * count :] = res[inner : inner + 8]
+            at = slabs * count + 2 * z
+            ref[at : at + 2] = res[inner + 2 * k : inner + 2 * k + 2]
 
 
 def inverse_x_half(field, table, parts):
     slabs, kx, wide = field[0].shape
     width = len(field) * kx
-    count = width // parts + 8
-    shape = jax.ShapeDtypeStruct((slabs, count, wide), jnp.float32)
+    shape = jax.ShapeDtypeStruct((slabs * width // parts + 8, wide), jnp.float32)
     ins = (*field, *table)
     return pl.pallas_call(
         inverse_x_half_kernel,
         in_specs=pieces_spec(len(ins)),
         out_specs=pieces_spec(parts),
         out_shape=[shape] * parts,
-        cost_estimate=cost(12 * slabs * parts * count * width * wide, (*ins, *[shape] * parts)),
+        cost_estimate=cost(12 * slabs * (width + 8 * parts) * width * wide, (*ins, *[shape] * parts)),
         compiler_params=pltpu.CompilerParams(vmem_limit_bytes=LIMIT),
         name="inverse_x_half",
     )(*ins)
 
 
 def inverse_y_partial_kernel(chips, *refs):
-    slabs, count, wide = refs[0].shape
     total = None
     outs, refs = refs[-chips:], refs[:-chips]
     for k, ins in enumerate((refs[:chips], refs[chips:-4])):
-        rows = jnp.concatenate([r[...].reshape(-1, wide) for r in ins], axis=0)
+        rows = jnp.concatenate([r[...] for r in ins], axis=0)
         table = [r[...] for r in refs[len(refs) - 4 :][2 * k : 2 * k + 2]]
         term = product3(split(rows), table, ((1,), (0,)))
         total = term if total is None else total + term
-    total = total.reshape(chips, slabs, count, -1)
     for k, ref in enumerate(outs):
-        ref[...] = total[k]
+        ref[...] = total[k * ref.shape[0] : (k + 1) * ref.shape[0]]
 
 
 def inverse_y_partial(keep, near, table):
-    slabs, count, wide = keep[0].shape
-    shape = jax.ShapeDtypeStruct((slabs, count, table[0].shape[1]), jnp.float32)
+    count, wide = keep[0].shape
+    shape = jax.ShapeDtypeStruct((count, table[0].shape[1]), jnp.float32)
     ins = (*keep, *near, *table)
     return pl.pallas_call(
         functools.partial(inverse_y_partial_kernel, len(keep)),
         in_specs=pieces_spec(len(ins)),
         out_specs=pieces_spec(len(keep)),
         out_shape=[shape] * len(keep),
-        cost_estimate=cost(12 * len(keep) * slabs * count * wide * shape.shape[2], (*ins, shape)),
+        cost_estimate=cost(12 * len(keep) * (count + 8) * wide * shape.shape[1], (*ins, shape, shape)),
         compiler_params=pltpu.CompilerParams(vmem_limit_bytes=LIMIT),
         name="inverse_y_partial",
     )(*ins)
@@ -507,21 +512,18 @@
 
 def combine(mine, near, scale):
     total = (mine + near) * scale
-    count = total.shape[1] - 8
-    low, high = total[0], total[1]
+    count = (total.shape[0] - 8) // 2
+    low, high = total[:count], total[count : 2 * count]
     odd = lax.axis_index("gz") % 2 == 1
-    first = jnp.where(odd, low[:count], high[:count])
-    second = jnp.where(odd, high[:count], low[:count])
-    return first, second, total[:, count:]
-
-
-def slopes_kernel(at_ref, first_ref, second_ref, rows_ref, gx_ref, gy_ref):
+    return jnp.where(odd, low, high), jnp.where(odd, high, low), total[2 * count :]
+
+
+def slopes_kernel(at_ref, first_ref, second_ref, outer_ref, gx_ref, gy_ref):
     parts = lax.axis_size("gx")
     odd = at_ref[2] % 2 == 1
-    first, second = first_ref[...], second_ref[...]
+    first, second, outer = first_ref[...], second_ref[...], outer_ref[...]
     for z, main in enumerate((jnp.where(odd, first, second), jnp.where(odd, second, first))):
-        total = jnp.concatenate([main, rows_ref[z]], axis=0)
-        differences(total, at_ref[0], parts, gx_ref.at[z], gy_ref.at[z])
+        differences(main, outer[2 * z :], at_ref[0], parts, gx_ref.at[z], gy_ref.at[z])
 
 
 def slopes(at, first, second, rows):
@@ -565,7 +567,7 @@
 def sums_y(rows, column, cut):
     near = rows[1::2]
     if cut:
-        near = [r[z] for r in near for z in range(r.shape[0])]
+        near = [part for r in near for part in (r[:68], r[68:])]
     near = [swap(r, "gx", 1) for r in near]
     return inverse_y_partial(rows[0::2], near, column)
 

time: 71.5 us -> 70.8 us (level)
  no operation moved by 1% of the time
where the time goes in v6:
time: 70.8 us; the launch traced here: 70.1 us
  starting transfers between devices  35.2 us (50%)
  waiting for transfers between devices  21.9 us (31%)
  Pallas kernels  9.53 us (13%)
  local copies, waits for them, and re-layouts  1.85 us (3%)
  other arithmetic  0.84 us (1%)
  between operations  0.79 us (1%)
    ppermute x29, starting transfers between devices, swap(): lax.ppermute(value, axis, [(s, s ^ mask) for s in range(lax.axis_size(axi...  32 us
    ppermute x29, waiting for transfers between devices, swap(): lax.ppermute(value, axis, [(s, s ^ mask) for s in range(lax.axis_size(axi...  19.4 us
    ppermute x1, starting transfers between devices, slope_z_pairs(): far = lax.ppermute(second, 'gz', pairs + [(b, a) for a, b in pairs])  3.2 us
    pallas_call x2, Pallas kernels, forward_half(): pl.pallas_call(forward_half_kernel, in_specs=pieces_spec(len(ins)), out_s...  2.7 us
    ppermute x1, waiting for transfers between devices, slope_z_pairs(): far = lax.ppermute(second, 'gz', pairs + [(b, a) for a, b in pairs])  2.47 us
    pallas_call x1, Pallas kernels, middle_half(): pl.pallas_call(middle_half_kernel, in_specs=[pl.BlockSpec(memory_space=SM...  2.43 us
    unnamed x8, local copies, waits for them, and re-layouts  1.82 us
  transfers between devices with their start and end apart: 30, of which 15 were waited for; matrix products, arithmetic and copies ran while one was open for 0% of the time, Pallas kernels for 10%

profile of v6, /device:TPU:8, one launch (start us, length us, event | category | flops | bytes accessed | tf_op | source)
XLA Modules:
  0.0 70.1 jit_solution(6449086768512888936)
XLA Ops:
  0.6 2.7 %collective-permute-start.6 = (f32[2,64,256]{2,1,0:T(8,128)}, f32[2,64,256]{2,1,0:T(8,128)S(1)}, u32[]{:S(2)}, u32[]{:S(2)}) collective-permute-start(f32[2,64,256]{2,1,0:T(8,128)} %density_ref.1), channel_id=1, source_target_pairs={{0,16},{4,20},{8,24},{12,28},{16,0},{20,4},{24,8},{28,12},{1,17},{... | collective-permute-start | bytes 393224 | tf_op jit(solution)/shard_map/ppermute | solution.py:556
  3.3 1.5 %collective-permute-start.1 = (f32[2,64,256]{2,1,0:T(8,128)}, f32[2,64,256]{2,1,0:T(8,128)S(1)}, u32[]{:S(2)}, u32[]{:S(2)}) collective-permute-start(f32[2,64,256]{2,1,0:T(8,128)} %density_ref.1), channel_id=1, source_target_pairs={{0,2},{1,3},{2,0},{3,1},{4,6},{5,7},{6,4},{7,5},{8,10},{9,11},{10,... | collective-permute-start | bytes 393224 | tf_op jit(solution)/shard_map/ppermute | solution.py:556
  9.1 1.5 %collective-permute-start.8 = (f32[2,64,256]{2,1,0:T(8,128)S(1)}, f32[2,64,256]{2,1,0:T(8,128)S(1)}, u32[]{:S(2)}, u32[]{:S(2)}) collective-permute-start(f32[2,64,256]{2,1,0:T(8,128)S(1)} %collective-permute-done.6.refs_0_), channel_id=1, source_target_pairs={{0,2},{1,3},{2,0},{3,1},{4,6},{5,7},{6,4},{7,5},{8,10},{9,11},{10,... | collective-permute-start | bytes 393224 | tf_op jit(solution)/shard_map/ppermute | solution.py:556
  11.8 1.3 %forward_half.2 = (f32[2,64,256]{2,1,0:T(8,128)S(1)}, f32[2,64,256]{2,1,0:T(8,128)S(1)}, f32[2,64,256]{2,1,0:T(8,128)S(1)}, f32[2,64,256]{2,1,0:T(8,128)S(1)}) custom-call(f32[2,64,256]{2,1,0:T(8,128)S(1)} %get-tuple-element.44.refs_0_, f32[2,64,256]{2,1,0:T(8,128)S(1)} %collective-permute-done.refs_1_, f32[2,64,256]{2,1,0:T(8,128)S(1)} %collective-permute-done.1.refs_2_, ...), custom_call_target="tpu_custom_call" | custom-call | flops 603979776 | bytes 1835008 | tf_op jit(solution)/shard_map/forward_half/pallas_call | solution.py:399
  13.2 1.6 %collective-permute-start.3 = (f32[2,64,256]{2,1,0:T(8,128)S(1)}, f32[2,64,256]{2,1,0:T(8,128)S(1)}, u32[]{:S(2)}, u32[]{:S(2)}) collective-permute-start(f32[2,64,256]{2,1,0:T(8,128)S(1)} %get-tuple-element.50), channel_id=1, source_target_pairs={{0,4},{4,0},{8,12},{12,8},{16,20},{20,16},{24,28},{28,24},{1,5},{5... | collective-permute-start | bytes 393224 | tf_op jit(solution)/shard_map/ppermute | solution.py:556
  15.2 1.5 %collective-permute-start.5 = (f32[2,64,256]{2,1,0:T(8,128)S(1)}, f32[2,64,256]{2,1,0:T(8,128)S(1)}, u32[]{:S(2)}, u32[]{:S(2)}) collective-permute-start(f32[2,64,256]{2,1,0:T(8,128)S(1)} %get-tuple-element.52), channel_id=1, source_target_pairs={{0,12},{4,8},{8,4},{12,0},{16,28},{20,24},{24,20},{28,16},{1,13},{... | collective-permute-start | bytes 393224 | tf_op jit(solution)/shard_map/ppermute | solution.py:556
  17.5 1.3 %forward_half.3 = (f32[2,64,256]{2,1,0:T(8,128)S(1)}, f32[2,64,256]{2,1,0:T(8,128)S(1)}, f32[2,64,256]{2,1,0:T(8,128)S(1)}, f32[2,64,256]{2,1,0:T(8,128)S(1)}) custom-call(f32[2,64,256]{2,1,0:T(8,128)S(1)} %collective-permute-done.6.refs_0_, f32[2,64,256]{2,1,0:T(8,128)S(1)} %collective-permute-done.7.refs_1_, ...), custom_call_target="tpu_custom_call" | custom-call | flops 603979776 | bytes 1835008 | tf_op jit(solution)/shard_map/forward_half/pallas_call | solution.py:399
  18.8 1.6 %collective-permute-start.10 = (f32[2,64,256]{2,1,0:T(8,128)S(1)}, f32[2,64,256]{2,1,0:T(8,128)S(1)}, u32[]{:S(2)}, u32[]{:S(2)}) collective-permute-start(f32[2,64,256]{2,1,0:T(8,128)S(1)} %get-tuple-element.55), channel_id=1, source_target_pairs={{0,4},{4,0},{8,12},{12,8},{16,20},{20,16},{24,28},{28,24},{1,5},{5... | collective-permute-start | bytes 393224 | tf_op jit(solution)/shard_map/ppermute | solution.py:556
  22.9 3.2 %collective-permute-done.10.refs_5_ = f32[2,64,256]{2,1,0:T(8,128)S(1)} collective-permute-done((f32[2,64,256]{2,1,0:T(8,128)S(1)}, f32[2,64,256]{2,1,0:T(8,128)S(1)}, u32[]{:S(2)}, u32[]{:S(2)}) %collective-permute-start.10) | collective-permute-done | bytes 131104 | tf_op jit(solution)/shard_map/ppermute | solution.py:556
  26.8 2.0 %collective-permute-done.12.refs_7_ = f32[2,64,256]{2,1,0:T(8,128)S(1)} collective-permute-done((f32[2,64,256]{2,1,0:T(8,128)S(1)}, f32[2,64,256]{2,1,0:T(8,128)S(1)}, u32[]{:S(2)}, u32[]{:S(2)}) %collective-permute-start.12) | collective-permute-done | bytes 131104 | tf_op jit(solution)/shard_map/ppermute | solution.py:556
  28.8 2.4 %middle_half.1 = (f32[2,64,256]{2,1,0:T(8,128)S(1)}, f32[2,64,256]{2,1,0:T(8,128)S(1)}, f32[2,64,256]{2,1,0:T(8,128)S(1)}, f32[2,64,256]{2,1,0:T(8,128)S(1)}, f3...) custom-call(s32[3]{0:T(128)S(1)} %pad_add_fusion.at_ref, ...), custom_call_target="tpu_custom_call" | custom-call | bytes 6291456 | tf_op jit(solution)/shard_map/middle_half/pallas_call | solution.py:440
  31.2 1.6 %collective-permute-start.16 = (f32[2,64,256]{2,1,0:T(8,128)S(1)}, f32[2,64,256]{2,1,0:T(8,128)S(1)}, u32[]{:S(2)}, u32[]{:S(2)}) collective-permute-start(f32[2,64,256]{2,1,0:T(8,128)S(1)} %get-tuple-element.66), channel_id=1, source_target_pairs={{0,4},{4,0},{8,12},{12,8},{16,20},{20,16},{24,28},{28,24},{1,5},{5... | collective-permute-start | bytes 393224 | tf_op jit(solution)/shard_map/ppermute | solution.py:556
  34.8 1.5 %collective-permute-start.13 = (f32[2,64,256]{2,1,0:T(8,128)S(1)}, f32[2,64,256]{2,1,0:T(8,128)S(1)}, u32[]{:S(2)}, u32[]{:S(2)}) collective-permute-start(f32[2,64,256]{2,1,0:T(8,128)S(1)} %get-tuple-element.59), channel_id=1, source_target_pairs={{0,4},{4,0},{8,12},{12,8},{16,20},{20,16},{24,28},{28,24},{1,5},{5... | collective-permute-start | bytes 393224 | tf_op jit(solution)/shard_map/ppermute | solution.py:556
  37.5 2.4 %collective-permute-start.15 = (f32[2,64,256]{2,1,0:T(8,128)S(1)}, f32[2,64,256]{2,1,0:T(8,128)S(1)}, u32[]{:S(2)}, u32[]{:S(2)}) collective-permute-start(f32[2,64,256]{2,1,0:T(8,128)S(1)} %get-tuple-element.61), channel_id=1, source_target_pairs={{0,12},{4,8},{8,4},{12,0},{16,28},{20,24},{24,20},{28,16},{1,13},{... | collective-permute-start | bytes 393224 | tf_op jit(solution)/shard_map/ppermute | solution.py:556
  39.9 2.0 %collective-permute-done.18.refs_3_ = f32[2,64,256]{2,1,0:T(8,128)S(1)} collective-permute-done((f32[2,64,256]{2,1,0:T(8,128)S(1)}, f32[2,64,256]{2,1,0:T(8,128)S(1)}, u32[]{:S(2)}, u32[]{:S(2)}) %collective-permute-start.18) | collective-permute-done | bytes 131104 | tf_op jit(solution)/shard_map/ppermute | solution.py:556
  45.7 1.5 %collective-permute-start.23 = (f32[136,256]{1,0:T(8,128)S(1)}, f32[136,256]{1,0:T(8,128)S(1)}, u32[]{:S(2)}, u32[]{:S(2)}) collective-permute-start(f32[136,256]{1,0:T(8,128)S(1)} %get-tuple-element.76), channel_id=1, source_target_pairs={{0,2},{1,3},{2,0},{3,1},{4,6},{5,7},{6,4},{7,5},{8,10},{9,11},{10,... | collective-permute-start | bytes 417800 | tf_op jit(solution)/shard_map/ppermute | solution.py:556
  48.5 3.2 %collective-permute-done.23 = f32[136,256]{1,0:T(8,128)S(1)} collective-permute-done((f32[136,256]{1,0:T(8,128)S(1)}, f32[136,256]{1,0:T(8,128)S(1)}, u32[]{:S(2)}, u32[]{:S(2)}) %collective-permute-start.23) | collective-permute-done | bytes 139296 | tf_op jit(solution)/shard_map/ppermute | solution.py:556
  51.7 3.5 %collective-permute-start.26 = (f32[136,256]{1,0:T(8,128)S(1)}, f32[136,256]{1,0:T(8,128)S(1)}, u32[]{:S(2)}, u32[]{:S(2)}) collective-permute-start(f32[136,256]{1,0:T(8,128)S(1)} %add.20), channel_id=1, source_target_pairs={{0,16},{4,20},{8,24},{12,28},{16,0},{20,4},{24,8},{28,12},{1,17},{... | collective-permute-start | bytes 417800 | tf_op jit(solution)/shard_map/ppermute | solution.py:556
  55.6 1.6 %collective-permute-start.27 = (f32[136,256]{1,0:T(8,128)S(1)}, f32[136,256]{1,0:T(8,128)S(1)}, u32[]{:S(2)}, u32[]{:S(2)}) collective-permute-start(f32[136,256]{1,0:T(8,128)S(1)} %get-tuple-element.82), channel_id=1, source_target_pairs={{0,2},{1,3},{2,0},{3,1},{4,6},{5,7},{6,4},{7,5},{8,10},{9,11},{10,... | collective-permute-start | bytes 417800 | tf_op jit(solution)/shard_map/ppermute | solution.py:556
  57.2 3.2 %collective-permute-done.26 = f32[136,256]{1,0:T(8,128)S(1)} collective-permute-done((f32[136,256]{1,0:T(8,128)S(1)}, f32[136,256]{1,0:T(8,128)S(1)}, u32[]{:S(2)}, u32[]{:S(2)}) %collective-permute-start.26) | collective-permute-done | bytes 139296 | tf_op jit(solution)/shard_map/ppermute | solution.py:556
  60.8 1.6 %collective-permute-start.28 = (f32[64,256]{1,0:T(8,128)S(1)}, f32[64,256]{1,0:T(8,128)S(1)}, u32[]{:S(2)}, u32[]{:S(2)}) collective-permute-start(f32[64,256]{1,0:T(8,128)S(1)} %get-tuple-element.88.first_ref), channel_id=1, source_target_pairs={{0,4},{4,0},{8,12},{12,8},{16,20},{20,16},{24,28},{28,24},{1,5},{5... | collective-permute-start | bytes 196616 | tf_op jit(solution)/shard_map/ppermute | solution.py:556
  62.4 3.2 %collective-permute-start.29 = (f32[64,256]{1,0:T(8,128)S(1)}, f32[64,256]{1,0:T(8,128)S(1)}, u32[]{:S(2)}, u32[]{:S(2)}) collective-permute-start(f32[64,256]{1,0:T(8,128)S(1)} %get-tuple-element.87.second_ref), channel_id=1, source_target_pairs={{4,8},{12,16},{20,24},{8,4},{16,12},{24,20},{5,9},{13,17},{21,25},... | collective-permute-start | bytes 196616 | tf_op jit(solution)/shard_map/ppermute | solution.py:547
  65.6 1.3 %slopes.1 = (f32[2,64,256]{2,1,0:T(8,128)}, f32[2,64,256]{2,1,0:T(8,128)}) custom-call(s32[3]{0:T(128)S(1)} %pad_add_fusion.at_ref, f32[64,256]{1,0:T(8,128)S(1)} %get-tuple-element.88.first_ref, f32[64,256]{1,0:T(8,128)S(1)} %get-tuple-element.87.second_ref, f32[8,256]{1,0:T(8,128)S(1)} %slice.30.outer_ref), custom_call_target="tpu_custom_call" | custom-call | bytes 401408 | tf_op jit(solution)/shard_map/slopes/pallas_call | solution.py:531
  66.9 2.5 %collective-permute-done.29 = f32[64,256]{1,0:T(8,128)S(1)} collective-permute-done((f32[64,256]{1,0:T(8,128)S(1)}, f32[64,256]{1,0:T(8,128)S(1)}, u32[]{:S(2)}, u32[]{:S(2)}) %collective-permute-start.29) | collective-permute-done | bytes 65568 | tf_op jit(solution)/shard_map/ppermute | solution.py:547
  (63 shorter events, 19.6 us)
Async XLA Ops:
  0.6 8.4 %collective-permute-start.6 = (f32[2,64,256]{2,1,0:T(8,128)}, f32[2,64,256]{2,1,0:T(8,128)S(1)}, u32[]{:S(2)}, u32[]{:S(2)}) collective-permute-start(f32[2,64,256]{2,1,0:T(8,128)} %density_ref.1), channel_id=1, source_target_pairs={{0,16},{4,20},{8,24},{12,28},{16,0},{20,4},{24,8},{28,12},{1,17},{... | collective-permute-start | bytes 393224 | tf_op jit(solution)/shard_map/ppermute | solution.py:556
  3.3 7.3 %collective-permute-start = (f32[2,64,256]{2,1,0:T(8,128)}, f32[2,64,256]{2,1,0:T(8,128)S(1)}, u32[]{:S(2)}, u32[]{:S(2)}) collective-permute-start(f32[2,64,256]{2,1,0:T(8,128)} %density_ref.1), channel_id=1, source_target_pairs={{0,1},{1,0},{2,3},{3,2},{4,5},{5,4},{6,7},{7,6},{8,9},{9,8},{10,11... | collective-permute-start | bytes 393224 | tf_op jit(solution)/shard_map/ppermute | solution.py:556
  3.3 7.6 %collective-permute-start.1 = (f32[2,64,256]{2,1,0:T(8,128)}, f32[2,64,256]{2,1,0:T(8,128)S(1)}, u32[]{:S(2)}, u32[]{:S(2)}) collective-permute-start(f32[2,64,256]{2,1,0:T(8,128)} %density_ref.1), channel_id=1, source_target_pairs={{0,2},{1,3},{2,0},{3,1},{4,6},{5,7},{6,4},{7,5},{8,10},{9,11},{10,... | collective-permute-start | bytes 393224 | tf_op jit(solution)/shard_map/ppermute | solution.py:556
  4.8 7.0 %collective-permute-start.2 = (f32[2,64,256]{2,1,0:T(8,128)}, f32[2,64,256]{2,1,0:T(8,128)S(1)}, u32[]{:S(2)}, u32[]{:S(2)}) collective-permute-start(f32[2,64,256]{2,1,0:T(8,128)} %density_ref.1), channel_id=1, source_target_pairs={{0,3},{1,2},{2,1},{3,0},{4,7},{5,6},{6,5},{7,4},{8,11},{9,10},{10,... | collective-permute-start | bytes 393224 | tf_op jit(solution)/shard_map/ppermute | solution.py:556
  9.1 6.2 %collective-permute-start.7 = (f32[2,64,256]{2,1,0:T(8,128)S(1)}, f32[2,64,256]{2,1,0:T(8,128)S(1)}, u32[]{:S(2)}, u32[]{:S(2)}) collective-permute-start(f32[2,64,256]{2,1,0:T(8,128)S(1)} %collective-permute-done.6.refs_0_), channel_id=1, source_target_pairs={{0,1},{1,0},{2,3},{3,2},{4,5},{5,4},{6,7},{7,6},{8,9},{9,8},{10,11... | collective-permute-start | bytes 393224 | tf_op jit(solution)/shard_map/ppermute | solution.py:556
  9.1 7.7 %collective-permute-start.8 = (f32[2,64,256]{2,1,0:T(8,128)S(1)}, f32[2,64,256]{2,1,0:T(8,128)S(1)}, u32[]{:S(2)}, u32[]{:S(2)}) collective-permute-start(f32[2,64,256]{2,1,0:T(8,128)S(1)} %collective-permute-done.6.refs_0_), channel_id=1, source_target_pairs={{0,2},{1,3},{2,0},{3,1},{4,6},{5,7},{6,4},{7,5},{8,10},{9,11},{10,... | collective-permute-start | bytes 393224 | tf_op jit(solution)/shard_map/ppermute | solution.py:556
  10.6 6.9 %collective-permute-start.9 = (f32[2,64,256]{2,1,0:T(8,128)S(1)}, f32[2,64,256]{2,1,0:T(8,128)S(1)}, u32[]{:S(2)}, u32[]{:S(2)}) collective-permute-start(f32[2,64,256]{2,1,0:T(8,128)S(1)} %collective-permute-done.6.refs_0_), channel_id=1, source_target_pairs={{0,3},{1,2},{2,1},{3,0},{4,7},{5,6},{6,5},{7,4},{8,11},{9,10},{10,... | collective-permute-start | bytes 393224 | tf_op jit(solution)/shard_map/ppermute | solution.py:556
  13.2 8.4 %collective-permute-start.3 = (f32[2,64,256]{2,1,0:T(8,128)S(1)}, f32[2,64,256]{2,1,0:T(8,128)S(1)}, u32[]{:S(2)}, u32[]{:S(2)}) collective-permute-start(f32[2,64,256]{2,1,0:T(8,128)S(1)} %get-tuple-element.50), channel_id=1, source_target_pairs={{0,4},{4,0},{8,12},{12,8},{16,20},{20,16},{24,28},{28,24},{1,5},{5... | collective-permute-start | bytes 393224 | tf_op jit(solution)/shard_map/ppermute | solution.py:556
  14.8 7.6 %collective-permute-start.4 = (f32[2,64,256]{2,1,0:T(8,128)S(1)}, f32[2,64,256]{2,1,0:T(8,128)S(1)}, u32[]{:S(2)}, u32[]{:S(2)}) collective-permute-start(f32[2,64,256]{2,1,0:T(8,128)S(1)} %get-tuple-element.51), channel_id=1, source_target_pairs={{0,8},{4,12},{8,0},{12,4},{16,24},{20,28},{24,16},{28,20},{1,9},{5... | collective-permute-start | bytes 393224 | tf_op jit(solution)/shard_map/ppermute | solution.py:556
  15.2 7.7 %collective-permute-start.5 = (f32[2,64,256]{2,1,0:T(8,128)S(1)}, f32[2,64,256]{2,1,0:T(8,128)S(1)}, u32[]{:S(2)}, u32[]{:S(2)}) collective-permute-start(f32[2,64,256]{2,1,0:T(8,128)S(1)} %get-tuple-element.52), channel_id=1, source_target_pairs={{0,12},{4,8},{8,4},{12,0},{16,28},{20,24},{24,20},{28,16},{1,13},{... | collective-permute-start | bytes 393224 | tf_op jit(solution)/shard_map/ppermute | solution.py:556
  18.8 7.3 %collective-permute-start.10 = (f32[2,64,256]{2,1,0:T(8,128)S(1)}, f32[2,64,256]{2,1,0:T(8,128)S(1)}, u32[]{:S(2)}, u32[]{:S(2)}) collective-permute-start(f32[2,64,256]{2,1,0:T(8,128)S(1)} %get-tuple-element.55), channel_id=1, source_target_pairs={{0,4},{4,0},{8,12},{12,8},{16,20},{20,16},{24,28},{28,24},{1,5},{5... | collective-permute-start | bytes 393224 | tf_op jit(solution)/shard_map/ppermute | solution.py:556
  20.4 6.3 %collective-permute-start.11 = (f32[2,64,256]{2,1,0:T(8,128)S(1)}, f32[2,64,256]{2,1,0:T(8,128)S(1)}, u32[]{:S(2)}, u32[]{:S(2)}) collective-permute-start(f32[2,64,256]{2,1,0:T(8,128)S(1)} %get-tuple-element.56), channel_id=1, source_target_pairs={{0,8},{4,12},{8,0},{12,4},{16,24},{20,28},{24,16},{28,20},{1,9},{5... | collective-permute-start | bytes 393224 | tf_op jit(solution)/shard_map/ppermute | solution.py:556
  21.6 7.2 %collective-permute-start.12 = (f32[2,64,256]{2,1,0:T(8,128)S(1)}, f32[2,64,256]{2,1,0:T(8,128)S(1)}, u32[]{:S(2)}, u32[]{:S(2)}) collective-permute-start(f32[2,64,256]{2,1,0:T(8,128)S(1)} %get-tuple-element.57), channel_id=1, source_target_pairs={{0,12},{4,8},{8,4},{12,0},{16,28},{20,24},{24,20},{28,16},{1,13},{... | collective-permute-start | bytes 393224 | tf_op jit(solution)/shard_map/ppermute | solution.py:556
  31.2 6.3 %collective-permute-start.16 = (f32[2,64,256]{2,1,0:T(8,128)S(1)}, f32[2,64,256]{2,1,0:T(8,128)S(1)}, u32[]{:S(2)}, u32[]{:S(2)}) collective-permute-start(f32[2,64,256]{2,1,0:T(8,128)S(1)} %get-tuple-element.66), channel_id=1, source_target_pairs={{0,4},{4,0},{8,12},{12,8},{16,20},{20,16},{24,28},{28,24},{1,5},{5... | collective-permute-start | bytes 393224 | tf_op jit(solution)/shard_map/ppermute | solution.py:556
  32.8 7.1 %collective-permute-start.17 = (f32[2,64,256]{2,1,0:T(8,128)S(1)}, f32[2,64,256]{2,1,0:T(8,128)S(1)}, u32[]{:S(2)}, u32[]{:S(2)}) collective-permute-start(f32[2,64,256]{2,1,0:T(8,128)S(1)} %get-tuple-element.67), channel_id=1, source_target_pairs={{0,8},{4,12},{8,0},{12,4},{16,24},{20,28},{24,16},{28,20},{1,9},{5... | collective-permute-start | bytes 393224 | tf_op jit(solution)/shard_map/ppermute | solution.py:556
  34.0 7.9 %collective-permute-start.18 = (f32[2,64,256]{2,1,0:T(8,128)S(1)}, f32[2,64,256]{2,1,0:T(8,128)S(1)}, u32[]{:S(2)}, u32[]{:S(2)}) collective-permute-start(f32[2,64,256]{2,1,0:T(8,128)S(1)} %get-tuple-element.68), channel_id=1, source_target_pairs={{0,12},{4,8},{8,4},{12,0},{16,28},{20,24},{24,20},{28,16},{1,13},{... | collective-permute-start | bytes 393224 | tf_op jit(solution)/shard_map/ppermute | solution.py:556
  34.8 12.5 %collective-permute-start.13 = (f32[2,64,256]{2,1,0:T(8,128)S(1)}, f32[2,64,256]{2,1,0:T(8,128)S(1)}, u32[]{:S(2)}, u32[]{:S(2)}) collective-permute-start(f32[2,64,256]{2,1,0:T(8,128)S(1)} %get-tuple-element.59), channel_id=1, source_target_pairs={{0,4},{4,0},{8,12},{12,8},{16,20},{20,16},{24,28},{28,24},{1,5},{5... | collective-permute-start | bytes 393224 | tf_op jit(solution)/shard_map/ppermute | solution.py:556
  36.3 11.0 %collective-permute-start.14 = (f32[2,64,256]{2,1,0:T(8,128)S(1)}, f32[2,64,256]{2,1,0:T(8,128)S(1)}, u32[]{:S(2)}, u32[]{:S(2)}) collective-permute-start(f32[2,64,256]{2,1,0:T(8,128)S(1)} %get-tuple-element.60), channel_id=1, source_target_pairs={{0,8},{4,12},{8,0},{12,4},{16,24},{20,28},{24,16},{28,20},{1,9},{5... | collective-permute-start | bytes 393224 | tf_op jit(solution)/shard_map/ppermute | solution.py:556
  37.5 9.8 %collective-permute-start.15 = (f32[2,64,256]{2,1,0:T(8,128)S(1)}, f32[2,64,256]{2,1,0:T(8,128)S(1)}, u32[]{:S(2)}, u32[]{:S(2)}) collective-permute-start(f32[2,64,256]{2,1,0:T(8,128)S(1)} %get-tuple-element.61), channel_id=1, source_target_pairs={{0,12},{4,8},{8,4},{12,0},{16,28},{20,24},{24,20},{28,16},{1,13},{... | collective-permute-start | bytes 393224 | tf_op jit(solution)/shard_map/ppermute | solution.py:556
  47.9 7.3 %collective-permute-start.24 = (f32[136,256]{1,0:T(8,128)S(1)}, f32[136,256]{1,0:T(8,128)S(1)}, u32[]{:S(2)}, u32[]{:S(2)}) collective-permute-start(f32[136,256]{1,0:T(8,128)S(1)} %get-tuple-element.79), channel_id=1, source_target_pairs={{0,1},{1,0},{2,3},{3,2},{4,5},{5,4},{6,7},{7,6},{8,9},{9,8},{10,11... | collective-permute-start | bytes 417800 | tf_op jit(solution)/shard_map/ppermute | solution.py:556
  48.0 7.2 %collective-permute-start.25 = (f32[136,256]{1,0:T(8,128)S(1)}, f32[136,256]{1,0:T(8,128)S(1)}, u32[]{:S(2)}, u32[]{:S(2)}) collective-permute-start(f32[136,256]{1,0:T(8,128)S(1)} %get-tuple-element.80), channel_id=1, source_target_pairs={{0,1},{1,0},{2,3},{3,2},{4,5},{5,4},{6,7},{7,6},{8,9},{9,8},{10,11... | collective-permute-start | bytes 417800 | tf_op jit(solution)/shard_map/ppermute | solution.py:556
  51.7 8.6 %collective-permute-start.26 = (f32[136,256]{1,0:T(8,128)S(1)}, f32[136,256]{1,0:T(8,128)S(1)}, u32[]{:S(2)}, u32[]{:S(2)}) collective-permute-start(f32[136,256]{1,0:T(8,128)S(1)} %add.20), channel_id=1, source_target_pairs={{0,16},{4,20},{8,24},{12,28},{16,0},{20,4},{24,8},{28,12},{1,17},{... | collective-permute-start | bytes 417800 | tf_op jit(solution)/shard_map/ppermute | solution.py:556
  60.8 6.2 %collective-permute-start.28 = (f32[64,256]{1,0:T(8,128)S(1)}, f32[64,256]{1,0:T(8,128)S(1)}, u32[]{:S(2)}, u32[]{:S(2)}) collective-permute-start(f32[64,256]{1,0:T(8,128)S(1)} %get-tuple-element.88.first_ref), channel_id=1, source_target_pairs={{0,4},{4,0},{8,12},{12,8},{16,20},{20,16},{24,28},{28,24},{1,5},{5... | collective-permute-start | bytes 196616 | tf_op jit(solution)/shard_map/ppermute | solution.py:556
  62.4 7.0 %collective-permute-start.29 = (f32[64,256]{1,0:T(8,128)S(1)}, f32[64,256]{1,0:T(8,128)S(1)}, u32[]{:S(2)}, u32[]{:S(2)}) collective-permute-start(f32[64,256]{1,0:T(8,128)S(1)} %get-tuple-element.87.second_ref), channel_id=1, source_target_pairs={{4,8},{12,16},{20,24},{8,4},{16,12},{24,20},{5,9},{13,17},{21,25},... | collective-permute-start | bytes 196616 | tf_op jit(solution)/shard_map/ppermute | solution.py:547
  (10 other events, 52.1 us)

commit v7 on v6

--- a/solution.py
+++ b/solution.py
@@ -377,10 +377,12 @@
     table_y = (yh_ref[...], yl_ref[...])
     table_x = (th_ref[...], tl_ref[...])
     kx = outs[0].shape[1]
-    for z in range(rows[0].shape[0]):
-        both = jnp.concatenate([r[z] for r in rows], axis=0)
-        spec = product3(split(both), table_y, ((1,), (1,)))
-        res = product3(table_x, turned_halves(spec), ((1,), (0,)))
+    slabs = rows[0].shape[0]
+    both = jnp.concatenate([r[z] for z in range(slabs) for r in rows], axis=0)
+    spec = product3(split(both), table_y, ((1,), (1,)))
+    width = spec.shape[0] // slabs
+    for z in range(slabs):
+        res = product3(table_x, turned_halves(spec[z * width : (z + 1) * width]), ((1,), (0,)))
         for k, ref in enumerate(outs):
             ref[z] = res[k * kx : (k + 1) * kx]
 

time: 70.8 us -> 70.8 us (level)
  no operation moved by 1% of the time
where the time goes in v7:
time: 70.8 us; the launch traced here: 70 us
  starting transfers between devices  35.2 us (50%)
  waiting for transfers between devices  22 us (31%)
  Pallas kernels  9.4 us (13%)
  local copies, waits for them, and re-layouts  1.85 us (3%)
  other arithmetic  0.84 us (1%)
  between operations  0.79 us (1%)
    ppermute x29, starting transfers between devices, swap(): lax.ppermute(value, axis, [(s, s ^ mask) for s in range(lax.axis_size(axi...  32 us
    ppermute x29, waiting for transfers between devices, swap(): lax.ppermute(value, axis, [(s, s ^ mask) for s in range(lax.axis_size(axi...  19.5 us
    ppermute x1, starting transfers between devices, slope_z_pairs(): far = lax.ppermute(second, 'gz', pairs + [(b, a) for a, b in pairs])  3.19 us
    pallas_call x2, Pallas kernels, forward_half(): pl.pallas_call(forward_half_kernel, in_specs=pieces_spec(len(ins)), out_s...  2.57 us
    ppermute x1, waiting for transfers between devices, slope_z_pairs(): far = lax.ppermute(second, 'gz', pairs + [(b, a) for a, b in pairs])  2.47 us
    pallas_call x1, Pallas kernels, middle_half(): pl.pallas_call(middle_half_kernel, in_specs=[pl.BlockSpec(memory_space=SM...  2.43 us
    unnamed x8, local copies, waits for them, and re-layouts  1.82 us
  transfers between devices with their start and end apart: 30, of which 15 were waited for; matrix products, arithmetic and copies ran while one was open for 0% of the time, Pallas kernels for 10%

profile of v7, /device:TPU:8, one launch (start us, length us, event | category | flops | bytes accessed | tf_op | source)
XLA Modules:
  0.0 70.0 jit_solution(9835834638798720381)
XLA Ops:
  0.6 2.7 %collective-permute-start.6 = (f32[2,64,256]{2,1,0:T(8,128)}, f32[2,64,256]{2,1,0:T(8,128)S(1)}, u32[]{:S(2)}, u32[]{:S(2)}) collective-permute-start(f32[2,64,256]{2,1,0:T(8,128)} %density_ref.1), channel_id=1, source_target_pairs={{0,16},{4,20},{8,24},{12,28},{16,0},{20,4},{24,8},{28,12},{1,17},{... | collective-permute-start | bytes 393224 | tf_op jit(solution)/shard_map/ppermute | solution.py:558
  3.3 1.5 %collective-permute-start.1 = (f32[2,64,256]{2,1,0:T(8,128)}, f32[2,64,256]{2,1,0:T(8,128)S(1)}, u32[]{:S(2)}, u32[]{:S(2)}) collective-permute-start(f32[2,64,256]{2,1,0:T(8,128)} %density_ref.1), channel_id=1, source_target_pairs={{0,2},{1,3},{2,0},{3,1},{4,6},{5,7},{6,4},{7,5},{8,10},{9,11},{10,... | collective-permute-start | bytes 393224 | tf_op jit(solution)/shard_map/ppermute | solution.py:558
  9.1 1.5 %collective-permute-start.8 = (f32[2,64,256]{2,1,0:T(8,128)S(1)}, f32[2,64,256]{2,1,0:T(8,128)S(1)}, u32[]{:S(2)}, u32[]{:S(2)}) collective-permute-start(f32[2,64,256]{2,1,0:T(8,128)S(1)} %collective-permute-done.6.refs_0_), channel_id=1, source_target_pairs={{0,2},{1,3},{2,0},{3,1},{4,6},{5,7},{6,4},{7,5},{8,10},{9,11},{10,... | collective-permute-start | bytes 393224 | tf_op jit(solution)/shard_map/ppermute | solution.py:558
  11.8 1.3 %forward_half.2 = (f32[2,64,256]{2,1,0:T(8,128)S(1)}, f32[2,64,256]{2,1,0:T(8,128)S(1)}, f32[2,64,256]{2,1,0:T(8,128)S(1)}, f32[2,64,256]{2,1,0:T(8,128)S(1)}) custom-call(f32[2,64,256]{2,1,0:T(8,128)S(1)} %get-tuple-element.44.refs_0_, f32[2,64,256]{2,1,0:T(8,128)S(1)} %collective-permute-done.refs_1_, f32[2,64,256]{2,1,0:T(8,128)S(1)} %collective-permute-done.1.refs_2_, ...), custom_call_target="tpu_custom_call" | custom-call | flops 603979776 | bytes 1835008 | tf_op jit(solution)/shard_map/forward_half/pallas_call | solution.py:401
  13.1 1.6 %collective-permute-start.3 = (f32[2,64,256]{2,1,0:T(8,128)S(1)}, f32[2,64,256]{2,1,0:T(8,128)S(1)}, u32[]{:S(2)}, u32[]{:S(2)}) collective-permute-start(f32[2,64,256]{2,1,0:T(8,128)S(1)} %get-tuple-element.50), channel_id=1, source_target_pairs={{0,4},{4,0},{8,12},{12,8},{16,20},{20,16},{24,28},{28,24},{1,5},{5... | collective-permute-start | bytes 393224 | tf_op jit(solution)/shard_map/ppermute | solution.py:558
  15.2 1.5 %collective-permute-start.5 = (f32[2,64,256]{2,1,0:T(8,128)S(1)}, f32[2,64,256]{2,1,0:T(8,128)S(1)}, u32[]{:S(2)}, u32[]{:S(2)}) collective-permute-start(f32[2,64,256]{2,1,0:T(8,128)S(1)} %get-tuple-element.52), channel_id=1, source_target_pairs={{0,12},{4,8},{8,4},{12,0},{16,28},{20,24},{24,20},{28,16},{1,13},{... | collective-permute-start | bytes 393224 | tf_op jit(solution)/shard_map/ppermute | solution.py:558
  17.5 1.3 %forward_half.3 = (f32[2,64,256]{2,1,0:T(8,128)S(1)}, f32[2,64,256]{2,1,0:T(8,128)S(1)}, f32[2,64,256]{2,1,0:T(8,128)S(1)}, f32[2,64,256]{2,1,0:T(8,128)S(1)}) custom-call(f32[2,64,256]{2,1,0:T(8,128)S(1)} %collective-permute-done.6.refs_0_, f32[2,64,256]{2,1,0:T(8,128)S(1)} %collective-permute-done.7.refs_1_, ...), custom_call_target="tpu_custom_call" | custom-call | flops 603979776 | bytes 1835008 | tf_op jit(solution)/shard_map/forward_half/pallas_call | solution.py:401
  18.8 1.6 %collective-permute-start.10 = (f32[2,64,256]{2,1,0:T(8,128)S(1)}, f32[2,64,256]{2,1,0:T(8,128)S(1)}, u32[]{:S(2)}, u32[]{:S(2)}) collective-permute-start(f32[2,64,256]{2,1,0:T(8,128)S(1)} %get-tuple-element.55), channel_id=1, source_target_pairs={{0,4},{4,0},{8,12},{12,8},{16,20},{20,16},{24,28},{28,24},{1,5},{5... | collective-permute-start | bytes 393224 | tf_op jit(solution)/shard_map/ppermute | solution.py:558
  22.9 3.2 %collective-permute-done.10.refs_5_ = f32[2,64,256]{2,1,0:T(8,128)S(1)} collective-permute-done((f32[2,64,256]{2,1,0:T(8,128)S(1)}, f32[2,64,256]{2,1,0:T(8,128)S(1)}, u32[]{:S(2)}, u32[]{:S(2)}) %collective-permute-start.10) | collective-permute-done | bytes 131104 | tf_op jit(solution)/shard_map/ppermute | solution.py:558
  26.7 2.0 %collective-permute-done.12.refs_7_ = f32[2,64,256]{2,1,0:T(8,128)S(1)} collective-permute-done((f32[2,64,256]{2,1,0:T(8,128)S(1)}, f32[2,64,256]{2,1,0:T(8,128)S(1)}, u32[]{:S(2)}, u32[]{:S(2)}) %collective-permute-start.12) | collective-permute-done | bytes 131104 | tf_op jit(solution)/shard_map/ppermute | solution.py:558
  28.7 2.4 %middle_half.1 = (f32[2,64,256]{2,1,0:T(8,128)S(1)}, f32[2,64,256]{2,1,0:T(8,128)S(1)}, f32[2,64,256]{2,1,0:T(8,128)S(1)}, f32[2,64,256]{2,1,0:T(8,128)S(1)}, f3...) custom-call(s32[3]{0:T(128)S(1)} %pad_add_fusion.at_ref, ...), custom_call_target="tpu_custom_call" | custom-call | bytes 6291456 | tf_op jit(solution)/shard_map/middle_half/pallas_call | solution.py:442
  31.1 1.6 %collective-permute-start.16 = (f32[2,64,256]{2,1,0:T(8,128)S(1)}, f32[2,64,256]{2,1,0:T(8,128)S(1)}, u32[]{:S(2)}, u32[]{:S(2)}) collective-permute-start(f32[2,64,256]{2,1,0:T(8,128)S(1)} %get-tuple-element.66), channel_id=1, source_target_pairs={{0,4},{4,0},{8,12},{12,8},{16,20},{20,16},{24,28},{28,24},{1,5},{5... | collective-permute-start | bytes 393224 | tf_op jit(solution)/shard_map/ppermute | solution.py:558
  34.7 1.5 %collective-permute-start.13 = (f32[2,64,256]{2,1,0:T(8,128)S(1)}, f32[2,64,256]{2,1,0:T(8,128)S(1)}, u32[]{:S(2)}, u32[]{:S(2)}) collective-permute-start(f32[2,64,256]{2,1,0:T(8,128)S(1)} %get-tuple-element.59), channel_id=1, source_target_pairs={{0,4},{4,0},{8,12},{12,8},{16,20},{20,16},{24,28},{28,24},{1,5},{5... | collective-permute-start | bytes 393224 | tf_op jit(solution)/shard_map/ppermute | solution.py:558
  37.4 2.4 %collective-permute-start.15 = (f32[2,64,256]{2,1,0:T(8,128)S(1)}, f32[2,64,256]{2,1,0:T(8,128)S(1)}, u32[]{:S(2)}, u32[]{:S(2)}) collective-permute-start(f32[2,64,256]{2,1,0:T(8,128)S(1)} %get-tuple-element.61), channel_id=1, source_target_pairs={{0,12},{4,8},{8,4},{12,0},{16,28},{20,24},{24,20},{28,16},{1,13},{... | collective-permute-start | bytes 393224 | tf_op jit(solution)/shard_map/ppermute | solution.py:558
  39.8 2.0 %collective-permute-done.18.refs_3_ = f32[2,64,256]{2,1,0:T(8,128)S(1)} collective-permute-done((f32[2,64,256]{2,1,0:T(8,128)S(1)}, f32[2,64,256]{2,1,0:T(8,128)S(1)}, u32[]{:S(2)}, u32[]{:S(2)}) %collective-permute-start.18) | collective-permute-done | bytes 131104 | tf_op jit(solution)/shard_map/ppermute | solution.py:558
  45.6 1.5 %collective-permute-start.23 = (f32[136,256]{1,0:T(8,128)S(1)}, f32[136,256]{1,0:T(8,128)S(1)}, u32[]{:S(2)}, u32[]{:S(2)}) collective-permute-start(f32[136,256]{1,0:T(8,128)S(1)} %get-tuple-element.76), channel_id=1, source_target_pairs={{0,2},{1,3},{2,0},{3,1},{4,6},{5,7},{6,4},{7,5},{8,10},{9,11},{10,... | collective-permute-start | bytes 417800 | tf_op jit(solution)/shard_map/ppermute | solution.py:558
  48.4 3.2 %collective-permute-done.23 = f32[136,256]{1,0:T(8,128)S(1)} collective-permute-done((f32[136,256]{1,0:T(8,128)S(1)}, f32[136,256]{1,0:T(8,128)S(1)}, u32[]{:S(2)}, u32[]{:S(2)}) %collective-permute-start.23) | collective-permute-done | bytes 139296 | tf_op jit(solution)/shard_map/ppermute | solution.py:558
  51.7 3.5 %collective-permute-start.26 = (f32[136,256]{1,0:T(8,128)S(1)}, f32[136,256]{1,0:T(8,128)S(1)}, u32[]{:S(2)}, u32[]{:S(2)}) collective-permute-start(f32[136,256]{1,0:T(8,128)S(1)} %add.20), channel_id=1, source_target_pairs={{0,16},{4,20},{8,24},{12,28},{16,0},{20,4},{24,8},{28,12},{1,17},{... | collective-permute-start | bytes 417800 | tf_op jit(solution)/shard_map/ppermute | solution.py:558
  55.5 1.6 %collective-permute-start.27 = (f32[136,256]{1,0:T(8,128)S(1)}, f32[136,256]{1,0:T(8,128)S(1)}, u32[]{:S(2)}, u32[]{:S(2)}) collective-permute-start(f32[136,256]{1,0:T(8,128)S(1)} %get-tuple-element.82), channel_id=1, source_target_pairs={{0,2},{1,3},{2,0},{3,1},{4,6},{5,7},{6,4},{7,5},{8,10},{9,11},{10,... | collective-permute-start | bytes 417800 | tf_op jit(solution)/shard_map/ppermute | solution.py:558
  57.1 3.2 %collective-permute-done.26 = f32[136,256]{1,0:T(8,128)S(1)} collective-permute-done((f32[136,256]{1,0:T(8,128)S(1)}, f32[136,256]{1,0:T(8,128)S(1)}, u32[]{:S(2)}, u32[]{:S(2)}) %collective-permute-start.26) | collective-permute-done | bytes 139296 | tf_op jit(solution)/shard_map/ppermute | solution.py:558
  60.7 1.6 %collective-permute-start.28 = (f32[64,256]{1,0:T(8,128)S(1)}, f32[64,256]{1,0:T(8,128)S(1)}, u32[]{:S(2)}, u32[]{:S(2)}) collective-permute-start(f32[64,256]{1,0:T(8,128)S(1)} %get-tuple-element.88.first_ref), channel_id=1, source_target_pairs={{0,4},{4,0},{8,12},{12,8},{16,20},{20,16},{24,28},{28,24},{1,5},{5... | collective-permute-start | bytes 196616 | tf_op jit(solution)/shard_map/ppermute | solution.py:558
  62.3 3.2 %collective-permute-start.29 = (f32[64,256]{1,0:T(8,128)S(1)}, f32[64,256]{1,0:T(8,128)S(1)}, u32[]{:S(2)}, u32[]{:S(2)}) collective-permute-start(f32[64,256]{1,0:T(8,128)S(1)} %get-tuple-element.87.second_ref), channel_id=1, source_target_pairs={{4,8},{12,16},{20,24},{8,4},{16,12},{24,20},{5,9},{13,17},{21,25},... | collective-permute-start | bytes 196616 | tf_op jit(solution)/shard_map/ppermute | solution.py:549
  65.5 1.3 %slopes.1 = (f32[2,64,256]{2,1,0:T(8,128)}, f32[2,64,256]{2,1,0:T(8,128)}) custom-call(s32[3]{0:T(128)S(1)} %pad_add_fusion.at_ref, f32[64,256]{1,0:T(8,128)S(1)} %get-tuple-element.88.first_ref, f32[64,256]{1,0:T(8,128)S(1)} %get-tuple-element.87.second_ref, f32[8,256]{1,0:T(8,128)S(1)} %slice.30.outer_ref), custom_call_target="tpu_custom_call" | custom-call | bytes 401408 | tf_op jit(solution)/shard_map/slopes/pallas_call | solution.py:533
  66.9 2.5 %collective-permute-done.29 = f32[64,256]{1,0:T(8,128)S(1)} collective-permute-done((f32[64,256]{1,0:T(8,128)S(1)}, f32[64,256]{1,0:T(8,128)S(1)}, u32[]{:S(2)}, u32[]{:S(2)}) %collective-permute-start.29) | collective-permute-done | bytes 65568 | tf_op jit(solution)/shard_map/ppermute | solution.py:549
  (63 shorter events, 19.6 us)
Async XLA Ops:
  0.6 8.4 %collective-permute-start.6 = (f32[2,64,256]{2,1,0:T(8,128)}, f32[2,64,256]{2,1,0:T(8,128)S(1)}, u32[]{:S(2)}, u32[]{:S(2)}) collective-permute-start(f32[2,64,256]{2,1,0:T(8,128)} %density_ref.1), channel_id=1, source_target_pairs={{0,16},{4,20},{8,24},{12,28},{16,0},{20,4},{24,8},{28,12},{1,17},{... | collective-permute-start | bytes 393224 | tf_op jit(solution)/shard_map/ppermute | solution.py:558
  3.3 7.3 %collective-permute-start = (f32[2,64,256]{2,1,0:T(8,128)}, f32[2,64,256]{2,1,0:T(8,128)S(1)}, u32[]{:S(2)}, u32[]{:S(2)}) collective-permute-start(f32[2,64,256]{2,1,0:T(8,128)} %density_ref.1), channel_id=1, source_target_pairs={{0,1},{1,0},{2,3},{3,2},{4,5},{5,4},{6,7},{7,6},{8,9},{9,8},{10,11... | collective-permute-start | bytes 393224 | tf_op jit(solution)/shard_map/ppermute | solution.py:558
  3.3 7.6 %collective-permute-start.1 = (f32[2,64,256]{2,1,0:T(8,128)}, f32[2,64,256]{2,1,0:T(8,128)S(1)}, u32[]{:S(2)}, u32[]{:S(2)}) collective-permute-start(f32[2,64,256]{2,1,0:T(8,128)} %density_ref.1), channel_id=1, source_target_pairs={{0,2},{1,3},{2,0},{3,1},{4,6},{5,7},{6,4},{7,5},{8,10},{9,11},{10,... | collective-permute-start | bytes 393224 | tf_op jit(solution)/shard_map/ppermute | solution.py:558
  4.8 7.0 %collective-permute-start.2 = (f32[2,64,256]{2,1,0:T(8,128)}, f32[2,64,256]{2,1,0:T(8,128)S(1)}, u32[]{:S(2)}, u32[]{:S(2)}) collective-permute-start(f32[2,64,256]{2,1,0:T(8,128)} %density_ref.1), channel_id=1, source_target_pairs={{0,3},{1,2},{2,1},{3,0},{4,7},{5,6},{6,5},{7,4},{8,11},{9,10},{10,... | collective-permute-start | bytes 393224 | tf_op jit(solution)/shard_map/ppermute | solution.py:558
  9.1 6.1 %collective-permute-start.7 = (f32[2,64,256]{2,1,0:T(8,128)S(1)}, f32[2,64,256]{2,1,0:T(8,128)S(1)}, u32[]{:S(2)}, u32[]{:S(2)}) collective-permute-start(f32[2,64,256]{2,1,0:T(8,128)S(1)} %collective-permute-done.6.refs_0_), channel_id=1, source_target_pairs={{0,1},{1,0},{2,3},{3,2},{4,5},{5,4},{6,7},{7,6},{8,9},{9,8},{10,11... | collective-permute-start | bytes 393224 | tf_op jit(solution)/shard_map/ppermute | solution.py:558
  9.1 7.6 %collective-permute-start.8 = (f32[2,64,256]{2,1,0:T(8,128)S(1)}, f32[2,64,256]{2,1,0:T(8,128)S(1)}, u32[]{:S(2)}, u32[]{:S(2)}) collective-permute-start(f32[2,64,256]{2,1,0:T(8,128)S(1)} %collective-permute-done.6.refs_0_), channel_id=1, source_target_pairs={{0,2},{1,3},{2,0},{3,1},{4,6},{5,7},{6,4},{7,5},{8,10},{9,11},{10,... | collective-permute-start | bytes 393224 | tf_op jit(solution)/shard_map/ppermute | solution.py:558
  10.6 6.9 %collective-permute-start.9 = (f32[2,64,256]{2,1,0:T(8,128)S(1)}, f32[2,64,256]{2,1,0:T(8,128)S(1)}, u32[]{:S(2)}, u32[]{:S(2)}) collective-permute-start(f32[2,64,256]{2,1,0:T(8,128)S(1)} %collective-permute-done.6.refs_0_), channel_id=1, source_target_pairs={{0,3},{1,2},{2,1},{3,0},{4,7},{5,6},{6,5},{7,4},{8,11},{9,10},{10,... | collective-permute-start | bytes 393224 | tf_op jit(solution)/shard_map/ppermute | solution.py:558
  13.1 8.4 %collective-permute-start.3 = (f32[2,64,256]{2,1,0:T(8,128)S(1)}, f32[2,64,256]{2,1,0:T(8,128)S(1)}, u32[]{:S(2)}, u32[]{:S(2)}) collective-permute-start(f32[2,64,256]{2,1,0:T(8,128)S(1)} %get-tuple-element.50), channel_id=1, source_target_pairs={{0,4},{4,0},{8,12},{12,8},{16,20},{20,16},{24,28},{28,24},{1,5},{5... | collective-permute-start | bytes 393224 | tf_op jit(solution)/shard_map/ppermute | solution.py:558
  14.7 7.6 %collective-permute-start.4 = (f32[2,64,256]{2,1,0:T(8,128)S(1)}, f32[2,64,256]{2,1,0:T(8,128)S(1)}, u32[]{:S(2)}, u32[]{:S(2)}) collective-permute-start(f32[2,64,256]{2,1,0:T(8,128)S(1)} %get-tuple-element.51), channel_id=1, source_target_pairs={{0,8},{4,12},{8,0},{12,4},{16,24},{20,28},{24,16},{28,20},{1,9},{5... | collective-permute-start | bytes 393224 | tf_op jit(solution)/shard_map/ppermute | solution.py:558
  15.2 7.7 %collective-permute-start.5 = (f32[2,64,256]{2,1,0:T(8,128)S(1)}, f32[2,64,256]{2,1,0:T(8,128)S(1)}, u32[]{:S(2)}, u32[]{:S(2)}) collective-permute-start(f32[2,64,256]{2,1,0:T(8,128)S(1)} %get-tuple-element.52), channel_id=1, source_target_pairs={{0,12},{4,8},{8,4},{12,0},{16,28},{20,24},{24,20},{28,16},{1,13},{... | collective-permute-start | bytes 393224 | tf_op jit(solution)/shard_map/ppermute | solution.py:558
  18.8 7.3 %collective-permute-start.10 = (f32[2,64,256]{2,1,0:T(8,128)S(1)}, f32[2,64,256]{2,1,0:T(8,128)S(1)}, u32[]{:S(2)}, u32[]{:S(2)}) collective-permute-start(f32[2,64,256]{2,1,0:T(8,128)S(1)} %get-tuple-element.55), channel_id=1, source_target_pairs={{0,4},{4,0},{8,12},{12,8},{16,20},{20,16},{24,28},{28,24},{1,5},{5... | collective-permute-start | bytes 393224 | tf_op jit(solution)/shard_map/ppermute | solution.py:558
  20.4 6.3 %collective-permute-start.11 = (f32[2,64,256]{2,1,0:T(8,128)S(1)}, f32[2,64,256]{2,1,0:T(8,128)S(1)}, u32[]{:S(2)}, u32[]{:S(2)}) collective-permute-start(f32[2,64,256]{2,1,0:T(8,128)S(1)} %get-tuple-element.56), channel_id=1, source_target_pairs={{0,8},{4,12},{8,0},{12,4},{16,24},{20,28},{24,16},{28,20},{1,9},{5... | collective-permute-start | bytes 393224 | tf_op jit(solution)/shard_map/ppermute | solution.py:558
  21.5 7.2 %collective-permute-start.12 = (f32[2,64,256]{2,1,0:T(8,128)S(1)}, f32[2,64,256]{2,1,0:T(8,128)S(1)}, u32[]{:S(2)}, u32[]{:S(2)}) collective-permute-start(f32[2,64,256]{2,1,0:T(8,128)S(1)} %get-tuple-element.57), channel_id=1, source_target_pairs={{0,12},{4,8},{8,4},{12,0},{16,28},{20,24},{24,20},{28,16},{1,13},{... | collective-permute-start | bytes 393224 | tf_op jit(solution)/shard_map/ppermute | solution.py:558
  31.1 6.3 %collective-permute-start.16 = (f32[2,64,256]{2,1,0:T(8,128)S(1)}, f32[2,64,256]{2,1,0:T(8,128)S(1)}, u32[]{:S(2)}, u32[]{:S(2)}) collective-permute-start(f32[2,64,256]{2,1,0:T(8,128)S(1)} %get-tuple-element.66), channel_id=1, source_target_pairs={{0,4},{4,0},{8,12},{12,8},{16,20},{20,16},{24,28},{28,24},{1,5},{5... | collective-permute-start | bytes 393224 | tf_op jit(solution)/shard_map/ppermute | solution.py:558
  32.7 7.1 %collective-permute-start.17 = (f32[2,64,256]{2,1,0:T(8,128)S(1)}, f32[2,64,256]{2,1,0:T(8,128)S(1)}, u32[]{:S(2)}, u32[]{:S(2)}) collective-permute-start(f32[2,64,256]{2,1,0:T(8,128)S(1)} %get-tuple-element.67), channel_id=1, source_target_pairs={{0,8},{4,12},{8,0},{12,4},{16,24},{20,28},{24,16},{28,20},{1,9},{5... | collective-permute-start | bytes 393224 | tf_op jit(solution)/shard_map/ppermute | solution.py:558
  33.9 7.9 %collective-permute-start.18 = (f32[2,64,256]{2,1,0:T(8,128)S(1)}, f32[2,64,256]{2,1,0:T(8,128)S(1)}, u32[]{:S(2)}, u32[]{:S(2)}) collective-permute-start(f32[2,64,256]{2,1,0:T(8,128)S(1)} %get-tuple-element.68), channel_id=1, source_target_pairs={{0,12},{4,8},{8,4},{12,0},{16,28},{20,24},{24,20},{28,16},{1,13},{... | collective-permute-start | bytes 393224 | tf_op jit(solution)/shard_map/ppermute | solution.py:558
  34.7 12.5 %collective-permute-start.13 = (f32[2,64,256]{2,1,0:T(8,128)S(1)}, f32[2,64,256]{2,1,0:T(8,128)S(1)}, u32[]{:S(2)}, u32[]{:S(2)}) collective-permute-start(f32[2,64,256]{2,1,0:T(8,128)S(1)} %get-tuple-element.59), channel_id=1, source_target_pairs={{0,4},{4,0},{8,12},{12,8},{16,20},{20,16},{24,28},{28,24},{1,5},{5... | collective-permute-start | bytes 393224 | tf_op jit(solution)/shard_map/ppermute | solution.py:558
  36.2 11.0 %collective-permute-start.14 = (f32[2,64,256]{2,1,0:T(8,128)S(1)}, f32[2,64,256]{2,1,0:T(8,128)S(1)}, u32[]{:S(2)}, u32[]{:S(2)}) collective-permute-start(f32[2,64,256]{2,1,0:T(8,128)S(1)} %get-tuple-element.60), channel_id=1, source_target_pairs={{0,8},{4,12},{8,0},{12,4},{16,24},{20,28},{24,16},{28,20},{1,9},{5... | collective-permute-start | bytes 393224 | tf_op jit(solution)/shard_map/ppermute | solution.py:558
  37.4 9.8 %collective-permute-start.15 = (f32[2,64,256]{2,1,0:T(8,128)S(1)}, f32[2,64,256]{2,1,0:T(8,128)S(1)}, u32[]{:S(2)}, u32[]{:S(2)}) collective-permute-start(f32[2,64,256]{2,1,0:T(8,128)S(1)} %get-tuple-element.61), channel_id=1, source_target_pairs={{0,12},{4,8},{8,4},{12,0},{16,28},{20,24},{24,20},{28,16},{1,13},{... | collective-permute-start | bytes 393224 | tf_op jit(solution)/shard_map/ppermute | solution.py:558
  47.8 7.3 %collective-permute-start.24 = (f32[136,256]{1,0:T(8,128)S(1)}, f32[136,256]{1,0:T(8,128)S(1)}, u32[]{:S(2)}, u32[]{:S(2)}) collective-permute-start(f32[136,256]{1,0:T(8,128)S(1)} %get-tuple-element.79), channel_id=1, source_target_pairs={{0,1},{1,0},{2,3},{3,2},{4,5},{5,4},{6,7},{7,6},{8,9},{9,8},{10,11... | collective-permute-start | bytes 417800 | tf_op jit(solution)/shard_map/ppermute | solution.py:558
  48.0 7.2 %collective-permute-start.25 = (f32[136,256]{1,0:T(8,128)S(1)}, f32[136,256]{1,0:T(8,128)S(1)}, u32[]{:S(2)}, u32[]{:S(2)}) collective-permute-start(f32[136,256]{1,0:T(8,128)S(1)} %get-tuple-element.80), channel_id=1, source_target_pairs={{0,1},{1,0},{2,3},{3,2},{4,5},{5,4},{6,7},{7,6},{8,9},{9,8},{10,11... | collective-permute-start | bytes 417800 | tf_op jit(solution)/shard_map/ppermute | solution.py:558
  51.7 8.6 %collective-permute-start.26 = (f32[136,256]{1,0:T(8,128)S(1)}, f32[136,256]{1,0:T(8,128)S(1)}, u32[]{:S(2)}, u32[]{:S(2)}) collective-permute-start(f32[136,256]{1,0:T(8,128)S(1)} %add.20), channel_id=1, source_target_pairs={{0,16},{4,20},{8,24},{12,28},{16,0},{20,4},{24,8},{28,12},{1,17},{... | collective-permute-start | bytes 417800 | tf_op jit(solution)/shard_map/ppermute | solution.py:558
  60.7 6.2 %collective-permute-start.28 = (f32[64,256]{1,0:T(8,128)S(1)}, f32[64,256]{1,0:T(8,128)S(1)}, u32[]{:S(2)}, u32[]{:S(2)}) collective-permute-start(f32[64,256]{1,0:T(8,128)S(1)} %get-tuple-element.88.first_ref), channel_id=1, source_target_pairs={{0,4},{4,0},{8,12},{12,8},{16,20},{20,16},{24,28},{28,24},{1,5},{5... | collective-permute-start | bytes 196616 | tf_op jit(solution)/shard_map/ppermute | solution.py:558
  62.3 7.0 %collective-permute-start.29 = (f32[64,256]{1,0:T(8,128)S(1)}, f32[64,256]{1,0:T(8,128)S(1)}, u32[]{:S(2)}, u32[]{:S(2)}) collective-permute-start(f32[64,256]{1,0:T(8,128)S(1)} %get-tuple-element.87.second_ref), channel_id=1, source_target_pairs={{4,8},{12,16},{20,24},{8,4},{16,12},{24,20},{5,9},{13,17},{21,25},... | collective-permute-start | bytes 196616 | tf_op jit(solution)/shard_map/ppermute | solution.py:549
  (10 other events, 51.9 us)

commit v8 on v7

--- a/solution.py
+++ b/solution.py
@@ -251,6 +251,10 @@
     row = lax.broadcasted_iota(jnp.int32, (slabs, 1, 1), 0)
     edge = ((row == 0) & (me == 0)) | ((row == slabs - 1) & (me == size - 1))
     return (padded[2:] - padded[:-2]) * jnp.where(edge, 1.0, 0.5)
+
+
+def diagonal_first(pieces):
+    return [pieces[0], *pieces[:0:-1]]
 
 
 def pieces_spec(count):
@@ -421,8 +425,8 @@
 
     def tile(i, carry):
         rows = pl.ds(pl.multiple_of(8 * i, 8), 8)
-        for k, slab in enumerate(place):
-            in_ref[slab] = ins[k][:, rows, :]
+        for ref, slab in zip(ins, diagonal_first(place[:group]) + diagonal_first(place[group:])):
+            in_ref[slab] = ref[:, rows, :]
         field = [(in_ref[a, b, :, :half], in_ref[a, b, :, half:]) for a, b in at]
         both = lambda ref: lambda k: (ref[0, k, rows, :], ref[1, k, rows, :])
         for (a, b), (re, im) in zip(at, through_z(field, both(g_ref), both(h_ref))):
@@ -437,7 +441,8 @@
 
 def middle_half(at, field, green, image_green):
     slabs, kx, wide = field[0].shape
-    ins = (*field, green, image_green)
+    group = len(field) // 2
+    ins = (*diagonal_first(field[:group]), *diagonal_first(field[group:]), green, image_green)
     shape = jax.ShapeDtypeStruct(field[0].shape, jnp.float32)
     return pl.pallas_call(
         middle_half_kernel,

time: 70.8 us -> 70.1 us (level)
  starting transfers between devices: 35.2 us -> 34.4 us
    ppermute x29, starting transfers between devices: 32 us -> 31.2 us  [swap(): lax.ppermute(value, axis, [(s, s ^ mask) for s in range(lax.axis_size(axi...]
where the time goes in v8:
time: 70.1 us; the launch traced here: 69.6 us
  starting transfers between devices  34.4 us (49%)
  waiting for transfers between devices  22.3 us (32%)
  Pallas kernels  9.41 us (13%)
  local copies, waits for them, and re-layouts  1.85 us (3%)
  other arithmetic  0.84 us (1%)
  between operations  0.79 us (1%)
    ppermute x29, starting transfers between devices, swap(): lax.ppermute(value, axis, [(s, s ^ mask) for s in range(lax.axis_size(axi...  31.2 us
    ppermute x29, waiting for transfers between devices, swap(): lax.ppermute(value, axis, [(s, s ^ mask) for s in range(lax.axis_size(axi...  19.9 us
    ppermute x1, starting transfers between devices, slope_z_pairs(): far = lax.ppermute(second, 'gz', pairs + [(b, a) for a, b in pairs])  3.26 us
    pallas_call x2, Pallas kernels, forward_half(): pl.pallas_call(forward_half_kernel, in_specs=pieces_spec(len(ins)), out_s...  2.57 us
    pallas_call x1, Pallas kernels, middle_half(): pl.pallas_call(middle_half_kernel, in_specs=[pl.BlockSpec(memory_space=SM...  2.45 us
    ppermute x1, waiting for transfers between devices, slope_z_pairs(): far = lax.ppermute(second, 'gz', pairs + [(b, a) for a, b in pairs])  2.4 us
    unnamed x8, local copies, waits for them, and re-layouts  1.82 us
  transfers between devices with their start and end apart: 30, of which 15 were waited for; matrix products, arithmetic and copies ran while one was open for 0% of the time, Pallas kernels for 10%

profile of v8, /device:TPU:8, one launch (start us, length us, event | category | flops | bytes accessed | tf_op | source)
XLA Modules:
  0.0 69.6 jit_solution(8046438161143610122)
XLA Ops:
  0.6 2.7 %collective-permute-start.6 = (f32[2,64,256]{2,1,0:T(8,128)}, f32[2,64,256]{2,1,0:T(8,128)S(1)}, u32[]{:S(2)}, u32[]{:S(2)}) collective-permute-start(f32[2,64,256]{2,1,0:T(8,128)} %density_ref.1), channel_id=1, source_target_pairs={{0,16},{4,20},{8,24},{12,28},{16,0},{20,4},{24,8},{28,12},{1,17},{... | collective-permute-start | bytes 393224 | tf_op jit(solution)/shard_map/ppermute | solution.py:563
  3.3 1.5 %collective-permute-start.1 = (f32[2,64,256]{2,1,0:T(8,128)}, f32[2,64,256]{2,1,0:T(8,128)S(1)}, u32[]{:S(2)}, u32[]{:S(2)}) collective-permute-start(f32[2,64,256]{2,1,0:T(8,128)} %density_ref.1), channel_id=1, source_target_pairs={{0,2},{1,3},{2,0},{3,1},{4,6},{5,7},{6,4},{7,5},{8,10},{9,11},{10,... | collective-permute-start | bytes 393224 | tf_op jit(solution)/shard_map/ppermute | solution.py:563
  9.1 1.5 %collective-permute-start.8 = (f32[2,64,256]{2,1,0:T(8,128)S(1)}, f32[2,64,256]{2,1,0:T(8,128)S(1)}, u32[]{:S(2)}, u32[]{:S(2)}) collective-permute-start(f32[2,64,256]{2,1,0:T(8,128)S(1)} %collective-permute-done.6.refs_0_), channel_id=1, source_target_pairs={{0,2},{1,3},{2,0},{3,1},{4,6},{5,7},{6,4},{7,5},{8,10},{9,11},{10,... | collective-permute-start | bytes 393224 | tf_op jit(solution)/shard_map/ppermute | solution.py:563
  11.8 1.3 %forward_half.2 = (f32[2,64,256]{2,1,0:T(8,128)S(1)}, f32[2,64,256]{2,1,0:T(8,128)S(1)}, f32[2,64,256]{2,1,0:T(8,128)S(1)}, f32[2,64,256]{2,1,0:T(8,128)S(1)}) custom-call(f32[2,64,256]{2,1,0:T(8,128)S(1)} %get-tuple-element.44.refs_0_, f32[2,64,256]{2,1,0:T(8,128)S(1)} %collective-permute-done.refs_1_, f32[2,64,256]{2,1,0:T(8,128)S(1)} %collective-permute-done.1.refs_2_, ...), custom_call_target="tpu_custom_call" | custom-call | flops 603979776 | bytes 1835008 | tf_op jit(solution)/shard_map/forward_half/pallas_call | solution.py:405
  13.1 1.5 %collective-permute-start.3 = (f32[2,64,256]{2,1,0:T(8,128)S(1)}, f32[2,64,256]{2,1,0:T(8,128)S(1)}, u32[]{:S(2)}, u32[]{:S(2)}) collective-permute-start(f32[2,64,256]{2,1,0:T(8,128)S(1)} %get-tuple-element.50), channel_id=1, source_target_pairs={{0,12},{4,8},{8,4},{12,0},{16,28},{20,24},{24,20},{28,16},{1,13},{... | collective-permute-start | bytes 393224 | tf_op jit(solution)/shard_map/ppermute | solution.py:563
  14.6 1.6 %collective-permute-start.4 = (f32[2,64,256]{2,1,0:T(8,128)S(1)}, f32[2,64,256]{2,1,0:T(8,128)S(1)}, u32[]{:S(2)}, u32[]{:S(2)}) collective-permute-start(f32[2,64,256]{2,1,0:T(8,128)S(1)} %get-tuple-element.51), channel_id=1, source_target_pairs={{0,8},{4,12},{8,0},{12,4},{16,24},{20,28},{24,16},{28,20},{1,9},{5... | collective-permute-start | bytes 393224 | tf_op jit(solution)/shard_map/ppermute | solution.py:563
  17.5 1.3 %forward_half.3 = (f32[2,64,256]{2,1,0:T(8,128)S(1)}, f32[2,64,256]{2,1,0:T(8,128)S(1)}, f32[2,64,256]{2,1,0:T(8,128)S(1)}, f32[2,64,256]{2,1,0:T(8,128)S(1)}) custom-call(f32[2,64,256]{2,1,0:T(8,128)S(1)} %collective-permute-done.6.refs_0_, f32[2,64,256]{2,1,0:T(8,128)S(1)} %collective-permute-done.7.refs_1_, ...), custom_call_target="tpu_custom_call" | custom-call | flops 603979776 | bytes 1835008 | tf_op jit(solution)/shard_map/forward_half/pallas_call | solution.py:405
  18.8 2.2 %collective-permute-start.10 = (f32[2,64,256]{2,1,0:T(8,128)S(1)}, f32[2,64,256]{2,1,0:T(8,128)S(1)}, u32[]{:S(2)}, u32[]{:S(2)}) collective-permute-start(f32[2,64,256]{2,1,0:T(8,128)S(1)} %get-tuple-element.55), channel_id=1, source_target_pairs={{0,12},{4,8},{8,4},{12,0},{16,28},{20,24},{24,20},{28,16},{1,13},{... | collective-permute-start | bytes 393224 | tf_op jit(solution)/shard_map/ppermute | solution.py:563
  22.6 3.5 %collective-permute-done.10.refs_5_ = f32[2,64,256]{2,1,0:T(8,128)S(1)} collective-permute-done((f32[2,64,256]{2,1,0:T(8,128)S(1)}, f32[2,64,256]{2,1,0:T(8,128)S(1)}, u32[]{:S(2)}, u32[]{:S(2)}) %collective-permute-start.10) | collective-permute-done | bytes 131104 | tf_op jit(solution)/shard_map/ppermute | solution.py:563
  26.0 2.5 %collective-permute-done.11.refs_6_ = f32[2,64,256]{2,1,0:T(8,128)S(1)} collective-permute-done((f32[2,64,256]{2,1,0:T(8,128)S(1)}, f32[2,64,256]{2,1,0:T(8,128)S(1)}, u32[]{:S(2)}, u32[]{:S(2)}) %collective-permute-start.11) | collective-permute-done | bytes 131104 | tf_op jit(solution)/shard_map/ppermute | solution.py:563
  28.5 2.4 %middle_half.1 = (f32[2,64,256]{2,1,0:T(8,128)S(1)}, f32[2,64,256]{2,1,0:T(8,128)S(1)}, f32[2,64,256]{2,1,0:T(8,128)S(1)}, f32[2,64,256]{2,1,0:T(8,128)S(1)}, f3...) custom-call(s32[3]{0:T(128)S(1)} %pad_add_fusion.at_ref, ...), custom_call_target="tpu_custom_call" | custom-call | bytes 6291456 | tf_op jit(solution)/shard_map/middle_half/pallas_call | solution.py:447
  31.0 1.5 %collective-permute-start.16 = (f32[2,64,256]{2,1,0:T(8,128)S(1)}, f32[2,64,256]{2,1,0:T(8,128)S(1)}, u32[]{:S(2)}, u32[]{:S(2)}) collective-permute-start(f32[2,64,256]{2,1,0:T(8,128)S(1)} %get-tuple-element.66), channel_id=1, source_target_pairs={{0,4},{4,0},{8,12},{12,8},{16,20},{20,16},{24,28},{28,24},{1,5},{5... | collective-permute-start | bytes 393224 | tf_op jit(solution)/shard_map/ppermute | solution.py:563
  34.5 1.4 %collective-permute-start.13 = (f32[2,64,256]{2,1,0:T(8,128)S(1)}, f32[2,64,256]{2,1,0:T(8,128)S(1)}, u32[]{:S(2)}, u32[]{:S(2)}) collective-permute-start(f32[2,64,256]{2,1,0:T(8,128)S(1)} %get-tuple-element.59), channel_id=1, source_target_pairs={{0,4},{4,0},{8,12},{12,8},{16,20},{20,16},{24,28},{28,24},{1,5},{5... | collective-permute-start | bytes 393224 | tf_op jit(solution)/shard_map/ppermute | solution.py:563
  37.1 1.6 %collective-permute-start.15 = (f32[2,64,256]{2,1,0:T(8,128)S(1)}, f32[2,64,256]{2,1,0:T(8,128)S(1)}, u32[]{:S(2)}, u32[]{:S(2)}) collective-permute-start(f32[2,64,256]{2,1,0:T(8,128)S(1)} %get-tuple-element.61), channel_id=1, source_target_pairs={{0,12},{4,8},{8,4},{12,0},{16,28},{20,24},{24,20},{28,16},{1,13},{... | collective-permute-start | bytes 393224 | tf_op jit(solution)/shard_map/ppermute | solution.py:563
  38.8 2.5 %collective-permute-done.18.refs_3_ = f32[2,64,256]{2,1,0:T(8,128)S(1)} collective-permute-done((f32[2,64,256]{2,1,0:T(8,128)S(1)}, f32[2,64,256]{2,1,0:T(8,128)S(1)}, u32[]{:S(2)}, u32[]{:S(2)}) %collective-permute-start.18) | collective-permute-done | bytes 131104 | tf_op jit(solution)/shard_map/ppermute | solution.py:563
  45.1 1.6 %collective-permute-start.23 = (f32[136,256]{1,0:T(8,128)S(1)}, f32[136,256]{1,0:T(8,128)S(1)}, u32[]{:S(2)}, u32[]{:S(2)}) collective-permute-start(f32[136,256]{1,0:T(8,128)S(1)} %get-tuple-element.76), channel_id=1, source_target_pairs={{0,2},{1,3},{2,0},{3,1},{4,6},{5,7},{6,4},{7,5},{8,10},{9,11},{10,... | collective-permute-start | bytes 417800 | tf_op jit(solution)/shard_map/ppermute | solution.py:563
  47.9 3.2 %collective-permute-done.23 = f32[136,256]{1,0:T(8,128)S(1)} collective-permute-done((f32[136,256]{1,0:T(8,128)S(1)}, f32[136,256]{1,0:T(8,128)S(1)}, u32[]{:S(2)}, u32[]{:S(2)}) %collective-permute-start.23) | collective-permute-done | bytes 139296 | tf_op jit(solution)/shard_map/ppermute | solution.py:563
  51.1 3.7 %collective-permute-start.26 = (f32[136,256]{1,0:T(8,128)S(1)}, f32[136,256]{1,0:T(8,128)S(1)}, u32[]{:S(2)}, u32[]{:S(2)}) collective-permute-start(f32[136,256]{1,0:T(8,128)S(1)} %add.20), channel_id=1, source_target_pairs={{0,16},{4,20},{8,24},{12,28},{16,0},{20,4},{24,8},{28,12},{1,17},{... | collective-permute-start | bytes 417800 | tf_op jit(solution)/shard_map/ppermute | solution.py:563
  55.3 1.6 %collective-permute-start.27 = (f32[136,256]{1,0:T(8,128)S(1)}, f32[136,256]{1,0:T(8,128)S(1)}, u32[]{:S(2)}, u32[]{:S(2)}) collective-permute-start(f32[136,256]{1,0:T(8,128)S(1)} %get-tuple-element.82), channel_id=1, source_target_pairs={{0,2},{1,3},{2,0},{3,1},{4,6},{5,7},{6,4},{7,5},{8,10},{9,11},{10,... | collective-permute-start | bytes 417800 | tf_op jit(solution)/shard_map/ppermute | solution.py:563
  56.8 3.2 %collective-permute-done.26 = f32[136,256]{1,0:T(8,128)S(1)} collective-permute-done((f32[136,256]{1,0:T(8,128)S(1)}, f32[136,256]{1,0:T(8,128)S(1)}, u32[]{:S(2)}, u32[]{:S(2)}) %collective-permute-start.26) | collective-permute-done | bytes 139296 | tf_op jit(solution)/shard_map/ppermute | solution.py:563
  60.4 1.5 %collective-permute-start.28 = (f32[64,256]{1,0:T(8,128)S(1)}, f32[64,256]{1,0:T(8,128)S(1)}, u32[]{:S(2)}, u32[]{:S(2)}) collective-permute-start(f32[64,256]{1,0:T(8,128)S(1)} %get-tuple-element.88.first_ref), channel_id=1, source_target_pairs={{0,4},{4,0},{8,12},{12,8},{16,20},{20,16},{24,28},{28,24},{1,5},{5... | collective-permute-start | bytes 196616 | tf_op jit(solution)/shard_map/ppermute | solution.py:563
  61.9 3.3 %collective-permute-start.29 = (f32[64,256]{1,0:T(8,128)S(1)}, f32[64,256]{1,0:T(8,128)S(1)}, u32[]{:S(2)}, u32[]{:S(2)}) collective-permute-start(f32[64,256]{1,0:T(8,128)S(1)} %get-tuple-element.87.second_ref), channel_id=1, source_target_pairs={{4,8},{12,16},{20,24},{8,4},{16,12},{24,20},{5,9},{13,17},{21,25},... | collective-permute-start | bytes 196616 | tf_op jit(solution)/shard_map/ppermute | solution.py:554
  65.2 1.3 %slopes.1 = (f32[2,64,256]{2,1,0:T(8,128)}, f32[2,64,256]{2,1,0:T(8,128)}) custom-call(s32[3]{0:T(128)S(1)} %pad_add_fusion.at_ref, f32[64,256]{1,0:T(8,128)S(1)} %get-tuple-element.88.first_ref, f32[64,256]{1,0:T(8,128)S(1)} %get-tuple-element.87.second_ref, f32[8,256]{1,0:T(8,128)S(1)} %slice.30.outer_ref), custom_call_target="tpu_custom_call" | custom-call | bytes 401408 | tf_op jit(solution)/shard_map/slopes/pallas_call | solution.py:538
  66.5 2.4 %collective-permute-done.29 = f32[64,256]{1,0:T(8,128)S(1)} collective-permute-done((f32[64,256]{1,0:T(8,128)S(1)}, f32[64,256]{1,0:T(8,128)S(1)}, u32[]{:S(2)}, u32[]{:S(2)}) %collective-permute-start.29) | collective-permute-done | bytes 65568 | tf_op jit(solution)/shard_map/ppermute | solution.py:554
  (63 shorter events, 18.4 us)
Async XLA Ops:
  0.6 8.4 %collective-permute-start.6 = (f32[2,64,256]{2,1,0:T(8,128)}, f32[2,64,256]{2,1,0:T(8,128)S(1)}, u32[]{:S(2)}, u32[]{:S(2)}) collective-permute-start(f32[2,64,256]{2,1,0:T(8,128)} %density_ref.1), channel_id=1, source_target_pairs={{0,16},{4,20},{8,24},{12,28},{16,0},{20,4},{24,8},{28,12},{1,17},{... | collective-permute-start | bytes 393224 | tf_op jit(solution)/shard_map/ppermute | solution.py:563
  3.3 7.3 %collective-permute-start = (f32[2,64,256]{2,1,0:T(8,128)}, f32[2,64,256]{2,1,0:T(8,128)S(1)}, u32[]{:S(2)}, u32[]{:S(2)}) collective-permute-start(f32[2,64,256]{2,1,0:T(8,128)} %density_ref.1), channel_id=1, source_target_pairs={{0,1},{1,0},{2,3},{3,2},{4,5},{5,4},{6,7},{7,6},{8,9},{9,8},{10,11... | collective-permute-start | bytes 393224 | tf_op jit(solution)/shard_map/ppermute | solution.py:563
  3.3 7.6 %collective-permute-start.1 = (f32[2,64,256]{2,1,0:T(8,128)}, f32[2,64,256]{2,1,0:T(8,128)S(1)}, u32[]{:S(2)}, u32[]{:S(2)}) collective-permute-start(f32[2,64,256]{2,1,0:T(8,128)} %density_ref.1), channel_id=1, source_target_pairs={{0,2},{1,3},{2,0},{3,1},{4,6},{5,7},{6,4},{7,5},{8,10},{9,11},{10,... | collective-permute-start | bytes 393224 | tf_op jit(solution)/shard_map/ppermute | solution.py:563
  4.8 7.0 %collective-permute-start.2 = (f32[2,64,256]{2,1,0:T(8,128)}, f32[2,64,256]{2,1,0:T(8,128)S(1)}, u32[]{:S(2)}, u32[]{:S(2)}) collective-permute-start(f32[2,64,256]{2,1,0:T(8,128)} %density_ref.1), channel_id=1, source_target_pairs={{0,3},{1,2},{2,1},{3,0},{4,7},{5,6},{6,5},{7,4},{8,11},{9,10},{10,... | collective-permute-start | bytes 393224 | tf_op jit(solution)/shard_map/ppermute | solution.py:563
  9.1 7.1 %collective-permute-start.7 = (f32[2,64,256]{2,1,0:T(8,128)S(1)}, f32[2,64,256]{2,1,0:T(8,128)S(1)}, u32[]{:S(2)}, u32[]{:S(2)}) collective-permute-start(f32[2,64,256]{2,1,0:T(8,128)S(1)} %collective-permute-done.6.refs_0_), channel_id=1, source_target_pairs={{0,1},{1,0},{2,3},{3,2},{4,5},{5,4},{6,7},{7,6},{8,9},{9,8},{10,11... | collective-permute-start | bytes 393224 | tf_op jit(solution)/shard_map/ppermute | solution.py:563
  9.1 7.6 %collective-permute-start.8 = (f32[2,64,256]{2,1,0:T(8,128)S(1)}, f32[2,64,256]{2,1,0:T(8,128)S(1)}, u32[]{:S(2)}, u32[]{:S(2)}) collective-permute-start(f32[2,64,256]{2,1,0:T(8,128)S(1)} %collective-permute-done.6.refs_0_), channel_id=1, source_target_pairs={{0,2},{1,3},{2,0},{3,1},{4,6},{5,7},{6,4},{7,5},{8,10},{9,11},{10,... | collective-permute-start | bytes 393224 | tf_op jit(solution)/shard_map/ppermute | solution.py:563
  10.6 6.9 %collective-permute-start.9 = (f32[2,64,256]{2,1,0:T(8,128)S(1)}, f32[2,64,256]{2,1,0:T(8,128)S(1)}, u32[]{:S(2)}, u32[]{:S(2)}) collective-permute-start(f32[2,64,256]{2,1,0:T(8,128)S(1)} %collective-permute-done.6.refs_0_), channel_id=1, source_target_pairs={{0,3},{1,2},{2,1},{3,0},{4,7},{5,6},{6,5},{7,4},{8,11},{9,10},{10,... | collective-permute-start | bytes 393224 | tf_op jit(solution)/shard_map/ppermute | solution.py:563
  13.1 8.7 %collective-permute-start.3 = (f32[2,64,256]{2,1,0:T(8,128)S(1)}, f32[2,64,256]{2,1,0:T(8,128)S(1)}, u32[]{:S(2)}, u32[]{:S(2)}) collective-permute-start(f32[2,64,256]{2,1,0:T(8,128)S(1)} %get-tuple-element.50), channel_id=1, source_target_pairs={{0,12},{4,8},{8,4},{12,0},{16,28},{20,24},{24,20},{28,16},{1,13},{... | collective-permute-start | bytes 393224 | tf_op jit(solution)/shard_map/ppermute | solution.py:563
  14.6 8.0 %collective-permute-start.4 = (f32[2,64,256]{2,1,0:T(8,128)S(1)}, f32[2,64,256]{2,1,0:T(8,128)S(1)}, u32[]{:S(2)}, u32[]{:S(2)}) collective-permute-start(f32[2,64,256]{2,1,0:T(8,128)S(1)} %get-tuple-element.51), channel_id=1, source_target_pairs={{0,8},{4,12},{8,0},{12,4},{16,24},{20,28},{24,16},{28,20},{1,9},{5... | collective-permute-start | bytes 393224 | tf_op jit(solution)/shard_map/ppermute | solution.py:563
  16.2 6.4 %collective-permute-start.5 = (f32[2,64,256]{2,1,0:T(8,128)S(1)}, f32[2,64,256]{2,1,0:T(8,128)S(1)}, u32[]{:S(2)}, u32[]{:S(2)}) collective-permute-start(f32[2,64,256]{2,1,0:T(8,128)S(1)} %get-tuple-element.52), channel_id=1, source_target_pairs={{0,4},{4,0},{8,12},{12,8},{16,20},{20,16},{24,28},{28,24},{1,5},{5... | collective-permute-start | bytes 393224 | tf_op jit(solution)/shard_map/ppermute | solution.py:563
  18.8 7.3 %collective-permute-start.10 = (f32[2,64,256]{2,1,0:T(8,128)S(1)}, f32[2,64,256]{2,1,0:T(8,128)S(1)}, u32[]{:S(2)}, u32[]{:S(2)}) collective-permute-start(f32[2,64,256]{2,1,0:T(8,128)S(1)} %get-tuple-element.55), channel_id=1, source_target_pairs={{0,12},{4,8},{8,4},{12,0},{16,28},{20,24},{24,20},{28,16},{1,13},{... | collective-permute-start | bytes 393224 | tf_op jit(solution)/shard_map/ppermute | solution.py:563
  20.9 7.6 %collective-permute-start.11 = (f32[2,64,256]{2,1,0:T(8,128)S(1)}, f32[2,64,256]{2,1,0:T(8,128)S(1)}, u32[]{:S(2)}, u32[]{:S(2)}) collective-permute-start(f32[2,64,256]{2,1,0:T(8,128)S(1)} %get-tuple-element.56), channel_id=1, source_target_pairs={{0,8},{4,12},{8,0},{12,4},{16,24},{20,28},{24,16},{28,20},{1,9},{5... | collective-permute-start | bytes 393224 | tf_op jit(solution)/shard_map/ppermute | solution.py:563
  21.8 6.7 %collective-permute-start.12 = (f32[2,64,256]{2,1,0:T(8,128)S(1)}, f32[2,64,256]{2,1,0:T(8,128)S(1)}, u32[]{:S(2)}, u32[]{:S(2)}) collective-permute-start(f32[2,64,256]{2,1,0:T(8,128)S(1)} %get-tuple-element.57), channel_id=1, source_target_pairs={{0,4},{4,0},{8,12},{12,8},{16,20},{20,16},{24,28},{28,24},{1,5},{5... | collective-permute-start | bytes 393224 | tf_op jit(solution)/shard_map/ppermute | solution.py:563
  31.0 6.1 %collective-permute-start.16 = (f32[2,64,256]{2,1,0:T(8,128)S(1)}, f32[2,64,256]{2,1,0:T(8,128)S(1)}, u32[]{:S(2)}, u32[]{:S(2)}) collective-permute-start(f32[2,64,256]{2,1,0:T(8,128)S(1)} %get-tuple-element.66), channel_id=1, source_target_pairs={{0,4},{4,0},{8,12},{12,8},{16,20},{20,16},{24,28},{28,24},{1,5},{5... | collective-permute-start | bytes 393224 | tf_op jit(solution)/shard_map/ppermute | solution.py:563
  32.4 6.4 %collective-permute-start.17 = (f32[2,64,256]{2,1,0:T(8,128)S(1)}, f32[2,64,256]{2,1,0:T(8,128)S(1)}, u32[]{:S(2)}, u32[]{:S(2)}) collective-permute-start(f32[2,64,256]{2,1,0:T(8,128)S(1)} %get-tuple-element.67), channel_id=1, source_target_pairs={{0,8},{4,12},{8,0},{12,4},{16,24},{20,28},{24,16},{28,20},{1,9},{5... | collective-permute-start | bytes 393224 | tf_op jit(solution)/shard_map/ppermute | solution.py:563
  33.6 7.7 %collective-permute-start.18 = (f32[2,64,256]{2,1,0:T(8,128)S(1)}, f32[2,64,256]{2,1,0:T(8,128)S(1)}, u32[]{:S(2)}, u32[]{:S(2)}) collective-permute-start(f32[2,64,256]{2,1,0:T(8,128)S(1)} %get-tuple-element.68), channel_id=1, source_target_pairs={{0,12},{4,8},{8,4},{12,0},{16,28},{20,24},{24,20},{28,16},{1,13},{... | collective-permute-start | bytes 393224 | tf_op jit(solution)/shard_map/ppermute | solution.py:563
  34.5 12.2 %collective-permute-start.13 = (f32[2,64,256]{2,1,0:T(8,128)S(1)}, f32[2,64,256]{2,1,0:T(8,128)S(1)}, u32[]{:S(2)}, u32[]{:S(2)}) collective-permute-start(f32[2,64,256]{2,1,0:T(8,128)S(1)} %get-tuple-element.59), channel_id=1, source_target_pairs={{0,4},{4,0},{8,12},{12,8},{16,20},{20,16},{24,28},{28,24},{1,5},{5... | collective-permute-start | bytes 393224 | tf_op jit(solution)/shard_map/ppermute | solution.py:563
  35.9 10.8 %collective-permute-start.14 = (f32[2,64,256]{2,1,0:T(8,128)S(1)}, f32[2,64,256]{2,1,0:T(8,128)S(1)}, u32[]{:S(2)}, u32[]{:S(2)}) collective-permute-start(f32[2,64,256]{2,1,0:T(8,128)S(1)} %get-tuple-element.60), channel_id=1, source_target_pairs={{0,8},{4,12},{8,0},{12,4},{16,24},{20,28},{24,16},{28,20},{1,9},{5... | collective-permute-start | bytes 393224 | tf_op jit(solution)/shard_map/ppermute | solution.py:563
  37.1 9.6 %collective-permute-start.15 = (f32[2,64,256]{2,1,0:T(8,128)S(1)}, f32[2,64,256]{2,1,0:T(8,128)S(1)}, u32[]{:S(2)}, u32[]{:S(2)}) collective-permute-start(f32[2,64,256]{2,1,0:T(8,128)S(1)} %get-tuple-element.61), channel_id=1, source_target_pairs={{0,12},{4,8},{8,4},{12,0},{16,28},{20,24},{24,20},{28,16},{1,13},{... | collective-permute-start | bytes 393224 | tf_op jit(solution)/shard_map/ppermute | solution.py:563
  47.3 7.5 %collective-permute-start.24 = (f32[136,256]{1,0:T(8,128)S(1)}, f32[136,256]{1,0:T(8,128)S(1)}, u32[]{:S(2)}, u32[]{:S(2)}) collective-permute-start(f32[136,256]{1,0:T(8,128)S(1)} %get-tuple-element.79), channel_id=1, source_target_pairs={{0,1},{1,0},{2,3},{3,2},{4,5},{5,4},{6,7},{7,6},{8,9},{9,8},{10,11... | collective-permute-start | bytes 417800 | tf_op jit(solution)/shard_map/ppermute | solution.py:563
  47.5 7.4 %collective-permute-start.25 = (f32[136,256]{1,0:T(8,128)S(1)}, f32[136,256]{1,0:T(8,128)S(1)}, u32[]{:S(2)}, u32[]{:S(2)}) collective-permute-start(f32[136,256]{1,0:T(8,128)S(1)} %get-tuple-element.80), channel_id=1, source_target_pairs={{0,1},{1,0},{2,3},{3,2},{4,5},{5,4},{6,7},{7,6},{8,9},{9,8},{10,11... | collective-permute-start | bytes 417800 | tf_op jit(solution)/shard_map/ppermute | solution.py:563
  51.1 8.9 %collective-permute-start.26 = (f32[136,256]{1,0:T(8,128)S(1)}, f32[136,256]{1,0:T(8,128)S(1)}, u32[]{:S(2)}, u32[]{:S(2)}) collective-permute-start(f32[136,256]{1,0:T(8,128)S(1)} %add.20), channel_id=1, source_target_pairs={{0,16},{4,20},{8,24},{12,28},{16,0},{20,4},{24,8},{28,12},{1,17},{... | collective-permute-start | bytes 417800 | tf_op jit(solution)/shard_map/ppermute | solution.py:563
  60.4 6.1 %collective-permute-start.28 = (f32[64,256]{1,0:T(8,128)S(1)}, f32[64,256]{1,0:T(8,128)S(1)}, u32[]{:S(2)}, u32[]{:S(2)}) collective-permute-start(f32[64,256]{1,0:T(8,128)S(1)} %get-tuple-element.88.first_ref), channel_id=1, source_target_pairs={{0,4},{4,0},{8,12},{12,8},{16,20},{20,16},{24,28},{28,24},{1,5},{5... | collective-permute-start | bytes 196616 | tf_op jit(solution)/shard_map/ppermute | solution.py:563
  61.9 7.0 %collective-permute-start.29 = (f32[64,256]{1,0:T(8,128)S(1)}, f32[64,256]{1,0:T(8,128)S(1)}, u32[]{:S(2)}, u32[]{:S(2)}) collective-permute-start(f32[64,256]{1,0:T(8,128)S(1)} %get-tuple-element.87.second_ref), channel_id=1, source_target_pairs={{4,8},{12,16},{20,24},{8,4},{16,12},{24,20},{5,9},{13,17},{21,25},... | collective-permute-start | bytes 196616 | tf_op jit(solution)/shard_map/ppermute | solution.py:554
  (10 other events, 51.6 us)
